TPU v7x, 512 devices: a whole 4x4x16 slice. The times are simulated.
512 devices in a mesh: band: 16 (over z), owner: 32 (over y, x, core).
Axes of the slice: x: 4, y: 4, z: 16, core: 2. Of those that a mesh axis runs over, the one named last changes fastest.
Arguments:
- user_factors: float32 [262144, 256], P(('band', 'owner')), may hold values from -1.5 to 1.5
- item_factors: float32 [16384, 256], P(('band', 'owner')), may hold values from -1.5 to 1.5
- ratings: bfloat16 [3, 8192, 128, 128], P(None, ('band', 'owner')), may hold values from -6 to 6
- tile_users: int32 [3, 8192], P(None, ('band', 'owner')), may hold values from 0 to 3, as said below
- tile_items: int32 [3, 8192], P(None, ('band', 'owner')), may hold values from 0 to 7, as said below
- tile_count: int32 [3, 512], P(None, ('band', 'owner')), may hold values from 1 to 16, as said below
Outputs:
- user_out: float32 [262144, 256], P(('band', 'owner'))
- item_out: float32 [16384, 256], P(('band', 'owner'))
Inputs may be any that keep to these rules, and one draw needn't show every extreme that they name: `tile_users`: within one device and tick, the slots name distinct tiles (user row, item column). `tile_items`: paired with tile_users: the slots of one device and tick name distinct tiles. `tile_count`: each value is 16, 8 or 4, at least 1; in every tick some device has 16.
All inputs are finite; a program needn't handle non-finite values.
Results may differ from a plain program's by a relative error of at most 0.0003.
Values sent between devices are 32-bit elements; how exact they have to be, the bound alone decides.
No kernel may reach another device: no remote copies, remote signals or barrier semaphores. Data moves between devices by JAX's collectives and lax.ppermute only.
A program may use at most 64 MiB of HBM per device.

v0:
```python
import jax
import jax.numpy as jnp
from jax import lax
from jax.sharding import PartitionSpec as P

R = 256
P_SIZE = 1024
TILE = 128
TICKS = 3
K_MAX = 16


user_rate = 0.02
item_rate = 0.005
shrink_rate = 0.05
highest = lax.Precision.HIGHEST


def joined_along(blocks, dim):
    blocks = jnp.moveaxis(blocks, 0, dim)
    lengths = blocks.shape
    return blocks.reshape(*lengths[:dim], lengths[dim] * lengths[dim + 1], *lengths[dim + 2 :])


def sent_to_all(array, axis):
    copies = jnp.broadcast_to(array, (lax.axis_size(axis), *array.shape))
    return lax.all_to_all(copies, axis, split_axis=0, concat_axis=0, tiled=True)


def gather_directly(array, axis, dim):
    return joined_along(sent_to_all(array, axis), dim)


def split_up(array, dim, length):
    before, after = (array.shape[:dim], array.shape[dim + 1 :])
    return jnp.moveaxis(array.reshape(*before, length, -1, *after), dim, 0)


def summed_on_arrival(array, axis, dim):
    blocks = split_up(array, dim, lax.axis_size(axis))
    arrived = lax.all_to_all(blocks, axis, split_axis=0, concat_axis=0, tiled=True)
    return arrived.sum(axis=0)


def passed_along(block, axis, distance):
    devices = range(lax.axis_size(axis))
    route = [((i - distance) % len(devices), i) for i in devices]
    return lax.ppermute(block, axis, route)


def dense_step(user_block, item_shard, rating_tiles, tile_rows, tile_cols, filled):
    tile_rows_count = user_block.shape[0]
    user_flat = user_block.reshape(-1, R)
    active = (jnp.arange(K_MAX) < filled).astype(jnp.float32)
    user_hot = (tile_rows[:, None] == jnp.arange(tile_rows_count)[None, :]).astype(
        jnp.float32
    ) * active[:, None]
    item_hot = (tile_cols[:, None] == jnp.arange(P_SIZE // TILE)[None, :]).astype(jnp.float32)
    rating_dense = jnp.einsum(
        "kt,ks,kui->tusi", user_hot, item_hot, rating_tiles.astype(jnp.float32), precision=highest
    ).reshape(tile_rows_count * TILE, P_SIZE)
    cell_mask = jnp.einsum("kt,ks->ts", user_hot, item_hot, precision=highest)
    mask_dense = jnp.broadcast_to(
        cell_mask[:, None, :, None], (tile_rows_count, TILE, P_SIZE // TILE, TILE)
    ).reshape(tile_rows_count * TILE, P_SIZE)
    piece = gather_directly(item_shard, "owner", 0)
    predicted = jnp.dot(user_flat, piece.T, precision=highest)
    errors = (rating_dense - predicted) * mask_dense
    user_grad = jnp.dot(errors, piece, precision=highest)
    item_rows = jnp.dot(errors.T, user_flat, precision=highest)
    item_grad = item_rows
    user_grad, item_grad = (user_grad, item_grad)
    return (user_grad.reshape(user_block.shape), item_grad)


def shards(user_factors, item_factors, ratings, tile_users, tile_items, tile_count):
    user_block = user_factors.reshape(-1, TILE, R)
    item_shard = item_factors
    for tick_index in range(TICKS):
        user_sum, item_grad = dense_step(
            user_block,
            item_shard,
            ratings[tick_index],
            tile_users[tick_index],
            tile_items[tick_index],
            tile_count[tick_index, 0],
        )
        user_block = user_block * (1.0 - user_rate * shrink_rate) + user_rate * user_sum
        item_share = summed_on_arrival(item_grad, "owner", 0)
        item_shard = item_shard * (1.0 - item_rate * shrink_rate) + item_rate * item_share
        if tick_index + 1 < TICKS:
            item_shard = passed_along(item_shard, "band", -1)
    return (user_block.reshape(-1, R), item_shard)


def solution(mesh):
    placed = (
        P(("band", "owner"), None),
        P(("band", "owner"), None),
        P(None, ("band", "owner"), None, None),
        P(None, ("band", "owner")),
        P(None, ("band", "owner")),
        P(None, ("band", "owner")),
    )
    return jax.shard_map(
        shards,
        mesh=mesh,
        in_specs=placed,
        out_specs=(P(("band", "owner"), None), P(("band", "owner"), None)),
        check_vma=False,
    )
```

profile of v0, /device:TPU:1, one launch (start us, length us, event | category | flops | bytes accessed | tf_op | source)
XLA Modules:
  0.0 191.0 jit_solution(6226598004085038095)
XLA Ops:
  0.7 2.0 %broadcast_in_dim.12 = f32[32,32,256]{2,1,0:T(8,128)} broadcast(f32[32,256]{1,0:T(8,128)} %param.7), dimensions={1,2} | broadcast | bytes 1081344 | tf_op jit(solution)/shard_map/broadcast_in_dim | solution.py:26
  2.6 10.4 %all-to-all-start = ((f32[32,32,256]{2,1,0:T(8,128)}), f32[32,32,256]{2,1,0:T(8,128)S(1)}, u32[]{:S(2)}, u32[]{:S(2)}) async-start(f32[32,32,256]{2,1,0:T(8,128)} %broadcast_in_dim.12), calls=%async_computation | async-start | bytes 2097152 | tf_op jit(solution)/shard_map/all_to_all | solution.py:27
  16.3 2.3 %fusion.5 = f32[8,4,128,128]{3,0,2,1:T(8,128)} fusion(bf16[1,16,128,128]{3,2,1,0:T(8,128)(2,1)S(1)} %get-tuple-element.2, f32[16,4]{0,1:T(4,128)S(1)} %get-tuple-element.16, f32[16,8]{0,1:T(8,128)S(1)} %fusion.23), kind=kOutput, calls=%fused_computation.17 | convolution fusion | flops 100663808 | bytes 2622208 | tf_op jit(solution)/shard_map/kt,ks,kui->tusi/dot_general | solution.py:59
  18.6 11.7 %all-to-all-done = f32[32,32,256]{2,1,0:T(8,128)S(1)} async-done(((f32[32,32,256]{2,1,0:T(8,128)}), f32[32,32,256]{2,1,0:T(8,128)S(1)}, u32[]{:S(2)}, u32[]{:S(2)}) %all-to-all-start) | async-done | bytes 1048608 | tf_op jit(solution)/shard_map/all_to_all | solution.py:27
  30.4 1.4 copy-done.2
  31.8 3.6 %bitcast_multiply_fusion.2 = f32[512,1024]{1,0:T(8,128)S(1)} fusion(f32[64,8,8,128]{3,2,1,0:T(8,128)S(1)} %bitcast.132, f32[64,8,8,128]{3,2,1,0:T(8,128)S(1)} %bitcast.131, f32[512,256]{1,0:T(8,128)} %param.6, f32[1024,256]{1,0:T(8,128)S(1)} %bitcast.123), kind=kOutput, calls=%fused_computation.4 | convolution fusion | flops 1611661312 | bytes 7864320 | tf_op jit(solution)/shard_map/dot_general | solution.py:67
  35.4 3.5 %fusion.35 = f32[1024,256]{1,0:T(8,128)S(1)} fusion(f32[512,1024]{1,0:T(8,128)S(1)} %bitcast_multiply_fusion.2, f32[512,256]{1,0:T(8,128)S(1)} %copy-done.5), kind=kOutput, calls=%fused_computation.63 | convolution fusion | flops 1610612736 | bytes 3670016 | tf_op jit(solution)/shard_map/dot_general | solution.py:70
  38.9 20.9 %all_to_all.30 = f32[32,32,256]{2,1,0:T(8,128)} all-to-all(f32[32,32,256]{2,1,0:T(8,128)S(1)} %bitcast.139), channel_id=1, replica_groups=mesh['band'=16,'owner'=32] {'owner'}, dimensions={0} | all-to-all | bytes 2097152 | tf_op jit(solution)/shard_map/all_to_all | solution.py:41
  59.8 1.3 reduce_sum.27
  61.1 9.2 %collective-permute-start = (f32[32,256]{1,0:T(8,128)S(1)}, f32[32,256]{1,0:T(8,128)S(1)}, u32[]{:S(2)}, u32[]{:S(2)}) collective-permute-start(f32[32,256]{1,0:T(8,128)S(1)} %multiply_add_fusion.2), channel_id=1, source_target_pairs={{32,0},{64,32},{96,64},{128,96},{160,128},{192,160},{224,192},{256... | collective-permute-start | bytes 98312 | tf_op jit(solution)/shard_map/ppermute | solution.py:48
  72.4 5.5 %all-to-all-start.2 = ((f32[32,32,256]{2,1,0:T(8,128)}), f32[32,32,256]{2,1,0:T(8,128)}, u32[]{:S(2)}, u32[]{:S(2)}) async-start(f32[32,32,256]{2,1,0:T(8,128)} %broadcast_in_dim.14), calls=%async_computation.2 | async-start | bytes 2097152 | tf_op jit(solution)/shard_map/all_to_all | solution.py:27
  79.1 3.4 %fusion.4 = f32[8,4,128,128]{3,0,2,1:T(8,128)} fusion(bf16[1,16,128,128]{3,2,1,0:T(8,128)(2,1)} %get-tuple-element.3, f32[16,4]{0,1:T(4,128)S(1)} %get-tuple-element.17, f32[16,8]{0,1:T(8,128)S(1)} %get-tuple-element.15), kind=kOutput, calls=%fused_computation.15 | convolution fusion | flops 100663808 | bytes 2622208 | tf_op jit(solution)/shard_map/kt,ks,kui->tusi/dot_general | solution.py:59
  82.5 2.6 %fusion.2 = f32[4,128,256]{2,1,0:T(8,128)} fusion(f32[4,128,256]{2,1,0:T(8,128)S(1)} %bitcast.140, f32[4,128,1024]{2,1,0:T(8,128)S(1)} %bitcast.120, f32[1024,256,1]{1,0,2:T(8,128)S(1)} %bitcast.124), kind=kOutput, calls=%fused_computation.11 | convolution fusion | flops 1610874880 | bytes 4194304 | tf_op jit(solution)/shard_map/dot_general | solution.py:69
  85.1 10.0 %all-to-all-done.2 = f32[32,32,256]{2,1,0:T(8,128)} async-done(((f32[32,32,256]{2,1,0:T(8,128)}), f32[32,32,256]{2,1,0:T(8,128)}, u32[]{:S(2)}, u32[]{:S(2)}) %all-to-all-start.2) | async-done | bytes 1048608 | tf_op jit(solution)/shard_map/all_to_all | solution.py:27
  95.3 1.4 copy-done
  96.7 3.8 %bitcast_multiply_fusion.1 = f32[512,1024]{1,0:T(8,128)S(1)} fusion(f32[64,8,8,128]{3,2,1,0:T(8,128)S(1)} %bitcast.133, f32[64,8,8,128]{3,2,1,0:T(8,128)S(1)} %bitcast.129, f32[512,256]{1,0:T(8,128)} %bitcast.135, f32[1024,256]{1,0:T(8,128)} %bitcast.22), kind=kOutput, calls=%fused_computation.2 | convolution fusion | flops 1611661312 | bytes 7864320 | tf_op jit(solution)/shard_map/dot_general | solution.py:67
  100.6 1.8 copy.16
  102.4 3.4 %fusion.36 = f32[32,32,256]{2,1,0:T(8,128)S(1)} fusion(f32[32,32,512]{2,1,0:T(8,128)} %bitcast.127, f32[512,256,1]{1,0,2:T(8,128)S(1)} %bitcast.136), kind=kOutput, calls=%fused_computation.64 | convolution fusion | flops 1610612736 | bytes 3670016 | tf_op jit(solution)/shard_map/dot_general | solution.py:70
  105.8 20.6 %all_to_all.31 = f32[32,32,256]{2,1,0:T(8,128)S(1)} all-to-all(f32[32,32,256]{2,1,0:T(8,128)S(1)} %fusion.36), channel_id=1, replica_groups=mesh['band'=16,'owner'=32] {'owner'}, dimensions={0} | all-to-all | bytes 2097152 | tf_op jit(solution)/shard_map/all_to_all | solution.py:41
  126.5 5.2 %collective-permute-start.1 = (f32[32,256]{1,0:T(8,128)S(1)}, f32[32,256]{1,0:T(8,128)S(1)}, u32[]{:S(2)}, u32[]{:S(2)}) collective-permute-start(f32[32,256]{1,0:T(8,128)S(1)} %multiply_add_fusion.1), channel_id=1, source_target_pairs={{32,0},{64,32},{96,64},{128,96},{160,128},{192,160},{224,192},{256... | collective-permute-start | bytes 98312 | tf_op jit(solution)/shard_map/ppermute | solution.py:48
  133.8 4.8 %all-to-all-start.4 = ((f32[32,32,256]{2,1,0:T(8,128)}), f32[32,32,256]{2,1,0:T(8,128)S(1)}, u32[]{:S(2)}, u32[]{:S(2)}) async-start(f32[32,32,256]{2,1,0:T(8,128)} %broadcast_in_dim.16), calls=%async_computation.4 | async-start | bytes 2097152 | tf_op jit(solution)/shard_map/all_to_all | solution.py:27
  138.8 3.4 %fusion.3 = f32[8,4,128,128]{3,0,2,1:T(8,128)} fusion(bf16[1,16,128,128]{3,2,1,0:T(8,128)(2,1)} %get-tuple-element.4, f32[16,4]{0,1:T(4,128)S(1)} %fusion.29, f32[16,8]{0,1:T(8,128)S(1)} %get-tuple-element.14), kind=kOutput, calls=%fused_computation.13 | convolution fusion | flops 100663808 | bytes 2622208 | tf_op jit(solution)/shard_map/kt,ks,kui->tusi/dot_general | solution.py:59
  142.2 3.8 %fusion.1 = f32[4,128,256]{2,1,0:T(8,128)} fusion(f32[4,128,1024]{2,1,0:T(8,128)S(1)} %bitcast.119, f32[1024,256,1]{1,0,2:T(8,128)} %bitcast.24, f32[4,128,256]{2,1,0:T(8,128)S(1)} %copy-done.4), kind=kOutput, calls=%fused_computation.9 | convolution fusion | flops 1611005952 | bytes 4194304 | tf_op jit(solution)/shard_map/dot_general | solution.py:69
  146.0 9.8 %all-to-all-done.4 = f32[32,32,256]{2,1,0:T(8,128)S(1)} async-done(((f32[32,32,256]{2,1,0:T(8,128)}), f32[32,32,256]{2,1,0:T(8,128)S(1)}, u32[]{:S(2)}, u32[]{:S(2)}) %all-to-all-start.4) | async-done | bytes 1048608 | tf_op jit(solution)/shard_map/all_to_all | solution.py:27
  156.0 1.4 copy-done.1
  157.4 3.5 %bitcast_multiply_fusion = f32[512,1024]{1,0:T(8,128)S(1)} fusion(f32[64,8,8,128]{3,2,1,0:T(8,128)S(1)} %bitcast.134, f32[64,8,8,128]{3,2,1,0:T(8,128)S(1)} %bitcast.130, f32[512,256]{1,0:T(8,128)} %bitcast.137, f32[1024,256]{1,0:T(8,128)S(1)} %bitcast.125), kind=kOutput, calls=%fused_computation | convolution fusion | flops 1611661312 | bytes 7864320 | tf_op jit(solution)/shard_map/dot_general | solution.py:67
  160.9 1.8 copy.17
  162.7 4.4 %fusion.37 = f32[32,32,256]{2,1,0:T(8,128)} fusion(f32[32,32,512]{2,1,0:T(8,128)} %bitcast.128, f32[512,256,1]{1,0,2:T(8,128)} %bitcast.138), kind=kOutput, calls=%fused_computation.65 | convolution fusion | flops 1610612736 | bytes 3670016 | tf_op jit(solution)/shard_map/dot_general | solution.py:70
  167.2 4.7 %all-to-all-start.5 = ((f32[32,32,256]{2,1,0:T(8,128)}), f32[32,32,256]{2,1,0:T(8,128)}, u32[]{:S(2)}, u32[]{:S(2)}) async-start(f32[32,32,256]{2,1,0:T(8,128)} %fusion.37), calls=%async_computation.5 | async-start | bytes 2097152 | tf_op jit(solution)/shard_map/all_to_all | solution.py:41
  171.9 3.6 %fusion = f32[4,128,256]{2,1,0:T(8,128)} fusion(f32[4,128,1024]{2,1,0:T(8,128)S(1)} %bitcast.122, f32[1024,256,1]{1,0,2:T(8,128)S(1)} %bitcast.126, f32[4,128,256]{2,1,0:T(8,128)} %fusion.1), kind=kOutput, calls=%fused_computation.7 | convolution fusion | flops 1611005952 | bytes 4194304 | tf_op jit(solution)/shard_map/dot_general | solution.py:69
  175.5 13.6 %all-to-all-done.5 = f32[32,32,256]{2,1,0:T(8,128)} async-done(((f32[32,32,256]{2,1,0:T(8,128)}), f32[32,32,256]{2,1,0:T(8,128)}, u32[]{:S(2)}, u32[]{:S(2)}) %all-to-all-start.5) | async-done | bytes 1048608 | tf_op jit(solution)/shard_map/all_to_all | solution.py:41
  189.1 1.3 reduce_sum.29
  (45 shorter events, 10.0 us)
Async XLA Ops:
  0.6 12.4 %copy-start.8 = (s32[3,1]{0,1:T(1,128)S(1)}, s32[3,1]{0,1:T(1,128)}, u32[]{:S(2)}) copy-start(s32[3,1]{0,1:T(1,128)} %param.11) | copy-start | bytes 40
  0.6 14.3 %copy-start.9 = (s32[3,16]{1,0:T(4,128)S(1)}, s32[3,16]{1,0:T(4,128)}, u32[]{:S(2)}) copy-start(s32[3,16]{1,0:T(4,128)} %param.9) | copy-start | bytes 580
  0.7 14.4 %copy-start.10 = (s32[3,16]{1,0:T(4,128)S(1)}, s32[3,16]{1,0:T(4,128)}, u32[]{:S(2)}) copy-start(s32[3,16]{1,0:T(4,128)} %param.10) | copy-start | bytes 580
  0.7 14.5 %copy-start.6 = (bf16[3,16,128,128]{3,2,1,0:T(8,128)(2,1)S(1)}, bf16[3,16,128,128]{3,2,1,0:T(8,128)(2,1)}, u32[]{:S(2)}) copy-start(bf16[3,16,128,128]{3,2,1,0:T(8,128)(2,1)} %param.8) | copy-start | bytes 4718596
  2.6 27.6 %all-to-all-start = ((f32[32,32,256]{2,1,0:T(8,128)}), f32[32,32,256]{2,1,0:T(8,128)S(1)}, u32[]{:S(2)}, u32[]{:S(2)}) async-start(f32[32,32,256]{2,1,0:T(8,128)} %broadcast_in_dim.12), calls=%async_computation | async-start | bytes 2097152 | tf_op jit(solution)/shard_map/all_to_all | solution.py:27
  30.2 1.6 copy-start.2
  31.8 3.6 %copy-start.5 = (f32[512,256]{1,0:T(8,128)S(1)}, f32[512,256]{1,0:T(8,128)}, u32[]{:S(2)}) copy-start(f32[512,256]{1,0:T(8,128)} %param.6) | copy-start | bytes 1572868
  38.9 22.2 %copy-start.7 = (f32[32,256]{1,0:T(8,128)S(1)}, f32[32,256]{1,0:T(8,128)}, u32[]{:S(2)}) copy-start(f32[32,256]{1,0:T(8,128)} %param.7) | copy-start | bytes 98308
  61.1 10.2 %collective-permute-start = (f32[32,256]{1,0:T(8,128)S(1)}, f32[32,256]{1,0:T(8,128)S(1)}, u32[]{:S(2)}, u32[]{:S(2)}) collective-permute-start(f32[32,256]{1,0:T(8,128)S(1)} %multiply_add_fusion.2), channel_id=1, source_target_pairs={{32,0},{64,32},{96,64},{128,96},{160,128},{192,160},{224,192},{256... | collective-permute-start | bytes 98312 | tf_op jit(solution)/shard_map/ppermute | solution.py:48
  72.4 22.7 %all-to-all-start.2 = ((f32[32,32,256]{2,1,0:T(8,128)}), f32[32,32,256]{2,1,0:T(8,128)}, u32[]{:S(2)}, u32[]{:S(2)}) async-start(f32[32,32,256]{2,1,0:T(8,128)} %broadcast_in_dim.14), calls=%async_computation.2 | async-start | bytes 2097152 | tf_op jit(solution)/shard_map/all_to_all | solution.py:27
  95.1 1.6 copy-start
  100.6 1.9 copy-start.3
  126.5 6.2 %collective-permute-start.1 = (f32[32,256]{1,0:T(8,128)S(1)}, f32[32,256]{1,0:T(8,128)S(1)}, u32[]{:S(2)}, u32[]{:S(2)}) collective-permute-start(f32[32,256]{1,0:T(8,128)S(1)} %multiply_add_fusion.1), channel_id=1, source_target_pairs={{32,0},{64,32},{96,64},{128,96},{160,128},{192,160},{224,192},{256... | collective-permute-start | bytes 98312 | tf_op jit(solution)/shard_map/ppermute | solution.py:48
  133.8 22.0 %all-to-all-start.4 = ((f32[32,32,256]{2,1,0:T(8,128)}), f32[32,32,256]{2,1,0:T(8,128)S(1)}, u32[]{:S(2)}, u32[]{:S(2)}) async-start(f32[32,32,256]{2,1,0:T(8,128)} %broadcast_in_dim.16), calls=%async_computation.4 | async-start | bytes 2097152 | tf_op jit(solution)/shard_map/all_to_all | solution.py:27
  138.6 3.6 %copy-start.4 = (f32[4,128,256]{2,1,0:T(8,128)S(1)}, f32[4,128,256]{2,1,0:T(8,128)}, u32[]{:S(2)}) copy-start(f32[4,128,256]{2,1,0:T(8,128)} %fusion.2) | copy-start | bytes 1572868
  155.8 1.6 copy-start.1
  167.2 21.9 %all-to-all-start.5 = ((f32[32,32,256]{2,1,0:T(8,128)}), f32[32,32,256]{2,1,0:T(8,128)}, u32[]{:S(2)}, u32[]{:S(2)}) async-start(f32[32,32,256]{2,1,0:T(8,128)} %fusion.37), calls=%async_computation.5 | async-start | bytes 2097152 | tf_op jit(solution)/shard_map/all_to_all | solution.py:41
where the time goes:
time: 192 us; the launch traced here: 191 us
  waiting for transfers between devices  46.4 us (24%)
  matrix products  41.7 us (22%)
  blocking collectives  41.5 us (22%)
  starting transfers between devices  39.7 us (21%)
  local copies, waits for them, and re-layouts  14.4 us (8%)
  other arithmetic  6.28 us (3%)
    all_to_all x2, blocking collectives, summed_on_arrival(): lax.all_to_all(blocks, axis, split_axis=0, concat_axis=0, tiled=True)  41.5 us
    all_to_all x3, waiting for transfers between devices, sent_to_all(): return lax.all_to_all(copies, axis, split_axis=0, concat_axis=0, tiled=True)  31.4 us
    all_to_all x3, starting transfers between devices, sent_to_all(): return lax.all_to_all(copies, axis, split_axis=0, concat_axis=0, tiled=True)  20.8 us
    ppermute x2, starting transfers between devices, passed_along(): return lax.ppermute(block, axis, route)  14.3 us
    all_to_all x1, waiting for transfers between devices, summed_on_arrival(): lax.all_to_all(blocks, axis, split_axis=0, concat_axis=0, tiled=True)  13.6 us
    dot_general x3, matrix products, dense_step(): item_rows = jnp.dot(errors.T, user_flat, precision=highest)  11.3 us
    dot_general x3, matrix products, dense_step(): predicted = jnp.dot(user_flat, piece.T, precision=highest)  10.9 us
    dot_general x3, matrix products, dense_step(): user_grad = jnp.dot(errors, piece, precision=highest)  10.1 us
  transfers between devices with their start and end apart: 6, of which 6 were waited for; matrix products, arithmetic and copies ran while one was open for 13% of the time, Pallas kernels for 0%

commit v1 on v0

v1 whole, which is shorter than its diff:
```python
import functools

import jax
import jax.numpy as jnp
from jax import lax
from jax.experimental import pallas as pl
from jax.experimental.pallas import tpu as pltpu
from jax.sharding import PartitionSpec as P

R = 256
P_SIZE = 1024
TILE = 128
HALF = TILE // 2
TICKS = 3
K_MAX = 16
U_DEV = 512
U_TILES = U_DEV // TILE
I_TILES = P_SIZE // TILE
ITEMS_CORE = P_SIZE // 2
CHIPS = 16
SHARE = 32
CELLS = U_TILES * I_TILES

user_rate = 0.02
item_rate = 0.005
shrink_rate = 0.05
bf16 = jnp.bfloat16
f32 = jnp.float32

SAME_CORE = [[2 * chip + core for chip in range(CHIPS)] for core in range(2)]
PARTNERS = [(i, i ^ 1) for i in range(2 * CHIPS)]


def halves(x):
    top = x.astype(bf16)
    return top, (x - top.astype(f32)).astype(bf16)


def dot3(a, b, dims):
    (a_top, a_low), (b_top, b_low) = a, b
    dot = lambda x, y: lax.dot_general(x, y, (dims, ((), ())), preferred_element_type=f32)
    return dot(a_top, b_top) + (dot(a_top, b_low) + dot(a_low, b_top))


VMEM = pl.BlockSpec(memory_space=pltpu.VMEM)
ANY = pl.BlockSpec(memory_space=pl.ANY)
SMEM = pl.BlockSpec(memory_space=pltpu.SMEM)
WIDTH = 2 * TILE
BLOCKS = 2 * U_DEV // WIDTH


def shape(dims, dtype):
    return jax.ShapeDtypeStruct(dims, dtype)


def call(kernel, outs, in_specs, out_specs, scratch, flops, nbytes, grant=60 * 1024):
    return pl.pallas_call(
        kernel,
        out_shape=outs,
        in_specs=in_specs,
        out_specs=out_specs,
        scratch_shapes=scratch,
        compiler_params=pltpu.CompilerParams(vmem_limit_bytes=grant * 1024),
        cost_estimate=pl.CostEstimate(flops=flops, bytes_accessed=nbytes, transcendentals=0),
    )


def turn_kernel(tick, core_ref, map_ref, tiles_hbm, kept_hbm, sent_hbm, tiles, kept, sent, turned, sems):
    core = core_ref[0]
    group = K_MAX // 4

    def fetch(g):
        slots = pl.ds(g * group, group)
        return pltpu.make_async_copy(tiles_hbm.at[tick, slots], tiles.at[slots], sems.at[g])

    def put(g, which):
        buf, hbm = ((kept, kept_hbm), (sent, sent_hbm))[which]
        slots = pl.ds(g * group, group)
        return pltpu.make_async_copy(buf.at[slots], hbm.at[slots], sems.at[4 + 2 * g + which])

    for g in range(4):
        fetch(g).start()
    lane = lax.broadcasted_iota(jnp.int32, (8, TILE), 1)
    row = jnp.zeros((8, TILE), jnp.int32)
    for cell in range(CELLS):
        row = jnp.where(lane == cell, map_ref[tick * CELLS + cell], row)
    sent[K_MAX, pl.ds(0, 8), :] = row.astype(f32)
    sent[K_MAX, pl.ds(8, HALF - 8), :] = jnp.zeros((HALF - 8, TILE), f32)
    last = pltpu.make_async_copy(sent.at[pl.ds(K_MAX, 1)], sent_hbm.at[pl.ds(K_MAX, 1)], sems.at[12])
    last.start()
    for g in range(4):
        fetch(g).wait()
        for k in range(g * group, (g + 1) * group):
            turned[k] = tiles[k].astype(f32).T
            for part in range(2):
                rows = pl.ds(part * SHARE, SHARE)
                mine = pl.multiple_of(part * HALF + core * SHARE, SHARE)
                theirs = pl.multiple_of(part * HALF + (1 - core) * SHARE, SHARE)
                kept[k, rows, :] = turned[k, pl.ds(mine, SHARE), :]
                sent[k, rows, :] = turned[k, pl.ds(theirs, SHARE), :]
        put(g, 0).start()
        put(g, 1).start()
    for g in range(4):
        put(g, 0).wait()
        put(g, 1).wait()
    last.wait()


def turned_tiles(tick, core, slot_map, ratings):
    return call(
        functools.partial(turn_kernel, tick),
        (shape((K_MAX, HALF, TILE), f32), shape((K_MAX + 1, HALF, TILE), f32)),
        [SMEM, SMEM, ANY], (ANY, ANY),
        [pltpu.VMEM((K_MAX, TILE, TILE), bf16), pltpu.VMEM((K_MAX, HALF, TILE), f32),
         pltpu.VMEM((K_MAX + 1, HALF, TILE), f32), pltpu.VMEM((K_MAX, TILE, TILE), f32),
         pltpu.SemaphoreType.DMA((13,))],
        1000000, 1600000,
    )(core, slot_map, ratings)


def split_kernel(own_ref, other_ref, top_ref, low_ref):
    for part, ref in enumerate((own_ref, other_ref)):
        rows = pl.ds(part * U_DEV, U_DEV)
        top_ref[rows, :], low_ref[rows, :] = halves(ref[...])


def split_users(own, other):
    out = shape((2 * U_DEV, R), bf16)
    return call(split_kernel, (out, out), [VMEM] * 2, (VMEM,) * 2, [], 1000000, 2000000)(own, other)


def error_kernel(own_map, other_map, panel_hbm, top_hbm, low_hbm, own_hbm, other_hbm,
                 grad_hbm, err_top_hbm, err_low_hbm,
                 panel_ref, top_ref, low_ref, own_tiles, other_tiles, predicted, err_top, err_low, grad_ref, sems):
    def rows(block):
        return pl.ds(block * WIDTH, WIDTH)

    loads = [pltpu.make_async_copy(panel_hbm, panel_ref, sems.at[0])]
    for block in range(BLOCKS):
        loads.append(pltpu.make_async_copy(top_hbm.at[rows(block)], top_ref.at[rows(block)], sems.at[1 + 2 * block]))
        loads.append(pltpu.make_async_copy(low_hbm.at[rows(block)], low_ref.at[rows(block)], sems.at[2 + 2 * block]))
    first = 1 + 2 * BLOCKS
    loads.append(pltpu.make_async_copy(own_hbm, own_tiles, sems.at[first]))
    loads.append(pltpu.make_async_copy(other_hbm.at[pl.ds(0, K_MAX)], other_tiles, sems.at[first + 1]))
    for copy in [*loads[:5], loads[first], *loads[5:first], loads[first + 1]]:
        copy.start()

    def put(block, which):
        source, into = ((err_top, err_top_hbm), (err_low, err_low_hbm))[which]
        return pltpu.make_async_copy(source.at[block], into.at[block], sems.at[first + 2 + 2 * block + which])

    def send(part):
        cut = pl.ds(part * TILE, TILE)
        return pltpu.make_async_copy(grad_ref.at[cut], grad_hbm.at[cut], sems.at[first + 2 + 2 * BLOCKS + part])

    loads[0].wait()
    panel = halves(panel_ref[...])

    def users(block):
        return top_ref[rows(block), :], low_ref[rows(block), :]

    def predict(block):
        loads[1 + 2 * block].wait()
        loads[2 + 2 * block].wait()
        predicted[block] = dot3(panel, users(block), ((1,), (1,)))

    predict(0)
    for block in range(BLOCKS):
        if block + 1 < BLOCKS:
            predict(block + 1)
        mine = block * WIDTH < U_DEV
        slot_map, tiles = (own_map, own_tiles) if mine else (other_map, other_tiles)
        if block * WIDTH % U_DEV == 0:
            loads[first if mine else first + 1].wait()
        for item in range(I_TILES):
            cut = pl.ds(item * HALF, HALF)
            for part in range(2):
                user = (block * 2 + part) % U_TILES
                slot = slot_map[user * I_TILES + item]
                lanes = pl.ds(part * TILE, TILE)
                error = tiles[jnp.maximum(slot, 0)] - predicted[block, cut, lanes]
                error = jnp.where(slot >= 0, error, 0.0)
                err_top[block, cut, lanes], err_low[block, cut, lanes] = halves(error)
        put(block, 0).start()
        put(block, 1).start()
        if block == 0:
            grad_ref[...] = dot3((err_top[block], err_low[block]), users(block), ((1,), (0,)))
        elif block + 1 < BLOCKS:
            grad_ref[...] += dot3((err_top[block], err_low[block]), users(block), ((1,), (0,)))
        else:
            for part in range(ITEMS_CORE // TILE):
                cut = pl.ds(part * TILE, TILE)
                grad_ref[cut, :] += dot3((err_top[block, cut, :], err_low[block, cut, :]), users(block), ((1,), (0,)))
                send(part).start()
    for block in range(BLOCKS):
        put(block, 0).wait()
        put(block, 1).wait()
    for part in range(ITEMS_CORE // TILE):
        send(part).wait()


def errors_and_item_grad(own_map, other_map, panel, top, low, own_tiles, other_tiles):
    err = (BLOCKS, ITEMS_CORE, WIDTH)
    tiles = pltpu.VMEM((K_MAX, HALF, TILE), f32)
    panel_shape = pltpu.VMEM((ITEMS_CORE, R), f32)
    user = pltpu.VMEM((2 * U_DEV, R), bf16)
    return call(
        error_kernel,
        (shape((ITEMS_CORE, R), f32), shape(err, bf16), shape(err, bf16)),
        [SMEM] * 2 + [ANY] * 5, (ANY,) * 3,
        [panel_shape, user, user, tiles, tiles, pltpu.VMEM(err, f32), pltpu.VMEM(err, bf16), pltpu.VMEM(err, bf16),
         panel_shape, pltpu.SemaphoreType.DMA((3 + 4 * BLOCKS + ITEMS_CORE // TILE,))],
        1600000000, 6000000, 54000,
    )(own_map, other_map, panel, top, low, own_tiles, other_tiles)


def user_grad_kernel(err_top_hbm, err_low_hbm, panel_hbm, grad_hbm, err_top, err_low, panel_ref, grad, sems):
    def fetch(block, which):
        source, into = ((err_top_hbm, err_top), (err_low_hbm, err_low))[which]
        return pltpu.make_async_copy(source.at[block], into.at[block], sems.at[2 * block + which])

    def put(block):
        rows = pl.ds(block * WIDTH, WIDTH)
        return pltpu.make_async_copy(grad.at[rows], grad_hbm.at[rows], sems.at[2 * BLOCKS + block])

    panel_copy = pltpu.make_async_copy(panel_hbm, panel_ref, sems.at[3 * BLOCKS])
    panel_copy.start()
    for block in range(BLOCKS):
        fetch(block, 0).start()
        fetch(block, 1).start()
    panel_copy.wait()
    panel = halves(panel_ref[...])
    for block in range(BLOCKS):
        fetch(block, 0).wait()
        fetch(block, 1).wait()
        grad[pl.ds(block * WIDTH, WIDTH), :] = dot3((err_top[block], err_low[block]), panel, ((0,), (0,)))
        put(block).start()
    for block in range(BLOCKS):
        put(block).wait()


def user_grads(err_top, err_low, panel):
    err = (BLOCKS, ITEMS_CORE, WIDTH)
    return call(
        user_grad_kernel,
        shape((2 * U_DEV, R), f32), [ANY] * 3, ANY,
        [pltpu.VMEM(err, bf16), pltpu.VMEM(err, bf16), pltpu.VMEM((ITEMS_CORE, R), f32),
         pltpu.VMEM((2 * U_DEV, R), f32), pltpu.SemaphoreType.DMA((3 * BLOCKS + 1,))],
        800000000, 4000000, 54000,
    )(err_top, err_low, panel)


def stepped(user, here, there):
    return user * (1.0 - user_rate * shrink_rate) + user_rate * (here + there)


def update_kernel(own_hbm, other_hbm, here_hbm, there_hbm, own_out, other_out, top_ref, low_ref,
                  user, here, there, sems):
    half = BLOCKS // 2

    def rows(block):
        return pl.ds(block * WIDTH, WIDTH)

    def part(block, own, other):
        return (own if block < half else other).at[rows(block % half)]

    def fetch(block, which):
        source, into = (
            (part(block, own_hbm, other_hbm), user),
            (here_hbm.at[rows(block)], here),
            (there_hbm.at[rows((block + half) % BLOCKS)], there),
        )[which]
        return pltpu.make_async_copy(source, into.at[rows(block)], sems.at[4 * block + which])

    def put(block):
        return pltpu.make_async_copy(user.at[rows(block)], part(block, own_out, other_out), sems.at[4 * block + 3])

    for block in range(BLOCKS):
        for which in range(3):
            fetch(block, which).start()
    for block in range(BLOCKS):
        for which in range(3):
            fetch(block, which).wait()
        new = stepped(user[rows(block), :], here[rows(block), :], there[rows(block), :])
        user[rows(block), :] = new
        put(block).start()
        top_ref[rows(block), :], low_ref[rows(block), :] = halves(new)
    for block in range(BLOCKS):
        put(block).wait()


def updated_users(own, other, here, there):
    out = shape((2 * U_DEV, R), bf16)
    new = shape((U_DEV, R), f32)
    both = pltpu.VMEM((2 * U_DEV, R), f32)
    return call(
        update_kernel, (new, new, out, out), [ANY] * 4, (ANY, ANY, VMEM, VMEM),
        [both, both, both, pltpu.SemaphoreType.DMA((4 * BLOCKS,))], 1000000, 5000000,
    )(own, other, here, there)


def swapped(x):
    return lax.ppermute(x, "owner", PARTNERS)


def exchanged(blocks):
    return lax.all_to_all(blocks, "owner", split_axis=0, concat_axis=0, axis_index_groups=SAME_CORE, tiled=True)


def passed_along(block, axis, distance):
    devices = range(lax.axis_size(axis))
    route = [((i - distance) % len(devices), i) for i in devices]
    return lax.ppermute(block, axis, route)


def slot_maps(tile_users, tile_items, tile_count):
    slots = jnp.arange(K_MAX)[None, :, None]
    cell = (tile_users * I_TILES + tile_items)[:, :, None]
    live = (slots < tile_count[:, :, None]) & (cell == jnp.arange(CELLS)[None, None, :])
    return jnp.max(jnp.where(live, slots, -1), axis=1).astype(jnp.int32)


def shards(user_factors, item_factors, ratings, tile_users, tile_items, tile_count):
    core = lax.rem(lax.axis_index("owner"), 2).reshape(1)
    own, share = user_factors, item_factors
    other = swapped(own)
    own_map = slot_maps(tile_users, tile_items, tile_count)
    top, low = split_users(own, other)
    for tick in range(TICKS):
        kept, sent = turned_tiles(tick, core, own_map.reshape(-1), ratings)
        got = swapped(sent)
        other_map = got[K_MAX, 0, :CELLS].astype(jnp.int32)
        panel = exchanged(jnp.broadcast_to(share[None], (CHIPS, SHARE, R))).reshape(ITEMS_CORE, R)
        item_grad, err_top, err_low = errors_and_item_grad(
            own_map[tick], other_map, panel, top, low, kept, got)
        parts = exchanged(item_grad.reshape(CHIPS, SHARE, R))
        here = user_grads(err_top, err_low, panel)
        if tick + 1 < TICKS:
            there = swapped(here)
            own, other, top, low = updated_users(own, other, here, there)
        else:
            there = swapped(here[U_DEV:])
            own, parts = lax.optimization_barrier((stepped(own, here[:U_DEV], there), parts))
        share = share * (1.0 - item_rate * shrink_rate) + item_rate * parts.sum(axis=0)
        if tick + 1 < TICKS:
            share = passed_along(share, "band", -1)
    return own, share


def solution(mesh):
    placed = (
        P(("band", "owner"), None),
        P(("band", "owner"), None),
        P(None, ("band", "owner"), None, None),
        P(None, ("band", "owner")),
        P(None, ("band", "owner")),
        P(None, ("band", "owner")),
    )
    return jax.shard_map(
        shards,
        mesh=mesh,
        in_specs=placed,
        out_specs=(P(("band", "owner"), None), P(("band", "owner"), None)),
        check_vma=False,
    )
```

time: 192 us -> 162 us (0.84)
  Pallas kernels: 0 us -> 49.5 us
  matrix products: 41.7 us -> 0 us
  blocking collectives: 41.5 us -> 0 us
  starting transfers between devices: 39.7 us -> 68.5 us
  waiting for transfers between devices: 46.4 us -> 30.7 us
  local copies, waits for them, and re-layouts: 14.4 us -> 7.33 us
  other arithmetic: 6.28 us -> 3.24 us
    pallas_call x0 -> x12, Pallas kernels: none -> 49.5 us  [the longest x3 18.2 us: errors_and_item_grad(): call(error_kernel, (shape((ITEMS_CORE, R), f32), shape(err, bf16), shape(...]
    dot_general x15 -> x0, matrix products: 41.7 us -> none  [the longest x3 11.3 us: dense_step(): item_rows = jnp.dot(errors.T, user_flat, precision=highest)]
    all_to_all x2 -> x0, blocking collectives: 41.5 us -> none  [summed_on_arrival(): lax.all_to_all(blocks, axis, split_axis=0, concat_axis=0, tiled=True)]
    ppermute x0 -> x7, starting transfers between devices: none -> 26.6 us  [swapped(): return lax.ppermute(x, 'owner', PARTNERS)]
    all_to_all x4 -> x6, waiting for transfers between devices: 45 us -> 28.7 us  [exchanged(): lax.all_to_all(blocks, 'owner', split_axis=0, concat_axis=0, axis_index_g...]
    dot_general x2 -> x0, local copies, waits for them, and re-layouts: 3.68 us -> none  [dense_step(): item_rows = jnp.dot(errors.T, user_flat, precision=highest)]
    all_to_all x4 -> x6, starting transfers between devices: 25.4 us -> 28.1 us  [exchanged(): lax.all_to_all(blocks, 'owner', split_axis=0, concat_axis=0, axis_index_g...]
    reduce_sum x3, other arithmetic: 2.66 us -> 0.11 us  [shards(): parts.sum(axis=0)]
  transfers between devices with their start and end apart: 6 -> 15, of which waited for: 6 -> 6; matrix products, arithmetic and copies ran while one was open for 13% -> 2% of each run, Pallas kernels for 0% -> 15%
where the time goes in v1:
time: 162 us; the launch traced here: 160 us
  starting transfers between devices  68.5 us (42%)
  Pallas kernels  49.5 us (31%)
  waiting for transfers between devices  30.7 us (19%)
  local copies, waits for them, and re-layouts  7.33 us (5%)
  other arithmetic  3.24 us (2%)
    all_to_all x6, waiting for transfers between devices, exchanged(): lax.all_to_all(blocks, 'owner', split_axis=0, concat_axis=0, axis_index_g...  28.7 us
    all_to_all x6, starting transfers between devices, exchanged(): lax.all_to_all(blocks, 'owner', split_axis=0, concat_axis=0, axis_index_g...  28.1 us
    ppermute x7, starting transfers between devices, swapped(): return lax.ppermute(x, 'owner', PARTNERS)  26.6 us
    pallas_call x3, Pallas kernels, errors_and_item_grad(): call(error_kernel, (shape((ITEMS_CORE, R), f32), shape(err, bf16), shape(...  18.2 us
    ppermute x2, starting transfers between devices, passed_along(): return lax.ppermute(block, axis, route)  13.9 us
    pallas_call x3, Pallas kernels, user_grads(): call(user_grad_kernel, shape((2 * U_DEV, R), f32), [ANY] * 3, ANY, [pltpu...  12.6 us
    pallas_call x3, Pallas kernels, turned_tiles(): call(functools.partial(turn_kernel, tick), (shape((K_MAX, HALF, TILE), f3...  8.97 us
    pallas_call x2, Pallas kernels, updated_users(): call(update_kernel, (new, new, out, out), [ANY] * 4, (ANY, ANY, VMEM, VME...  7.38 us
  transfers between devices with their start and end apart: 15, of which 6 were waited for; matrix products, arithmetic and copies ran while one was open for 2% of the time, Pallas kernels for 15%

profile of v1, /device:TPU:1, one launch (start us, length us, event | category | flops | bytes accessed | tf_op | source)
XLA Modules:
  0.0 160.4 jit_solution(16494570980794451573)
XLA Ops:
  2.9 3.0 %shard_map.80 = (f32[16,64,128]{2,1,0:T(8,128)}, f32[17,64,128]{2,1,0:T(8,128)}) custom-call(s32[1]{0:T(128)} %bitcast.2.core_ref, s32[96]{0:T(128)} %reshape.65.map_ref, bf16[3,16,128,128]{3,2,1,0:T(8,128)(2,1)} %tiles_hbm.5), custom_call_target="tpu_custom_call" | custom-call | flops 1000000 | bytes 1600000 | tf_op jit(solution)/shard_map/pallas_call | solution.py:110
  5.9 8.7 %collective-permute-start.1 = (f32[17,64,128]{2,1,0:T(8,128)}, f32[17,64,128]{2,1,0:T(8,128)S(1)}, u32[]{:S(2)}, u32[]{:S(2)}) collective-permute-start(f32[17,64,128]{2,1,0:T(8,128)} %get-tuple-element.28), channel_id=1, source_target_pairs={{0,1},{1,0},{2,3},{3,2},{4,5},{5,4},{6,7},{7,6},{8,9},{9,8},{10,11... | collective-permute-start | bytes 1671176 | tf_op jit(solution)/shard_map/ppermute | solution.py:303
  14.6 1.9 %collective-permute-start = (f32[512,256]{1,0:T(8,128)S(1)}, f32[512,256]{1,0:T(8,128)S(1)}, u32[]{:S(2)}, u32[]{:S(2)}) collective-permute-start(f32[512,256]{1,0:T(8,128)S(1)} %copy-done.1), channel_id=1, source_target_pairs={{0,1},{1,0},{2,3},{3,2},{4,5},{5,4},{6,7},{7,6},{8,9},{9,8},{10,11... | collective-permute-start | bytes 1572872 | tf_op jit(solution)/shard_map/ppermute | solution.py:303
  17.4 3.6 %all-to-all-start = ((f32[16,32,256]{2,1,0:T(8,128)}), f32[16,32,256]{2,1,0:T(8,128)S(1)}, u32[]{:S(2)}, u32[]{:S(2)}) async-start(f32[16,32,256]{2,1,0:T(8,128)} %broadcast_in_dim.20), calls=%async_computation | async-start | bytes 1048576 | tf_op jit(solution)/shard_map/all_to_all | solution.py:307
  21.8 2.3 %shard_map.81 = (bf16[1024,256]{1,0:T(8,128)(2,1)}, bf16[1024,256]{1,0:T(8,128)(2,1)}) custom-call(f32[512,256]{1,0:T(8,128)} %own_hbm.1, f32[512,256]{1,0:T(8,128)} %copy-done.2), custom_call_target="tpu_custom_call" | custom-call | flops 1000000 | bytes 2000000 | tf_op jit(solution)/shard_map/pallas_call | solution.py:129
  24.2 7.6 %all-to-all-done = f32[16,32,256]{2,1,0:T(8,128)S(1)} async-done(((f32[16,32,256]{2,1,0:T(8,128)}), f32[16,32,256]{2,1,0:T(8,128)S(1)}, u32[]{:S(2)}, u32[]{:S(2)}) %all-to-all-start) | async-done | bytes 524320 | tf_op jit(solution)/shard_map/all_to_all | solution.py:307
  31.8 6.1 %shard_map.82 = (f32[512,256]{1,0:T(8,128)}, bf16[4,512,256]{2,1,0:T(8,128)(2,1)}, bf16[4,512,256]{2,1,0:T(8,128)(2,1)}) custom-call(s32[32]{0:T(128)S(1)} %get-tuple-element.54.own_map, s32[32]{0:T(128)S(1)} %fusion.5.other_map, f32[512,256]{1,0:T(8,128)S(1)} %bitcast.20, bf16[1024,256]{1,0:T(8,128)(2,1)} %get-tuple-element.29.top_hbm, ...), custom_call_target="tpu_custom_call" | custom-call | flops 1600000000 | bytes 6000000 | tf_op jit(solution)/shard_map/pallas_call | solution.py:207
  37.9 3.6 %all-to-all-start.1 = ((f32[16,32,256]{2,1,0:T(8,128)}), f32[16,32,256]{2,1,0:T(8,128)S(1)}, u32[]{:S(2)}, u32[]{:S(2)}) async-start(f32[16,32,256]{2,1,0:T(8,128)} %bitcast.7), calls=%async_computation.1 | async-start | bytes 1048576 | tf_op jit(solution)/shard_map/all_to_all | solution.py:307
  41.4 4.2 %shard_map.83.here_hbm = f32[1024,256]{1,0:T(8,128)} custom-call(bf16[4,512,256]{2,1,0:T(8,128)(2,1)} %get-tuple-element.32.err_top_hbm, bf16[4,512,256]{2,1,0:T(8,128)(2,1)} %get-tuple-element.33.err_low_hbm, f32[512,256]{1,0:T(8,128)S(1)} %bitcast.21), custom_call_target="tpu_custom_call" | custom-call | flops 800000000 | bytes 4000000 | tf_op jit(solution)/shard_map/pallas_call | solution.py:244
  45.6 3.6 %collective-permute-start.2 = (f32[1024,256]{1,0:T(8,128)}, f32[1024,256]{1,0:T(8,128)S(1)}, u32[]{:S(2)}, u32[]{:S(2)}) collective-permute-start(f32[1024,256]{1,0:T(8,128)} %shard_map.83.here_hbm), channel_id=1, source_target_pairs={{0,1},{1,0},{2,3},{3,2},{4,5},{5,4},{6,7},{7,6},{8,9},{9,8},{10,11... | collective-permute-start | bytes 3145736 | tf_op jit(solution)/shard_map/ppermute | solution.py:303
  49.2 3.0 %shard_map.85 = (f32[16,64,128]{2,1,0:T(8,128)}, f32[17,64,128]{2,1,0:T(8,128)}) custom-call(s32[1]{0:T(128)} %bitcast.2.core_ref, s32[96]{0:T(128)} %reshape.65.map_ref, bf16[3,16,128,128]{3,2,1,0:T(8,128)(2,1)} %tiles_hbm.5), custom_call_target="tpu_custom_call" | custom-call | flops 1000000 | bytes 1600000 | tf_op jit(solution)/shard_map/pallas_call | solution.py:110
  52.2 1.9 %collective-permute-start.3 = (f32[17,64,128]{2,1,0:T(8,128)}, f32[17,64,128]{2,1,0:T(8,128)S(1)}, u32[]{:S(2)}, u32[]{:S(2)}) collective-permute-start(f32[17,64,128]{2,1,0:T(8,128)} %get-tuple-element.36), channel_id=1, source_target_pairs={{0,1},{1,0},{2,3},{3,2},{4,5},{5,4},{6,7},{7,6},{8,9},{9,8},{10,11... | collective-permute-start | bytes 1671176 | tf_op jit(solution)/shard_map/ppermute | solution.py:303
  54.2 9.0 %collective-permute-start.4 = (f32[32,256]{1,0:T(8,128)S(1)}, f32[32,256]{1,0:T(8,128)S(1)}, u32[]{:S(2)}, u32[]{:S(2)}) collective-permute-start(f32[32,256]{1,0:T(8,128)S(1)} %multiply_add_fusion.2), channel_id=1, source_target_pairs={{32,0},{64,32},{96,64},{128,96},{160,128},{192,160},{224,192},{256... | collective-permute-start | bytes 98312 | tf_op jit(solution)/shard_map/ppermute | solution.py:313
  65.1 6.9 %all-to-all-start.2 = ((f32[16,32,256]{2,1,0:T(8,128)}), f32[16,32,256]{2,1,0:T(8,128)S(1)}, u32[]{:S(2)}, u32[]{:S(2)}) async-start(f32[16,32,256]{2,1,0:T(8,128)} %broadcast_in_dim.21), calls=%async_computation.2 | async-start | bytes 1048576 | tf_op jit(solution)/shard_map/all_to_all | solution.py:307
  73.1 3.7 %shard_map.84 = (f32[512,256]{1,0:T(8,128)}, f32[512,256]{1,0:T(8,128)}, bf16[1024,256]{1,0:T(8,128)(2,1)}, bf16[1024,256]{1,0:T(8,128)(2,1)}) custom-call(f32[512,256]{1,0:T(8,128)} %own_hbm.1, f32[512,256]{1,0:T(8,128)} %copy-done.2, f32[1024,256]{1,0:T(8,128)} %shard_map.83.here_hbm, f32[1024,256]{1,0:T(8,128)} %copy-done.4), custom_call_target="tpu_custom_call" | custom-call | flops 1000000 | bytes 5000000 | tf_op jit(solution)/shard_map/pallas_call | solution.py:296
  76.8 5.3 %all-to-all-done.2 = f32[16,32,256]{2,1,0:T(8,128)S(1)} async-done(((f32[16,32,256]{2,1,0:T(8,128)}), f32[16,32,256]{2,1,0:T(8,128)S(1)}, u32[]{:S(2)}, u32[]{:S(2)}) %all-to-all-start.2) | async-done | bytes 524320 | tf_op jit(solution)/shard_map/all_to_all | solution.py:307
  82.1 6.1 %shard_map.86 = (f32[512,256]{1,0:T(8,128)}, bf16[4,512,256]{2,1,0:T(8,128)(2,1)}, bf16[4,512,256]{2,1,0:T(8,128)(2,1)}) custom-call(s32[32]{0:T(128)S(1)} %get-tuple-element.56.own_map, s32[32]{0:T(128)S(1)} %fusion.4.other_map, f32[512,256]{1,0:T(8,128)S(1)} %bitcast.22, bf16[1024,256]{1,0:T(8,128)(2,1)} %get-tuple-element.38.top_hbm, ...), custom_call_target="tpu_custom_call" | custom-call | flops 1600000000 | bytes 6000000 | tf_op jit(solution)/shard_map/pallas_call | solution.py:207
  88.2 3.6 %all-to-all-start.3 = ((f32[16,32,256]{2,1,0:T(8,128)}), f32[16,32,256]{2,1,0:T(8,128)S(1)}, u32[]{:S(2)}, u32[]{:S(2)}) async-start(f32[16,32,256]{2,1,0:T(8,128)} %bitcast.11), calls=%async_computation.3 | async-start | bytes 1048576 | tf_op jit(solution)/shard_map/all_to_all | solution.py:307
  91.8 4.2 %shard_map.87.here_hbm = f32[1024,256]{1,0:T(8,128)} custom-call(bf16[4,512,256]{2,1,0:T(8,128)(2,1)} %get-tuple-element.41.err_top_hbm, bf16[4,512,256]{2,1,0:T(8,128)(2,1)} %get-tuple-element.42.err_low_hbm, f32[512,256]{1,0:T(8,128)S(1)} %bitcast.23), custom_call_target="tpu_custom_call" | custom-call | flops 800000000 | bytes 4000000 | tf_op jit(solution)/shard_map/pallas_call | solution.py:244
  96.0 4.3 %collective-permute-start.5 = (f32[1024,256]{1,0:T(8,128)}, f32[1024,256]{1,0:T(8,128)S(1)}, u32[]{:S(2)}, u32[]{:S(2)}) collective-permute-start(f32[1024,256]{1,0:T(8,128)} %shard_map.87.here_hbm), channel_id=1, source_target_pairs={{0,1},{1,0},{2,3},{3,2},{4,5},{5,4},{6,7},{7,6},{8,9},{9,8},{10,11... | collective-permute-start | bytes 3145736 | tf_op jit(solution)/shard_map/ppermute | solution.py:303
  100.3 3.0 %shard_map.89 = (f32[16,64,128]{2,1,0:T(8,128)}, f32[17,64,128]{2,1,0:T(8,128)}) custom-call(s32[1]{0:T(128)} %bitcast.2.core_ref, s32[96]{0:T(128)} %reshape.65.map_ref, bf16[3,16,128,128]{3,2,1,0:T(8,128)(2,1)} %tiles_hbm.5), custom_call_target="tpu_custom_call" | custom-call | flops 1000000 | bytes 1600000 | tf_op jit(solution)/shard_map/pallas_call | solution.py:110
  103.3 1.9 %collective-permute-start.6 = (f32[17,64,128]{2,1,0:T(8,128)}, f32[17,64,128]{2,1,0:T(8,128)S(1)}, u32[]{:S(2)}, u32[]{:S(2)}) collective-permute-start(f32[17,64,128]{2,1,0:T(8,128)} %get-tuple-element.44), channel_id=1, source_target_pairs={{0,1},{1,0},{2,3},{3,2},{4,5},{5,4},{6,7},{7,6},{8,9},{9,8},{10,11... | collective-permute-start | bytes 1671176 | tf_op jit(solution)/shard_map/ppermute | solution.py:303
  105.3 4.9 %collective-permute-start.7 = (f32[32,256]{1,0:T(8,128)S(1)}, f32[32,256]{1,0:T(8,128)S(1)}, u32[]{:S(2)}, u32[]{:S(2)}) collective-permute-start(f32[32,256]{1,0:T(8,128)S(1)} %multiply_add_fusion.1), channel_id=1, source_target_pairs={{32,0},{64,32},{96,64},{128,96},{160,128},{192,160},{224,192},{256... | collective-permute-start | bytes 98312 | tf_op jit(solution)/shard_map/ppermute | solution.py:313
  112.0 6.9 %all-to-all-start.4 = ((f32[16,32,256]{2,1,0:T(8,128)}), f32[16,32,256]{2,1,0:T(8,128)S(1)}, u32[]{:S(2)}, u32[]{:S(2)}) async-start(f32[16,32,256]{2,1,0:T(8,128)} %broadcast_in_dim.22), calls=%async_computation.4 | async-start | bytes 1048576 | tf_op jit(solution)/shard_map/all_to_all | solution.py:307
  120.0 3.7 %shard_map.88 = (f32[512,256]{1,0:T(8,128)}, f32[512,256]{1,0:T(8,128)}, bf16[1024,256]{1,0:T(8,128)(2,1)}, bf16[1024,256]{1,0:T(8,128)(2,1)}) custom-call(f32[512,256]{1,0:T(8,128)} %get-tuple-element.34.own_hbm, f32[512,256]{1,0:T(8,128)} %get-tuple-element.35.other_hbm, f32[1024,256]{1,0:T(8,128)} %shard_map.87.here_hbm, f32[1024,256]{1,0:T(8,128)} %copy-done.3), custom_call_target="tpu_custom_call" | custom-call | flops 1000000 | bytes 5000000 | tf_op jit(solution)/shard_map/pallas_call | solution.py:296
  123.7 5.4 %all-to-all-done.4 = f32[16,32,256]{2,1,0:T(8,128)S(1)} async-done(((f32[16,32,256]{2,1,0:T(8,128)}), f32[16,32,256]{2,1,0:T(8,128)S(1)}, u32[]{:S(2)}, u32[]{:S(2)}) %all-to-all-start.4) | async-done | bytes 524320 | tf_op jit(solution)/shard_map/all_to_all | solution.py:307
  129.1 6.1 %shard_map.90 = (f32[512,256]{1,0:T(8,128)}, bf16[4,512,256]{2,1,0:T(8,128)(2,1)}, bf16[4,512,256]{2,1,0:T(8,128)(2,1)}) custom-call(s32[32]{0:T(128)S(1)} %get-tuple-element.55.own_map, s32[32]{0:T(128)S(1)} %fusion.3.other_map, f32[512,256]{1,0:T(8,128)S(1)} %bitcast.24, bf16[1024,256]{1,0:T(8,128)(2,1)} %get-tuple-element.46.top_hbm, ...), custom_call_target="tpu_custom_call" | custom-call | flops 1600000000 | bytes 6000000 | tf_op jit(solution)/shard_map/pallas_call | solution.py:207
  135.1 4.2 %shard_map.91 = f32[1024,256]{1,0:T(8,128)} custom-call(bf16[4,512,256]{2,1,0:T(8,128)(2,1)} %get-tuple-element.49.err_top_hbm, bf16[4,512,256]{2,1,0:T(8,128)(2,1)} %get-tuple-element.50.err_low_hbm, f32[512,256]{1,0:T(8,128)S(1)} %bitcast.25), custom_call_target="tpu_custom_call" | custom-call | flops 800000000 | bytes 4000000 | tf_op jit(solution)/shard_map/pallas_call | solution.py:244
  139.4 1.2 slice.36
  140.6 4.3 %collective-permute-start.8 = (f32[512,256]{1,0:T(8,128)S(1)}, f32[512,256]{1,0:T(8,128)S(1)}, u32[]{:S(2)}, u32[]{:S(2)}) collective-permute-start(f32[512,256]{1,0:T(8,128)S(1)} %slice.36), channel_id=1, source_target_pairs={{0,1},{1,0},{2,3},{3,2},{4,5},{5,4},{6,7},{7,6},{8,9},{9,8},{10,11... | collective-permute-start | bytes 1572872 | tf_op jit(solution)/shard_map/ppermute | solution.py:303
  144.8 3.6 %all-to-all-start.5 = ((f32[16,32,256]{2,1,0:T(8,128)}), f32[16,32,256]{2,1,0:T(8,128)S(1)}, u32[]{:S(2)}, u32[]{:S(2)}) async-start(f32[16,32,256]{2,1,0:T(8,128)} %bitcast.13), calls=%async_computation.5 | async-start | bytes 1048576 | tf_op jit(solution)/shard_map/all_to_all | solution.py:307
  149.4 10.4 %all-to-all-done.5 = f32[16,32,256]{2,1,0:T(8,128)S(1)} async-done(((f32[16,32,256]{2,1,0:T(8,128)}), f32[16,32,256]{2,1,0:T(8,128)S(1)}, u32[]{:S(2)}, u32[]{:S(2)}) %all-to-all-start.5) | async-done | bytes 524320 | tf_op jit(solution)/shard_map/all_to_all | solution.py:307
  (49 shorter events, 11.4 us)
Async XLA Ops:
  0.6 14.0 %copy-start.1 = (f32[512,256]{1,0:T(8,128)S(1)}, f32[512,256]{1,0:T(8,128)}, u32[]{:S(2)}) copy-start(f32[512,256]{1,0:T(8,128)} %own_hbm.1) | copy-start | bytes 1572868
  0.6 15.9 %copy-start.6 = (f32[32,256]{1,0:T(8,128)S(1)}, f32[32,256]{1,0:T(8,128)}, u32[]{:S(2)}) copy-start(f32[32,256]{1,0:T(8,128)} %param.7) | copy-start | bytes 98308
  5.9 18.3 %collective-permute-start.1 = (f32[17,64,128]{2,1,0:T(8,128)}, f32[17,64,128]{2,1,0:T(8,128)S(1)}, u32[]{:S(2)}, u32[]{:S(2)}) collective-permute-start(f32[17,64,128]{2,1,0:T(8,128)} %get-tuple-element.28), channel_id=1, source_target_pairs={{0,1},{1,0},{2,3},{3,2},{4,5},{5,4},{6,7},{7,6},{8,9},{9,8},{10,11... | collective-permute-start | bytes 1671176 | tf_op jit(solution)/shard_map/ppermute | solution.py:303
  14.6 6.4 %collective-permute-start = (f32[512,256]{1,0:T(8,128)S(1)}, f32[512,256]{1,0:T(8,128)S(1)}, u32[]{:S(2)}, u32[]{:S(2)}) collective-permute-start(f32[512,256]{1,0:T(8,128)S(1)} %copy-done.1), channel_id=1, source_target_pairs={{0,1},{1,0},{2,3},{3,2},{4,5},{5,4},{6,7},{7,6},{8,9},{9,8},{10,11... | collective-permute-start | bytes 1572872 | tf_op jit(solution)/shard_map/ppermute | solution.py:303
  17.4 14.4 %all-to-all-start = ((f32[16,32,256]{2,1,0:T(8,128)}), f32[16,32,256]{2,1,0:T(8,128)S(1)}, u32[]{:S(2)}, u32[]{:S(2)}) async-start(f32[16,32,256]{2,1,0:T(8,128)} %broadcast_in_dim.20), calls=%async_computation | async-start | bytes 1048576 | tf_op jit(solution)/shard_map/all_to_all | solution.py:307
  21.0 0.8 copy-start.2
  24.2 7.6 %copy-start.9 = (f32[17,64,128]{2,1,0:T(8,128)}, f32[17,64,128]{2,1,0:T(8,128)S(1)}, u32[]{:S(2)}) copy-start(f32[17,64,128]{2,1,0:T(8,128)S(1)} %collective-permute-done.1.other_hbm) | copy-start | bytes 1671172
  37.9 16.3 %all-to-all-start.1 = ((f32[16,32,256]{2,1,0:T(8,128)}), f32[16,32,256]{2,1,0:T(8,128)S(1)}, u32[]{:S(2)}, u32[]{:S(2)}) async-start(f32[16,32,256]{2,1,0:T(8,128)} %bitcast.7), calls=%async_computation.1 | async-start | bytes 1048576 | tf_op jit(solution)/shard_map/all_to_all | solution.py:307
  45.6 26.4 %collective-permute-start.2 = (f32[1024,256]{1,0:T(8,128)}, f32[1024,256]{1,0:T(8,128)S(1)}, u32[]{:S(2)}, u32[]{:S(2)}) collective-permute-start(f32[1024,256]{1,0:T(8,128)} %shard_map.83.here_hbm), channel_id=1, source_target_pairs={{0,1},{1,0},{2,3},{3,2},{4,5},{5,4},{6,7},{7,6},{8,9},{9,8},{10,11... | collective-permute-start | bytes 3145736 | tf_op jit(solution)/shard_map/ppermute | solution.py:303
  52.2 19.8 %collective-permute-start.3 = (f32[17,64,128]{2,1,0:T(8,128)}, f32[17,64,128]{2,1,0:T(8,128)S(1)}, u32[]{:S(2)}, u32[]{:S(2)}) collective-permute-start(f32[17,64,128]{2,1,0:T(8,128)} %get-tuple-element.36), channel_id=1, source_target_pairs={{0,1},{1,0},{2,3},{3,2},{4,5},{5,4},{6,7},{7,6},{8,9},{9,8},{10,11... | collective-permute-start | bytes 1671176 | tf_op jit(solution)/shard_map/ppermute | solution.py:303
  54.2 10.0 %collective-permute-start.4 = (f32[32,256]{1,0:T(8,128)S(1)}, f32[32,256]{1,0:T(8,128)S(1)}, u32[]{:S(2)}, u32[]{:S(2)}) collective-permute-start(f32[32,256]{1,0:T(8,128)S(1)} %multiply_add_fusion.2), channel_id=1, source_target_pairs={{32,0},{64,32},{96,64},{128,96},{160,128},{192,160},{224,192},{256... | collective-permute-start | bytes 98312 | tf_op jit(solution)/shard_map/ppermute | solution.py:313
  65.1 17.0 %all-to-all-start.2 = ((f32[16,32,256]{2,1,0:T(8,128)}), f32[16,32,256]{2,1,0:T(8,128)S(1)}, u32[]{:S(2)}, u32[]{:S(2)}) async-start(f32[16,32,256]{2,1,0:T(8,128)} %broadcast_in_dim.21), calls=%async_computation.2 | async-start | bytes 1048576 | tf_op jit(solution)/shard_map/all_to_all | solution.py:307
  72.0 10.1 %copy-start.8 = (f32[17,64,128]{2,1,0:T(8,128)}, f32[17,64,128]{2,1,0:T(8,128)S(1)}, u32[]{:S(2)}) copy-start(f32[17,64,128]{2,1,0:T(8,128)S(1)} %collective-permute-done.3.other_hbm) | copy-start | bytes 1671172
  72.0 1.0 copy-start.4
  88.2 17.0 %all-to-all-start.3 = ((f32[16,32,256]{2,1,0:T(8,128)}), f32[16,32,256]{2,1,0:T(8,128)S(1)}, u32[]{:S(2)}, u32[]{:S(2)}) async-start(f32[16,32,256]{2,1,0:T(8,128)} %bitcast.11), calls=%async_computation.3 | async-start | bytes 1048576 | tf_op jit(solution)/shard_map/all_to_all | solution.py:307
  96.0 23.0 %collective-permute-start.5 = (f32[1024,256]{1,0:T(8,128)}, f32[1024,256]{1,0:T(8,128)S(1)}, u32[]{:S(2)}, u32[]{:S(2)}) collective-permute-start(f32[1024,256]{1,0:T(8,128)} %shard_map.87.here_hbm), channel_id=1, source_target_pairs={{0,1},{1,0},{2,3},{3,2},{4,5},{5,4},{6,7},{7,6},{8,9},{9,8},{10,11... | collective-permute-start | bytes 3145736 | tf_op jit(solution)/shard_map/ppermute | solution.py:303
  103.3 15.7 %collective-permute-start.6 = (f32[17,64,128]{2,1,0:T(8,128)}, f32[17,64,128]{2,1,0:T(8,128)S(1)}, u32[]{:S(2)}, u32[]{:S(2)}) collective-permute-start(f32[17,64,128]{2,1,0:T(8,128)} %get-tuple-element.44), channel_id=1, source_target_pairs={{0,1},{1,0},{2,3},{3,2},{4,5},{5,4},{6,7},{7,6},{8,9},{9,8},{10,11... | collective-permute-start | bytes 1671176 | tf_op jit(solution)/shard_map/ppermute | solution.py:303
  105.3 5.9 %collective-permute-start.7 = (f32[32,256]{1,0:T(8,128)S(1)}, f32[32,256]{1,0:T(8,128)S(1)}, u32[]{:S(2)}, u32[]{:S(2)}) collective-permute-start(f32[32,256]{1,0:T(8,128)S(1)} %multiply_add_fusion.1), channel_id=1, source_target_pairs={{32,0},{64,32},{96,64},{128,96},{160,128},{192,160},{224,192},{256... | collective-permute-start | bytes 98312 | tf_op jit(solution)/shard_map/ppermute | solution.py:313
  112.0 17.0 %all-to-all-start.4 = ((f32[16,32,256]{2,1,0:T(8,128)}), f32[16,32,256]{2,1,0:T(8,128)S(1)}, u32[]{:S(2)}, u32[]{:S(2)}) async-start(f32[16,32,256]{2,1,0:T(8,128)} %broadcast_in_dim.22), calls=%async_computation.4 | async-start | bytes 1048576 | tf_op jit(solution)/shard_map/all_to_all | solution.py:307
  118.9 10.1 %copy-start.7 = (f32[17,64,128]{2,1,0:T(8,128)}, f32[17,64,128]{2,1,0:T(8,128)S(1)}, u32[]{:S(2)}) copy-start(f32[17,64,128]{2,1,0:T(8,128)S(1)} %collective-permute-done.6.other_hbm) | copy-start | bytes 1671172
  119.0 1.0 copy-start.3
  139.4 9.1 %copy-start = (f32[1024,256]{1,0:T(8,128)S(1)}, f32[1024,256]{1,0:T(8,128)}, u32[]{:S(2)}) copy-start(f32[1024,256]{1,0:T(8,128)} %shard_map.91) | copy-start | bytes 3145732
  139.4 9.1 %copy-start.5 = (f32[512,256]{1,0:T(8,128)S(1)}, f32[512,256]{1,0:T(8,128)}, u32[]{:S(2)}) copy-start(f32[512,256]{1,0:T(8,128)} %get-tuple-element.43) | copy-start | bytes 1572868
  140.6 7.9 %collective-permute-start.8 = (f32[512,256]{1,0:T(8,128)S(1)}, f32[512,256]{1,0:T(8,128)S(1)}, u32[]{:S(2)}, u32[]{:S(2)}) collective-permute-start(f32[512,256]{1,0:T(8,128)S(1)} %slice.36), channel_id=1, source_target_pairs={{0,1},{1,0},{2,3},{3,2},{4,5},{5,4},{6,7},{7,6},{8,9},{9,8},{10,11... | collective-permute-start | bytes 1572872 | tf_op jit(solution)/shard_map/ppermute | solution.py:303
  144.8 14.9 %all-to-all-start.5 = ((f32[16,32,256]{2,1,0:T(8,128)}), f32[16,32,256]{2,1,0:T(8,128)S(1)}, u32[]{:S(2)}, u32[]{:S(2)}) async-start(f32[16,32,256]{2,1,0:T(8,128)} %bitcast.13), calls=%async_computation.5 | async-start | bytes 1048576 | tf_op jit(solution)/shard_map/all_to_all | solution.py:307

commit v2 on v1

v2 whole, which is shorter than its diff:
```python
import functools

import jax
import jax.numpy as jnp
from jax import lax
from jax.experimental import pallas as pl
from jax.experimental.pallas import tpu as pltpu
from jax.sharding import PartitionSpec as P

R = 256
P_SIZE = 1024
TILE = 128
HALF = TILE // 2
TICKS = 3
K_MAX = 16
U_DEV = 512
U_TILES = U_DEV // TILE
I_TILES = P_SIZE // TILE
ITEMS_CORE = P_SIZE // 2
CHIPS = 16
SHARE = 32
CELLS = U_TILES * I_TILES

user_rate = 0.02
item_rate = 0.005
shrink_rate = 0.05
bf16 = jnp.bfloat16
f32 = jnp.float32

SAME_CORE = [[2 * chip + core for chip in range(CHIPS)] for core in range(2)]
PARTNERS = [(i, i ^ 1) for i in range(2 * CHIPS)]


def halves(x):
    top = x.astype(bf16)
    return top, (x - top.astype(f32)).astype(bf16)


def dot3(a, b, dims):
    (a_top, a_low), (b_top, b_low) = a, b
    dot = lambda x, y: lax.dot_general(x, y, (dims, ((), ())), preferred_element_type=f32)
    return dot(a_top, b_top) + (dot(a_top, b_low) + dot(a_low, b_top))


VMEM = pl.BlockSpec(memory_space=pltpu.VMEM)
ANY = pl.BlockSpec(memory_space=pl.ANY)
SMEM = pl.BlockSpec(memory_space=pltpu.SMEM)
WIDTH = 2 * TILE
BLOCKS = 2 * U_DEV // WIDTH
STEP_GRANT = 53800
UPDATE_GRANT = 60 * 1024


def shape(dims, dtype):
    return jax.ShapeDtypeStruct(dims, dtype)


def call(kernel, outs, in_specs, out_specs, scratch, flops, nbytes, grant=60 * 1024):
    return pl.pallas_call(
        kernel,
        out_shape=outs,
        in_specs=in_specs,
        out_specs=out_specs,
        scratch_shapes=scratch,
        compiler_params=pltpu.CompilerParams(vmem_limit_bytes=grant * 1024),
        cost_estimate=pl.CostEstimate(flops=flops, bytes_accessed=nbytes, transcendentals=0),
    )


def turn_kernel(tick, core_ref, map_ref, tiles_hbm, kept_hbm, sent_hbm, tiles, kept, sent, turned, sems):
    core = core_ref[0]
    group = K_MAX // 4

    def fetch(g):
        slots = pl.ds(g * group, group)
        return pltpu.make_async_copy(tiles_hbm.at[tick, slots], tiles.at[slots], sems.at[g])

    def put(g, which):
        buf, hbm = ((kept, kept_hbm), (sent, sent_hbm))[which]
        slots = pl.ds(g * group, group)
        return pltpu.make_async_copy(buf.at[slots], hbm.at[slots], sems.at[4 + 2 * g + which])

    for g in range(4):
        fetch(g).start()
    lane = lax.broadcasted_iota(jnp.int32, (8, TILE), 1)
    row = jnp.zeros((8, TILE), jnp.int32)
    for cell in range(CELLS):
        row = jnp.where(lane == cell, map_ref[tick * CELLS + cell], row)
    sent[K_MAX, pl.ds(0, 8), :] = row.astype(f32)
    sent[K_MAX, pl.ds(8, HALF - 8), :] = jnp.zeros((HALF - 8, TILE), f32)
    last = pltpu.make_async_copy(sent.at[pl.ds(K_MAX, 1)], sent_hbm.at[pl.ds(K_MAX, 1)], sems.at[12])
    last.start()
    for g in range(4):
        fetch(g).wait()
        for k in range(g * group, (g + 1) * group):
            turned[k] = tiles[k].T
            for part in range(2):
                rows = pl.ds(part * SHARE, SHARE)
                mine = pl.multiple_of(part * HALF + core * SHARE, SHARE)
                theirs = pl.multiple_of(part * HALF + (1 - core) * SHARE, SHARE)
                kept[k, rows, :] = turned[k, pl.ds(mine, SHARE), :]
                sent[k, rows, :] = turned[k, pl.ds(theirs, SHARE), :].astype(f32)
        put(g, 0).start()
        put(g, 1).start()
    for g in range(4):
        put(g, 0).wait()
        put(g, 1).wait()
    last.wait()


def turned_tiles(tick, core, slot_map, ratings):
    tile = pltpu.VMEM((K_MAX, TILE, TILE), bf16)
    return call(
        functools.partial(turn_kernel, tick),
        (shape((K_MAX, HALF, TILE), bf16), shape((K_MAX + 1, HALF, TILE), f32)),
        [SMEM, SMEM, ANY], (ANY, ANY),
        [tile, pltpu.VMEM((K_MAX, HALF, TILE), bf16), pltpu.VMEM((K_MAX + 1, HALF, TILE), f32), tile,
         pltpu.SemaphoreType.DMA((13,))],
        1000000, 1600000,
    )(core, slot_map, ratings)


def step_kernel(own_map, other_map, panel_hbm, own_users, other_users, own_hbm, other_hbm, item_hbm, user_hbm,
                panel_ref, users, own_tiles, other_tiles, predicted, item_grad, user_grad, sems):
    half = BLOCKS // 2
    parts = ITEMS_CORE // TILE

    def rows(block):
        return pl.ds(block * WIDTH, WIDTH)

    panel_load = pltpu.make_async_copy(panel_hbm, panel_ref, sems.at[0])
    own_load = pltpu.make_async_copy(own_hbm, own_tiles, sems.at[1])
    other_load = pltpu.make_async_copy(other_hbm.at[pl.ds(0, K_MAX)], other_tiles, sems.at[2])
    user_loads = [
        pltpu.make_async_copy(
            (own_users if block < half else other_users).at[rows(block % half)], users.at[rows(block)],
            sems.at[3 + block])
        for block in range(BLOCKS)
    ]
    for copy in [panel_load, user_loads[0], own_load, *user_loads[1:], other_load]:
        copy.start()

    def send_items(part):
        cut = pl.ds(part * TILE, TILE)
        return pltpu.make_async_copy(item_grad.at[cut], item_hbm.at[cut], sems.at[3 + BLOCKS + part])

    def send_users(block):
        return pltpu.make_async_copy(
            user_grad.at[rows(block)], user_hbm.at[rows(block)], sems.at[3 + BLOCKS + parts + block])

    panel_load.wait()
    panel = halves(panel_ref[...])

    def predict(block):
        user_loads[block].wait()
        split = halves(users[rows(block), :])
        predicted[block] = dot3(panel, split, ((1,), (1,)))
        return split

    split = predict(0)
    for block in range(BLOCKS):
        after = predict(block + 1) if block + 1 < BLOCKS else None
        slot_map, tiles = (own_map, own_tiles) if block < half else (other_map, other_tiles)
        if block % half == 0:
            (own_load if block < half else other_load).wait()
        tops, lows = [], []
        for item in range(I_TILES):
            cut = pl.ds(item * HALF, HALF)
            errors = []
            for part in range(2):
                slot = slot_map[(block * 2 + part) % U_TILES * I_TILES + item]
                error = tiles[jnp.maximum(slot, 0)].astype(f32) - predicted[block, cut, pl.ds(part * TILE, TILE)]
                errors.append(jnp.where(slot >= 0, error, 0.0))
            top, low = halves(jnp.concatenate(errors, axis=1))
            tops.append(top)
            lows.append(low)
        error = jnp.concatenate(tops, axis=0), jnp.concatenate(lows, axis=0)
        user_grad[rows(block), :] = dot3(error, panel, ((0,), (0,)))
        send_users(block).start()
        if block == 0:
            item_grad[...] = dot3(error, split, ((1,), (0,)))
        elif block + 1 < BLOCKS:
            item_grad[...] += dot3(error, split, ((1,), (0,)))
        else:
            for part in range(parts):
                cut = slice(part * TILE, (part + 1) * TILE)
                item_grad[cut, :] += dot3((error[0][cut], error[1][cut]), split, ((1,), (0,)))
                send_items(part).start()
        split = after
    for block in range(BLOCKS):
        send_users(block).wait()
    for part in range(parts):
        send_items(part).wait()


def item_and_user_grads(own_map, other_map, panel, own, other, own_tiles, other_tiles):
    half_panel = pltpu.VMEM((ITEMS_CORE, R), f32)
    both = pltpu.VMEM((2 * U_DEV, R), f32)
    cut = (K_MAX, HALF, TILE)
    return call(
        step_kernel,
        (shape((ITEMS_CORE, R), f32), shape((2 * U_DEV, R), f32)),
        [SMEM] * 2 + [ANY] * 5, (ANY,) * 2,
        [half_panel, both, pltpu.VMEM(cut, bf16), pltpu.VMEM(cut, f32),
         pltpu.VMEM((BLOCKS, ITEMS_CORE, WIDTH), f32), half_panel, both,
         pltpu.SemaphoreType.DMA((3 + 2 * BLOCKS + ITEMS_CORE // TILE,))],
        2400000000, 4000000, STEP_GRANT,
    )(own_map, other_map, panel, own, other, own_tiles, other_tiles)


def stepped(user, here, there):
    return user * (1.0 - user_rate * shrink_rate) + user_rate * (here + there)


def update_kernel(own_hbm, other_hbm, here_hbm, there_hbm, own_out, other_out, user, here, there, sems):
    half = BLOCKS // 2

    def rows(block):
        return pl.ds(block * WIDTH, WIDTH)

    def part(block, own, other):
        return (own if block < half else other).at[rows(block % half)]

    def fetch(block, which):
        source, into = (
            (part(block, own_hbm, other_hbm), user),
            (here_hbm.at[rows(block)], here),
            (there_hbm.at[rows((block + half) % BLOCKS)], there),
        )[which]
        return pltpu.make_async_copy(source, into.at[rows(block)], sems.at[4 * block + which])

    def put(block):
        return pltpu.make_async_copy(user.at[rows(block)], part(block, own_out, other_out), sems.at[4 * block + 3])

    for block in range(BLOCKS):
        for which in range(3):
            fetch(block, which).start()
    for block in range(BLOCKS):
        for which in range(3):
            fetch(block, which).wait()
        user[rows(block), :] = stepped(user[rows(block), :], here[rows(block), :], there[rows(block), :])
        put(block).start()
    for block in range(BLOCKS):
        put(block).wait()


def updated_users(own, other, here, there):
    new = shape((U_DEV, R), f32)
    both = pltpu.VMEM((2 * U_DEV, R), f32)
    return call(
        update_kernel, (new, new), [ANY] * 4, (ANY, ANY),
        [both, both, both, pltpu.SemaphoreType.DMA((4 * BLOCKS,))], 1000000, 4000000, UPDATE_GRANT,
    )(own, other, here, there)


def swapped(x):
    return lax.ppermute(x, "owner", PARTNERS)


def exchanged(blocks):
    return lax.all_to_all(blocks, "owner", split_axis=0, concat_axis=0, axis_index_groups=SAME_CORE, tiled=True)


def passed_along(block, axis, distance):
    devices = range(lax.axis_size(axis))
    route = [((i - distance) % len(devices), i) for i in devices]
    return lax.ppermute(block, axis, route)


def slot_maps(tile_users, tile_items, tile_count):
    slots = jnp.arange(K_MAX)[None, :, None]
    cell = (tile_users * I_TILES + tile_items)[:, :, None]
    live = (slots < tile_count[:, :, None]) & (cell == jnp.arange(CELLS)[None, None, :])
    return jnp.max(jnp.where(live, slots, -1), axis=1).astype(jnp.int32)


def shards(user_factors, item_factors, ratings, tile_users, tile_items, tile_count):
    core = lax.rem(lax.axis_index("owner"), 2).reshape(1)
    own, share = user_factors, item_factors
    other = swapped(own)
    own_map = slot_maps(tile_users, tile_items, tile_count)
    for tick in range(TICKS):
        kept, sent = turned_tiles(tick, core, own_map.reshape(-1), ratings)
        got = swapped(sent)
        other_map = got[K_MAX, 0, :CELLS].astype(jnp.int32)
        panel = exchanged(jnp.broadcast_to(share[None], (CHIPS, SHARE, R))).reshape(ITEMS_CORE, R)
        item_grad, here = item_and_user_grads(own_map[tick], other_map, panel, own, other, kept, got)
        parts = exchanged(item_grad.reshape(CHIPS, SHARE, R))
        if tick + 1 < TICKS:
            there = swapped(here)
            own, other = updated_users(own, other, here, there)
        else:
            there = swapped(here[U_DEV:])
            own, parts = lax.optimization_barrier((stepped(own, here[:U_DEV], there), parts))
        share = share * (1.0 - item_rate * shrink_rate) + item_rate * parts.sum(axis=0)
        if tick + 1 < TICKS:
            share = passed_along(share, "band", -1)
    return own, share


def solution(mesh):
    placed = (
        P(("band", "owner"), None),
        P(("band", "owner"), None),
        P(None, ("band", "owner"), None, None),
        P(None, ("band", "owner")),
        P(None, ("band", "owner")),
        P(None, ("band", "owner")),
    )
    return jax.shard_map(
        shards,
        mesh=mesh,
        in_specs=placed,
        out_specs=(P(("band", "owner"), None), P(("band", "owner"), None)),
        check_vma=False,
    )
```

time: 162 us -> 152 us (0.938)
  Pallas kernels: 49.5 us -> 34.6 us
  waiting for transfers between devices: 30.7 us -> 38 us
  starting transfers between devices: 68.5 us -> 66.7 us
    pallas_call x12 -> x8, Pallas kernels: 49.5 us -> 34.6 us  [the longest x3 20.7 us: item_and_user_grads(): call(step_kernel, (shape((ITEMS_CORE, R), f32), shape((2 * U_DEV, R), f32...]
    all_to_all x6, waiting for transfers between devices: 28.7 us -> 35.9 us  [exchanged(): lax.all_to_all(blocks, 'owner', split_axis=0, concat_axis=0, axis_index_g...]
  transfers between devices with their start and end apart: 15 -> 15, of which waited for: 6 -> 8; matrix products, arithmetic and copies ran while one was open for 2% -> 2% of each run, Pallas kernels for 15% -> 7%
where the time goes in v2:
time: 152 us; the launch traced here: 151 us
  starting transfers between devices  66.7 us (44%)
  waiting for transfers between devices  38 us (25%)
  Pallas kernels  34.6 us (23%)
  local copies, waits for them, and re-layouts  7.07 us (5%)
  other arithmetic  3.24 us (2%)
    all_to_all x6, waiting for transfers between devices, exchanged(): lax.all_to_all(blocks, 'owner', split_axis=0, concat_axis=0, axis_index_g...  35.9 us
    all_to_all x6, starting transfers between devices, exchanged(): lax.all_to_all(blocks, 'owner', split_axis=0, concat_axis=0, axis_index_g...  26.7 us
    ppermute x7, starting transfers between devices, swapped(): return lax.ppermute(x, 'owner', PARTNERS)  26.7 us
    pallas_call x3, Pallas kernels, item_and_user_grads(): call(step_kernel, (shape((ITEMS_CORE, R), f32), shape((2 * U_DEV, R), f32...  20.7 us
    ppermute x2, starting transfers between devices, passed_along(): return lax.ppermute(block, axis, route)  13.3 us
    pallas_call x3, Pallas kernels, turned_tiles(): call(functools.partial(turn_kernel, tick), (shape((K_MAX, HALF, TILE), bf...  8.49 us
    pallas_call x2, Pallas kernels, updated_users(): call(update_kernel, (new, new), [ANY] * 4, (ANY, ANY), [both, both, both,...  5.41 us
  transfers between devices with their start and end apart: 15, of which 8 were waited for; matrix products, arithmetic and copies ran while one was open for 2% of the time, Pallas kernels for 7%

profile of v2, /device:TPU:1, one launch (start us, length us, event | category | flops | bytes accessed | tf_op | source)
XLA Modules:
  0.0 150.6 jit_solution(17944461735503192955)
XLA Ops:
  2.8 2.8 %shard_map.80 = (bf16[16,64,128]{2,1,0:T(8,128)(2,1)}, f32[17,64,128]{2,1,0:T(8,128)}) custom-call(s32[1]{0:T(128)} %bitcast.2.core_ref, s32[96]{0:T(128)} %reshape.65.map_ref, bf16[3,16,128,128]{3,2,1,0:T(8,128)(2,1)} %tiles_hbm.5), custom_call_target="tpu_custom_call" | custom-call | flops 1000000 | bytes 1600000 | tf_op jit(solution)/shard_map/pallas_call | solution.py:113
  5.7 8.9 %collective-permute-start.1 = (f32[17,64,128]{2,1,0:T(8,128)}, f32[17,64,128]{2,1,0:T(8,128)S(1)}, u32[]{:S(2)}, u32[]{:S(2)}) collective-permute-start(f32[17,64,128]{2,1,0:T(8,128)} %get-tuple-element.20), channel_id=1, source_target_pairs={{0,1},{1,0},{2,3},{3,2},{4,5},{5,4},{6,7},{7,6},{8,9},{9,8},{10,11... | collective-permute-start | bytes 1671176 | tf_op jit(solution)/shard_map/ppermute | solution.py:257
  14.6 1.9 %collective-permute-start = (f32[512,256]{1,0:T(8,128)S(1)}, f32[512,256]{1,0:T(8,128)S(1)}, u32[]{:S(2)}, u32[]{:S(2)}) collective-permute-start(f32[512,256]{1,0:T(8,128)S(1)} %copy-done.6), channel_id=1, source_target_pairs={{0,1},{1,0},{2,3},{3,2},{4,5},{5,4},{6,7},{7,6},{8,9},{9,8},{10,11... | collective-permute-start | bytes 1572872 | tf_op jit(solution)/shard_map/ppermute | solution.py:257
  17.4 3.6 %all-to-all-start = ((f32[16,32,256]{2,1,0:T(8,128)}), f32[16,32,256]{2,1,0:T(8,128)S(1)}, u32[]{:S(2)}, u32[]{:S(2)}) async-start(f32[16,32,256]{2,1,0:T(8,128)} %broadcast_in_dim.20), calls=%async_computation | async-start | bytes 1048576 | tf_op jit(solution)/shard_map/all_to_all | solution.py:261
  21.0 10.8 %all-to-all-done = f32[16,32,256]{2,1,0:T(8,128)S(1)} async-done(((f32[16,32,256]{2,1,0:T(8,128)}), f32[16,32,256]{2,1,0:T(8,128)S(1)}, u32[]{:S(2)}, u32[]{:S(2)}) %all-to-all-start) | async-done | bytes 524320 | tf_op jit(solution)/shard_map/all_to_all | solution.py:261
  32.5 6.9 %shard_map.81 = (f32[512,256]{1,0:T(8,128)}, f32[1024,256]{1,0:T(8,128)}) custom-call(s32[32]{0:T(128)S(1)} %get-tuple-element.38.own_map, s32[32]{0:T(128)S(1)} %fusion.3.other_map, f32[512,256]{1,0:T(8,128)S(1)} %bitcast.22, f32[512,256]{1,0:T(8,128)} %own_hbm.1, f32[512,256]{1,0:T(8,128)} %copy-done.7, bf16[16,64,128]{2,1,0:T(8,128)(2,1)S(1)} %copy-done.2, ...), custom_call_target="tpu_custom_call" | custom-call | flops 2400000000 | bytes 4000000 | tf_op jit(solution)/shard_map/pallas_call | solution.py:200
  39.4 3.6 %all-to-all-start.1 = ((f32[16,32,256]{2,1,0:T(8,128)}), f32[16,32,256]{2,1,0:T(8,128)S(1)}, u32[]{:S(2)}, u32[]{:S(2)}) async-start(f32[16,32,256]{2,1,0:T(8,128)} %bitcast.7), calls=%async_computation.1 | async-start | bytes 1048576 | tf_op jit(solution)/shard_map/all_to_all | solution.py:261
  43.0 3.6 %collective-permute-start.2 = (f32[1024,256]{1,0:T(8,128)}, f32[1024,256]{1,0:T(8,128)S(1)}, u32[]{:S(2)}, u32[]{:S(2)}) collective-permute-start(f32[1024,256]{1,0:T(8,128)} %get-tuple-element.22.here_hbm), channel_id=1, source_target_pairs={{0,1},{1,0},{2,3},{3,2},{4,5},{5,4},{6,7},{7,6},{8,9},{9,8},{10,11... | collective-permute-start | bytes 3145736 | tf_op jit(solution)/shard_map/ppermute | solution.py:257
  46.6 2.8 %shard_map.83 = (bf16[16,64,128]{2,1,0:T(8,128)(2,1)}, f32[17,64,128]{2,1,0:T(8,128)}) custom-call(s32[1]{0:T(128)} %bitcast.2.core_ref, s32[96]{0:T(128)} %reshape.65.map_ref, bf16[3,16,128,128]{3,2,1,0:T(8,128)(2,1)} %tiles_hbm.5), custom_call_target="tpu_custom_call" | custom-call | flops 1000000 | bytes 1600000 | tf_op jit(solution)/shard_map/pallas_call | solution.py:113
  49.4 1.9 %collective-permute-start.3 = (f32[17,64,128]{2,1,0:T(8,128)}, f32[17,64,128]{2,1,0:T(8,128)S(1)}, u32[]{:S(2)}, u32[]{:S(2)}) collective-permute-start(f32[17,64,128]{2,1,0:T(8,128)} %get-tuple-element.25), channel_id=1, source_target_pairs={{0,1},{1,0},{2,3},{3,2},{4,5},{5,4},{6,7},{7,6},{8,9},{9,8},{10,11... | collective-permute-start | bytes 1671176 | tf_op jit(solution)/shard_map/ppermute | solution.py:257
  51.4 1.8 %all-to-all-done.1 = f32[16,32,256]{2,1,0:T(8,128)S(1)} async-done(((f32[16,32,256]{2,1,0:T(8,128)}), f32[16,32,256]{2,1,0:T(8,128)S(1)}, u32[]{:S(2)}, u32[]{:S(2)}) %all-to-all-start.1) | async-done | bytes 524320 | tf_op jit(solution)/shard_map/all_to_all | solution.py:261
  53.2 8.6 %collective-permute-start.4 = (f32[32,256]{1,0:T(8,128)S(1)}, f32[32,256]{1,0:T(8,128)S(1)}, u32[]{:S(2)}, u32[]{:S(2)}) collective-permute-start(f32[32,256]{1,0:T(8,128)S(1)} %multiply_add_fusion.3), channel_id=1, source_target_pairs={{32,0},{64,32},{96,64},{128,96},{160,128},{192,160},{224,192},{256... | collective-permute-start | bytes 98312 | tf_op jit(solution)/shard_map/ppermute | solution.py:267
  61.7 1.0 collective-permute-done.4
  63.6 5.5 %all-to-all-start.2 = ((f32[16,32,256]{2,1,0:T(8,128)}), f32[16,32,256]{2,1,0:T(8,128)S(1)}, u32[]{:S(2)}, u32[]{:S(2)}) async-start(f32[16,32,256]{2,1,0:T(8,128)} %broadcast_in_dim.21), calls=%async_computation.2 | async-start | bytes 1048576 | tf_op jit(solution)/shard_map/all_to_all | solution.py:261
  69.2 1.0 copy-done.4
  70.2 2.7 %shard_map.82 = (f32[512,256]{1,0:T(8,128)}, f32[512,256]{1,0:T(8,128)}) custom-call(f32[512,256]{1,0:T(8,128)} %own_hbm.1, f32[512,256]{1,0:T(8,128)} %copy-done.7, f32[1024,256]{1,0:T(8,128)} %get-tuple-element.22.here_hbm, f32[1024,256]{1,0:T(8,128)} %copy-done.4), custom_call_target="tpu_custom_call" | custom-call | flops 1000000 | bytes 4000000 | tf_op jit(solution)/shard_map/pallas_call | solution.py:250
  72.9 6.4 %all-to-all-done.2 = f32[16,32,256]{2,1,0:T(8,128)S(1)} async-done(((f32[16,32,256]{2,1,0:T(8,128)}), f32[16,32,256]{2,1,0:T(8,128)S(1)}, u32[]{:S(2)}, u32[]{:S(2)}) %all-to-all-start.2) | async-done | bytes 524320 | tf_op jit(solution)/shard_map/all_to_all | solution.py:261
  79.3 6.9 %shard_map.84 = (f32[512,256]{1,0:T(8,128)}, f32[1024,256]{1,0:T(8,128)}) custom-call(s32[32]{0:T(128)S(1)} %get-tuple-element.40.own_map, s32[32]{0:T(128)S(1)} %fusion.2.other_map, f32[512,256]{1,0:T(8,128)S(1)} %bitcast.21, f32[512,256]{1,0:T(8,128)} %get-tuple-element.23.own_users.own_hbm, f32[512,256]{1,0:T(8,128)} %get-tuple-element.24.other_users.other_hbm, ...), custom_call_target="tpu_custom_call" | custom-call | flops 2400000000 | bytes 4000000 | tf_op jit(solution)/shard_map/pallas_call | solution.py:200
  86.2 3.6 %all-to-all-start.3 = ((f32[16,32,256]{2,1,0:T(8,128)}), f32[16,32,256]{2,1,0:T(8,128)S(1)}, u32[]{:S(2)}, u32[]{:S(2)}) async-start(f32[16,32,256]{2,1,0:T(8,128)} %bitcast.11), calls=%async_computation.3 | async-start | bytes 1048576 | tf_op jit(solution)/shard_map/all_to_all | solution.py:261
  89.7 4.3 %collective-permute-start.5 = (f32[1024,256]{1,0:T(8,128)}, f32[1024,256]{1,0:T(8,128)S(1)}, u32[]{:S(2)}, u32[]{:S(2)}) collective-permute-start(f32[1024,256]{1,0:T(8,128)} %get-tuple-element.28.here_hbm), channel_id=1, source_target_pairs={{0,1},{1,0},{2,3},{3,2},{4,5},{5,4},{6,7},{7,6},{8,9},{9,8},{10,11... | collective-permute-start | bytes 3145736 | tf_op jit(solution)/shard_map/ppermute | solution.py:257
  94.0 2.8 %shard_map.86 = (bf16[16,64,128]{2,1,0:T(8,128)(2,1)}, f32[17,64,128]{2,1,0:T(8,128)}) custom-call(s32[1]{0:T(128)} %bitcast.2.core_ref, s32[96]{0:T(128)} %reshape.65.map_ref, bf16[3,16,128,128]{3,2,1,0:T(8,128)(2,1)} %tiles_hbm.5), custom_call_target="tpu_custom_call" | custom-call | flops 1000000 | bytes 1600000 | tf_op jit(solution)/shard_map/pallas_call | solution.py:113
  96.9 1.9 %collective-permute-start.6 = (f32[17,64,128]{2,1,0:T(8,128)}, f32[17,64,128]{2,1,0:T(8,128)S(1)}, u32[]{:S(2)}, u32[]{:S(2)}) collective-permute-start(f32[17,64,128]{2,1,0:T(8,128)} %get-tuple-element.30), channel_id=1, source_target_pairs={{0,1},{1,0},{2,3},{3,2},{4,5},{5,4},{6,7},{7,6},{8,9},{9,8},{10,11... | collective-permute-start | bytes 1671176 | tf_op jit(solution)/shard_map/ppermute | solution.py:257
  99.1 4.7 %collective-permute-start.7 = (f32[32,256]{1,0:T(8,128)S(1)}, f32[32,256]{1,0:T(8,128)S(1)}, u32[]{:S(2)}, u32[]{:S(2)}) collective-permute-start(f32[32,256]{1,0:T(8,128)S(1)} %multiply_add_fusion.2), channel_id=1, source_target_pairs={{32,0},{64,32},{96,64},{128,96},{160,128},{192,160},{224,192},{256... | collective-permute-start | bytes 98312 | tf_op jit(solution)/shard_map/ppermute | solution.py:267
  103.8 1.0 collective-permute-done.7
  105.6 6.9 %all-to-all-start.4 = ((f32[16,32,256]{2,1,0:T(8,128)}), f32[16,32,256]{2,1,0:T(8,128)S(1)}, u32[]{:S(2)}, u32[]{:S(2)}) async-start(f32[16,32,256]{2,1,0:T(8,128)} %broadcast_in_dim.22), calls=%async_computation.4 | async-start | bytes 1048576 | tf_op jit(solution)/shard_map/all_to_all | solution.py:261
  113.5 2.7 %shard_map.85 = (f32[512,256]{1,0:T(8,128)}, f32[512,256]{1,0:T(8,128)}) custom-call(f32[512,256]{1,0:T(8,128)} %get-tuple-element.23.own_users.own_hbm, f32[512,256]{1,0:T(8,128)} %get-tuple-element.24.other_users.other_hbm, f32[1024,256]{1,0:T(8,128)} %get-tuple-element.28.here_hbm, f32[1024,256]{1,0:T(8,128)} %copy-done.3), custom_call_target="tpu_custom_call" | custom-call | flops 1000000 | bytes 4000000 | tf_op jit(solution)/shard_map/pallas_call | solution.py:250
  116.2 6.4 %all-to-all-done.4 = f32[16,32,256]{2,1,0:T(8,128)S(1)} async-done(((f32[16,32,256]{2,1,0:T(8,128)}), f32[16,32,256]{2,1,0:T(8,128)S(1)}, u32[]{:S(2)}, u32[]{:S(2)}) %all-to-all-start.4) | async-done | bytes 524320 | tf_op jit(solution)/shard_map/all_to_all | solution.py:261
  122.6 6.9 %shard_map.87 = (f32[512,256]{1,0:T(8,128)}, f32[1024,256]{1,0:T(8,128)}) custom-call(s32[32]{0:T(128)S(1)} %get-tuple-element.39.own_map, s32[32]{0:T(128)S(1)} %fusion.1.other_map, f32[512,256]{1,0:T(8,128)S(1)} %bitcast.20, f32[512,256]{1,0:T(8,128)} %get-tuple-element.29.own_users, f32[512,256]{1,0:T(8,128)} %get-tuple-element.32.other_users, ...), custom_call_target="tpu_custom_call" | custom-call | flops 2400000000 | bytes 4000000 | tf_op jit(solution)/shard_map/pallas_call | solution.py:200
  129.6 1.2 slice.31
  130.8 4.3 %collective-permute-start.8 = (f32[512,256]{1,0:T(8,128)S(1)}, f32[512,256]{1,0:T(8,128)S(1)}, u32[]{:S(2)}, u32[]{:S(2)}) collective-permute-start(f32[512,256]{1,0:T(8,128)S(1)} %slice.31), channel_id=1, source_target_pairs={{0,1},{1,0},{2,3},{3,2},{4,5},{5,4},{6,7},{7,6},{8,9},{9,8},{10,11... | collective-permute-start | bytes 1572872 | tf_op jit(solution)/shard_map/ppermute | solution.py:257
  135.0 3.6 %all-to-all-start.5 = ((f32[16,32,256]{2,1,0:T(8,128)}), f32[16,32,256]{2,1,0:T(8,128)S(1)}, u32[]{:S(2)}, u32[]{:S(2)}) async-start(f32[16,32,256]{2,1,0:T(8,128)} %bitcast.13), calls=%async_computation.5 | async-start | bytes 1048576 | tf_op jit(solution)/shard_map/all_to_all | solution.py:261
  139.6 10.4 %all-to-all-done.5 = f32[16,32,256]{2,1,0:T(8,128)S(1)} async-done(((f32[16,32,256]{2,1,0:T(8,128)}), f32[16,32,256]{2,1,0:T(8,128)S(1)}, u32[]{:S(2)}, u32[]{:S(2)}) %all-to-all-start.5) | async-done | bytes 524320 | tf_op jit(solution)/shard_map/all_to_all | solution.py:261
  (51 shorter events, 8.4 us)
Async XLA Ops:
  0.6 13.9 %copy-start.6 = (f32[512,256]{1,0:T(8,128)S(1)}, f32[512,256]{1,0:T(8,128)}, u32[]{:S(2)}) copy-start(f32[512,256]{1,0:T(8,128)} %own_hbm.1) | copy-start | bytes 1572868
  0.6 15.9 %copy-start.9 = (f32[32,256]{1,0:T(8,128)S(1)}, f32[32,256]{1,0:T(8,128)}, u32[]{:S(2)}) copy-start(f32[32,256]{1,0:T(8,128)} %param.7) | copy-start | bytes 98308
  5.7 26.9 %copy-start.2 = (bf16[16,64,128]{2,1,0:T(8,128)(2,1)S(1)}, bf16[16,64,128]{2,1,0:T(8,128)(2,1)}, u32[]{:S(2)}) copy-start(bf16[16,64,128]{2,1,0:T(8,128)(2,1)} %get-tuple-element.21.own_hbm) | copy-start | bytes 786436
  5.7 15.3 %collective-permute-start.1 = (f32[17,64,128]{2,1,0:T(8,128)}, f32[17,64,128]{2,1,0:T(8,128)S(1)}, u32[]{:S(2)}, u32[]{:S(2)}) collective-permute-start(f32[17,64,128]{2,1,0:T(8,128)} %get-tuple-element.20), channel_id=1, source_target_pairs={{0,1},{1,0},{2,3},{3,2},{4,5},{5,4},{6,7},{7,6},{8,9},{9,8},{10,11... | collective-permute-start | bytes 1671176 | tf_op jit(solution)/shard_map/ppermute | solution.py:257
  14.6 17.2 %collective-permute-start = (f32[512,256]{1,0:T(8,128)S(1)}, f32[512,256]{1,0:T(8,128)S(1)}, u32[]{:S(2)}, u32[]{:S(2)}) collective-permute-start(f32[512,256]{1,0:T(8,128)S(1)} %copy-done.6), channel_id=1, source_target_pairs={{0,1},{1,0},{2,3},{3,2},{4,5},{5,4},{6,7},{7,6},{8,9},{9,8},{10,11... | collective-permute-start | bytes 1572872 | tf_op jit(solution)/shard_map/ppermute | solution.py:257
  17.4 14.4 %all-to-all-start = ((f32[16,32,256]{2,1,0:T(8,128)}), f32[16,32,256]{2,1,0:T(8,128)S(1)}, u32[]{:S(2)}, u32[]{:S(2)}) async-start(f32[16,32,256]{2,1,0:T(8,128)} %broadcast_in_dim.20), calls=%async_computation | async-start | bytes 1048576 | tf_op jit(solution)/shard_map/all_to_all | solution.py:261
  21.0 10.8 %copy-start.12 = (f32[17,64,128]{2,1,0:T(8,128)}, f32[17,64,128]{2,1,0:T(8,128)S(1)}, u32[]{:S(2)}) copy-start(f32[17,64,128]{2,1,0:T(8,128)S(1)} %collective-permute-done.1.other_hbm) | copy-start | bytes 1671172
  31.7 0.8 copy-start.7
  39.4 13.7 %all-to-all-start.1 = ((f32[16,32,256]{2,1,0:T(8,128)}), f32[16,32,256]{2,1,0:T(8,128)S(1)}, u32[]{:S(2)}, u32[]{:S(2)}) async-start(f32[16,32,256]{2,1,0:T(8,128)} %bitcast.7), calls=%async_computation.1 | async-start | bytes 1048576 | tf_op jit(solution)/shard_map/all_to_all | solution.py:261
  43.0 26.2 %collective-permute-start.2 = (f32[1024,256]{1,0:T(8,128)}, f32[1024,256]{1,0:T(8,128)S(1)}, u32[]{:S(2)}, u32[]{:S(2)}) collective-permute-start(f32[1024,256]{1,0:T(8,128)} %get-tuple-element.22.here_hbm), channel_id=1, source_target_pairs={{0,1},{1,0},{2,3},{3,2},{4,5},{5,4},{6,7},{7,6},{8,9},{9,8},{10,11... | collective-permute-start | bytes 3145736 | tf_op jit(solution)/shard_map/ppermute | solution.py:257
  49.4 19.7 %collective-permute-start.3 = (f32[17,64,128]{2,1,0:T(8,128)}, f32[17,64,128]{2,1,0:T(8,128)S(1)}, u32[]{:S(2)}, u32[]{:S(2)}) collective-permute-start(f32[17,64,128]{2,1,0:T(8,128)} %get-tuple-element.25), channel_id=1, source_target_pairs={{0,1},{1,0},{2,3},{3,2},{4,5},{5,4},{6,7},{7,6},{8,9},{9,8},{10,11... | collective-permute-start | bytes 1671176 | tf_op jit(solution)/shard_map/ppermute | solution.py:257
  53.2 9.6 %collective-permute-start.4 = (f32[32,256]{1,0:T(8,128)S(1)}, f32[32,256]{1,0:T(8,128)S(1)}, u32[]{:S(2)}, u32[]{:S(2)}) collective-permute-start(f32[32,256]{1,0:T(8,128)S(1)} %multiply_add_fusion.3), channel_id=1, source_target_pairs={{32,0},{64,32},{96,64},{128,96},{160,128},{192,160},{224,192},{256... | collective-permute-start | bytes 98312 | tf_op jit(solution)/shard_map/ppermute | solution.py:267
  63.6 15.7 %all-to-all-start.2 = ((f32[16,32,256]{2,1,0:T(8,128)}), f32[16,32,256]{2,1,0:T(8,128)S(1)}, u32[]{:S(2)}, u32[]{:S(2)}) async-start(f32[16,32,256]{2,1,0:T(8,128)} %broadcast_in_dim.21), calls=%async_computation.2 | async-start | bytes 1048576 | tf_op jit(solution)/shard_map/all_to_all | solution.py:261
  69.2 10.1 %copy-start.11 = (f32[17,64,128]{2,1,0:T(8,128)}, f32[17,64,128]{2,1,0:T(8,128)S(1)}, u32[]{:S(2)}) copy-start(f32[17,64,128]{2,1,0:T(8,128)S(1)} %collective-permute-done.3.other_hbm) | copy-start | bytes 1671172
  69.2 10.1 %copy-start.1 = (bf16[16,64,128]{2,1,0:T(8,128)(2,1)S(1)}, bf16[16,64,128]{2,1,0:T(8,128)(2,1)}, u32[]{:S(2)}) copy-start(bf16[16,64,128]{2,1,0:T(8,128)(2,1)} %get-tuple-element.27.own_hbm) | copy-start | bytes 786436
  69.2 1.0 copy-start.4
  86.2 12.9 %all-to-all-start.3 = ((f32[16,32,256]{2,1,0:T(8,128)}), f32[16,32,256]{2,1,0:T(8,128)S(1)}, u32[]{:S(2)}, u32[]{:S(2)}) async-start(f32[16,32,256]{2,1,0:T(8,128)} %bitcast.11), calls=%async_computation.3 | async-start | bytes 1048576 | tf_op jit(solution)/shard_map/all_to_all | solution.py:261
  89.7 22.8 %collective-permute-start.5 = (f32[1024,256]{1,0:T(8,128)}, f32[1024,256]{1,0:T(8,128)S(1)}, u32[]{:S(2)}, u32[]{:S(2)}) collective-permute-start(f32[1024,256]{1,0:T(8,128)} %get-tuple-element.28.here_hbm), channel_id=1, source_target_pairs={{0,1},{1,0},{2,3},{3,2},{4,5},{5,4},{6,7},{7,6},{8,9},{9,8},{10,11... | collective-permute-start | bytes 3145736 | tf_op jit(solution)/shard_map/ppermute | solution.py:257
  96.9 15.6 %collective-permute-start.6 = (f32[17,64,128]{2,1,0:T(8,128)}, f32[17,64,128]{2,1,0:T(8,128)S(1)}, u32[]{:S(2)}, u32[]{:S(2)}) collective-permute-start(f32[17,64,128]{2,1,0:T(8,128)} %get-tuple-element.30), channel_id=1, source_target_pairs={{0,1},{1,0},{2,3},{3,2},{4,5},{5,4},{6,7},{7,6},{8,9},{9,8},{10,11... | collective-permute-start | bytes 1671176 | tf_op jit(solution)/shard_map/ppermute | solution.py:257
  99.1 5.7 %collective-permute-start.7 = (f32[32,256]{1,0:T(8,128)S(1)}, f32[32,256]{1,0:T(8,128)S(1)}, u32[]{:S(2)}, u32[]{:S(2)}) collective-permute-start(f32[32,256]{1,0:T(8,128)S(1)} %multiply_add_fusion.2), channel_id=1, source_target_pairs={{32,0},{64,32},{96,64},{128,96},{160,128},{192,160},{224,192},{256... | collective-permute-start | bytes 98312 | tf_op jit(solution)/shard_map/ppermute | solution.py:267
  105.6 17.0 %all-to-all-start.4 = ((f32[16,32,256]{2,1,0:T(8,128)}), f32[16,32,256]{2,1,0:T(8,128)S(1)}, u32[]{:S(2)}, u32[]{:S(2)}) async-start(f32[16,32,256]{2,1,0:T(8,128)} %broadcast_in_dim.22), calls=%async_computation.4 | async-start | bytes 1048576 | tf_op jit(solution)/shard_map/all_to_all | solution.py:261
  112.5 10.1 %copy-start.10 = (f32[17,64,128]{2,1,0:T(8,128)}, f32[17,64,128]{2,1,0:T(8,128)S(1)}, u32[]{:S(2)}) copy-start(f32[17,64,128]{2,1,0:T(8,128)S(1)} %collective-permute-done.6.other_hbm) | copy-start | bytes 1671172
  112.5 10.1 %copy-start = (bf16[16,64,128]{2,1,0:T(8,128)(2,1)S(1)}, bf16[16,64,128]{2,1,0:T(8,128)(2,1)}, u32[]{:S(2)}) copy-start(bf16[16,64,128]{2,1,0:T(8,128)(2,1)} %get-tuple-element.33.own_hbm) | copy-start | bytes 786436
  112.5 1.0 copy-start.3
  129.6 9.1 %copy-start.5 = (f32[1024,256]{1,0:T(8,128)S(1)}, f32[1024,256]{1,0:T(8,128)}, u32[]{:S(2)}) copy-start(f32[1024,256]{1,0:T(8,128)} %get-tuple-element.34) | copy-start | bytes 3145732
  129.6 9.1 %copy-start.8 = (f32[512,256]{1,0:T(8,128)S(1)}, f32[512,256]{1,0:T(8,128)}, u32[]{:S(2)}) copy-start(f32[512,256]{1,0:T(8,128)} %get-tuple-element.29.own_users) | copy-start | bytes 1572868
  130.8 7.9 %collective-permute-start.8 = (f32[512,256]{1,0:T(8,128)S(1)}, f32[512,256]{1,0:T(8,128)S(1)}, u32[]{:S(2)}, u32[]{:S(2)}) collective-permute-start(f32[512,256]{1,0:T(8,128)S(1)} %slice.31), channel_id=1, source_target_pairs={{0,1},{1,0},{2,3},{3,2},{4,5},{5,4},{6,7},{7,6},{8,9},{9,8},{10,11... | collective-permute-start | bytes 1572872 | tf_op jit(solution)/shard_map/ppermute | solution.py:257
  135.0 14.9 %all-to-all-start.5 = ((f32[16,32,256]{2,1,0:T(8,128)}), f32[16,32,256]{2,1,0:T(8,128)S(1)}, u32[]{:S(2)}, u32[]{:S(2)}) async-start(f32[16,32,256]{2,1,0:T(8,128)} %bitcast.13), calls=%async_computation.5 | async-start | bytes 1048576 | tf_op jit(solution)/shard_map/all_to_all | solution.py:261

commit v3 on v2

--- a/solution.py
+++ b/solution.py
@@ -47,7 +47,7 @@
 SMEM = pl.BlockSpec(memory_space=pltpu.SMEM)
 WIDTH = 2 * TILE
 BLOCKS = 2 * U_DEV // WIDTH
-STEP_GRANT = 53800
+STEP_GRANT = 54000
 UPDATE_GRANT = 60 * 1024
 
 
@@ -67,7 +67,8 @@
     )
 
 
-def turn_kernel(tick, core_ref, map_ref, tiles_hbm, kept_hbm, sent_hbm, tiles, kept, sent, turned, sems):
+def turn_kernel(tick, core_ref, rows_ref, cols_ref, count_ref, tiles_hbm, kept_hbm, sent_hbm,
+                tiles, kept, sent, turned, sems):
     core = core_ref[0]
     group = K_MAX // 4
 
@@ -83,9 +84,10 @@
     for g in range(4):
         fetch(g).start()
     lane = lax.broadcasted_iota(jnp.int32, (8, TILE), 1)
-    row = jnp.zeros((8, TILE), jnp.int32)
-    for cell in range(CELLS):
-        row = jnp.where(lane == cell, map_ref[tick * CELLS + cell], row)
+    row = jnp.full((8, TILE), -1, jnp.int32)
+    for k in range(K_MAX):
+        cell = rows_ref[tick, k] * I_TILES + cols_ref[tick, k]
+        row = jnp.where((lane == cell) & (k < count_ref[tick, 0]), k, row)
     sent[K_MAX, pl.ds(0, 8), :] = row.astype(f32)
     sent[K_MAX, pl.ds(8, HALF - 8), :] = jnp.zeros((HALF - 8, TILE), f32)
     last = pltpu.make_async_copy(sent.at[pl.ds(K_MAX, 1)], sent_hbm.at[pl.ds(K_MAX, 1)], sems.at[12])
@@ -98,7 +100,7 @@
                 rows = pl.ds(part * SHARE, SHARE)
                 mine = pl.multiple_of(part * HALF + core * SHARE, SHARE)
                 theirs = pl.multiple_of(part * HALF + (1 - core) * SHARE, SHARE)
-                kept[k, rows, :] = turned[k, pl.ds(mine, SHARE), :]
+                kept[k, rows, :] = turned[k, pl.ds(mine, SHARE), :].astype(f32)
                 sent[k, rows, :] = turned[k, pl.ds(theirs, SHARE), :].astype(f32)
         put(g, 0).start()
         put(g, 1).start()
@@ -108,20 +110,21 @@
     last.wait()
 
 
-def turned_tiles(tick, core, slot_map, ratings):
+def turned_tiles(tick, core, rows, cols, count, ratings):
     tile = pltpu.VMEM((K_MAX, TILE, TILE), bf16)
     return call(
         functools.partial(turn_kernel, tick),
-        (shape((K_MAX, HALF, TILE), bf16), shape((K_MAX + 1, HALF, TILE), f32)),
-        [SMEM, SMEM, ANY], (ANY, ANY),
-        [tile, pltpu.VMEM((K_MAX, HALF, TILE), bf16), pltpu.VMEM((K_MAX + 1, HALF, TILE), f32), tile,
+        (shape((K_MAX, HALF, TILE), f32), shape((K_MAX + 1, HALF, TILE), f32)),
+        [SMEM] * 4 + [ANY], (ANY, ANY),
+        [tile, pltpu.VMEM((K_MAX, HALF, TILE), f32), pltpu.VMEM((K_MAX + 1, HALF, TILE), f32), tile,
          pltpu.SemaphoreType.DMA((13,))],
         1000000, 1600000,
-    )(core, slot_map, ratings)
-
-
-def step_kernel(own_map, other_map, panel_hbm, own_users, other_users, own_hbm, other_hbm, item_hbm, user_hbm,
-                panel_ref, users, own_tiles, other_tiles, predicted, item_grad, user_grad, sems):
+    )(core, rows, cols, count, ratings)
+
+
+def step_kernel(tick, last, rows_ref, cols_ref, count_ref, other_map, panel_hbm, own_users, other_users, own_hbm, other_hbm, *refs):
+    item_hbm, *user_hbm = refs[:3] if last else refs[:2]
+    panel_ref, users, own_tiles, other_tiles, predicted, item_grad, user_grad, own_map, sems = refs[-9:]
     half = BLOCKS // 2
     parts = ITEMS_CORE // TILE
 
@@ -137,75 +140,105 @@
             sems.at[3 + block])
         for block in range(BLOCKS)
     ]
-    for copy in [panel_load, user_loads[0], own_load, *user_loads[1:], other_load]:
-        copy.start()
 
     def send_items(part):
         cut = pl.ds(part * TILE, TILE)
         return pltpu.make_async_copy(item_grad.at[cut], item_hbm.at[cut], sems.at[3 + BLOCKS + part])
 
     def send_users(block):
-        return pltpu.make_async_copy(
-            user_grad.at[rows(block)], user_hbm.at[rows(block)], sems.at[3 + BLOCKS + parts + block])
-
-    panel_load.wait()
-    panel = halves(panel_ref[...])
+        into = user_hbm[block // half].at[rows(block % half)] if last else user_hbm[0].at[rows(block)]
+        return pltpu.make_async_copy(user_grad.at[rows(block)], into, sems.at[3 + BLOCKS + parts + block])
+
+    for copy in [panel_load, *user_loads[:2], own_load, *user_loads[2:], other_load]:
+        copy.start()
+    for cell in range(CELLS):
+        own_map[cell] = -1
+    for k in range(K_MAX):
+        cell = rows_ref[tick, k] * I_TILES + cols_ref[tick, k]
+        own_map[cell] = jnp.where(k < count_ref[tick, 0], k, own_map[cell])
+
+    def split(block):
+        return halves(users[rows(block), :])
 
     def predict(block):
-        user_loads[block].wait()
-        split = halves(users[rows(block), :])
-        predicted[block] = dot3(panel, split, ((1,), (1,)))
-        return split
-
-    split = predict(0)
-    for block in range(BLOCKS):
-        after = predict(block + 1) if block + 1 < BLOCKS else None
-        slot_map, tiles = (own_map, own_tiles) if block < half else (other_map, other_tiles)
-        if block % half == 0:
-            (own_load if block < half else other_load).wait()
+        predicted[block] = dot3(panel, split(block), ((1,), (1,)))
+
+    def errors(block):
+        tiles = own_tiles if block < half else other_tiles
         tops, lows = [], []
         for item in range(I_TILES):
             cut = pl.ds(item * HALF, HALF)
-            errors = []
+            cells = []
             for part in range(2):
-                slot = slot_map[(block * 2 + part) % U_TILES * I_TILES + item]
-                error = tiles[jnp.maximum(slot, 0)].astype(f32) - predicted[block, cut, pl.ds(part * TILE, TILE)]
-                errors.append(jnp.where(slot >= 0, error, 0.0))
-            top, low = halves(jnp.concatenate(errors, axis=1))
+                place = (block * 2 + part) % U_TILES * I_TILES + item
+                slot = (own_map if block < half else other_map)[place]
+                cell = tiles[jnp.maximum(slot, 0)] - predicted[block, cut, pl.ds(part * TILE, TILE)]
+                cells.append(jnp.where(slot >= 0, cell, 0.0))
+            top, low = halves(jnp.concatenate(cells, axis=1))
             tops.append(top)
             lows.append(low)
-        error = jnp.concatenate(tops, axis=0), jnp.concatenate(lows, axis=0)
+        return jnp.concatenate(tops, axis=0), jnp.concatenate(lows, axis=0)
+
+    def user_part(block, error):
         user_grad[rows(block), :] = dot3(error, panel, ((0,), (0,)))
-        send_users(block).start()
+
+    def item_part(block, error):
+        grad = dot3(error, split(block), ((1,), (0,)))
         if block == 0:
-            item_grad[...] = dot3(error, split, ((1,), (0,)))
-        elif block + 1 < BLOCKS:
-            item_grad[...] += dot3(error, split, ((1,), (0,)))
+            item_grad[...] = grad
         else:
-            for part in range(parts):
-                cut = slice(part * TILE, (part + 1) * TILE)
-                item_grad[cut, :] += dot3((error[0][cut], error[1][cut]), split, ((1,), (0,)))
-                send_items(part).start()
-        split = after
+            item_grad[...] += grad
+
+    panel_load.wait()
+    user_loads[0].wait()
+    user_loads[1].wait()
+    panel = halves(panel_ref[...])
+    predict(0)
+    predict(1)
+    own_load.wait()
+    user_loads[2].wait()
+    user_loads[3].wait()
+    other_load.wait()
+    error = errors(0)
+    predict(2)
+    item_part(0, error)
+    user_part(0, error)
+    error = errors(1)
+    predict(3)
+    item_part(1, error)
+    user_part(1, error)
+    send_users(0).start()
+    send_users(1).start()
+    error = errors(2)
+    later = errors(3)
+    user_part(2, error)
+    item_part(2, error)
+    item_part(3, later)
+    for part in range(parts):
+        send_items(part).start()
+    send_users(2).start()
+    user_part(3, later)
+    send_users(3).start()
     for block in range(BLOCKS):
         send_users(block).wait()
     for part in range(parts):
         send_items(part).wait()
 
 
-def item_and_user_grads(own_map, other_map, panel, own, other, own_tiles, other_tiles):
+def item_and_user_grads(tick, last, rows, cols, count, other_map, panel, own, other, own_tiles, other_tiles):
     half_panel = pltpu.VMEM((ITEMS_CORE, R), f32)
     both = pltpu.VMEM((2 * U_DEV, R), f32)
     cut = (K_MAX, HALF, TILE)
+    users = [shape((U_DEV, R), f32)] * 2 if last else [shape((2 * U_DEV, R), f32)]
     return call(
-        step_kernel,
-        (shape((ITEMS_CORE, R), f32), shape((2 * U_DEV, R), f32)),
-        [SMEM] * 2 + [ANY] * 5, (ANY,) * 2,
-        [half_panel, both, pltpu.VMEM(cut, bf16), pltpu.VMEM(cut, f32),
-         pltpu.VMEM((BLOCKS, ITEMS_CORE, WIDTH), f32), half_panel, both,
+        functools.partial(step_kernel, tick, last),
+        (shape((ITEMS_CORE, R), f32), *users),
+        [SMEM] * 4 + [ANY] * 5, (ANY,) * (1 + len(users)),
+        [half_panel, both, pltpu.VMEM(cut, f32), pltpu.VMEM(cut, f32),
+         pltpu.VMEM((BLOCKS, ITEMS_CORE, WIDTH), f32), half_panel, both, pltpu.SMEM((CELLS,), jnp.int32),
          pltpu.SemaphoreType.DMA((3 + 2 * BLOCKS + ITEMS_CORE // TILE,))],
         2400000000, 4000000, STEP_GRANT,
-    )(own_map, other_map, panel, own, other, own_tiles, other_tiles)
+    )(rows, cols, count, other_map, panel, own, other, own_tiles, other_tiles)
 
 
 def stepped(user, here, there):
@@ -267,34 +300,30 @@
     return lax.ppermute(block, axis, route)
 
 
-def slot_maps(tile_users, tile_items, tile_count):
-    slots = jnp.arange(K_MAX)[None, :, None]
-    cell = (tile_users * I_TILES + tile_items)[:, :, None]
-    live = (slots < tile_count[:, :, None]) & (cell == jnp.arange(CELLS)[None, None, :])
-    return jnp.max(jnp.where(live, slots, -1), axis=1).astype(jnp.int32)
-
-
 def shards(user_factors, item_factors, ratings, tile_users, tile_items, tile_count):
     core = lax.rem(lax.axis_index("owner"), 2).reshape(1)
     own, share = user_factors, item_factors
     other = swapped(own)
-    own_map = slot_maps(tile_users, tile_items, tile_count)
     for tick in range(TICKS):
-        kept, sent = turned_tiles(tick, core, own_map.reshape(-1), ratings)
+        kept, sent = turned_tiles(tick, core, tile_users, tile_items, tile_count, ratings)
         got = swapped(sent)
+        if tick == 0:
+            got, other = lax.optimization_barrier((got, other))
         other_map = got[K_MAX, 0, :CELLS].astype(jnp.int32)
         panel = exchanged(jnp.broadcast_to(share[None], (CHIPS, SHARE, R))).reshape(ITEMS_CORE, R)
-        item_grad, here = item_and_user_grads(own_map[tick], other_map, panel, own, other, kept, got)
+        item_grad, *here = item_and_user_grads(
+            tick, tick + 1 == TICKS, tile_users, tile_items, tile_count, other_map, panel, own, other, kept, got)
         parts = exchanged(item_grad.reshape(CHIPS, SHARE, R))
         if tick + 1 < TICKS:
-            there = swapped(here)
-            own, other = updated_users(own, other, here, there)
+            there = swapped(here[0])
         else:
-            there = swapped(here[U_DEV:])
-            own, parts = lax.optimization_barrier((stepped(own, here[:U_DEV], there), parts))
+            there = swapped(here[1])
+            own, parts = lax.optimization_barrier((stepped(own, here[0], there), parts))
         share = share * (1.0 - item_rate * shrink_rate) + item_rate * parts.sum(axis=0)
         if tick + 1 < TICKS:
+            share, there = lax.optimization_barrier((share, there))
             share = passed_along(share, "band", -1)
+            own, other = updated_users(own, other, here[0], there)
     return own, share
 
 

time: 152 us -> 153 us (level)
  waiting for transfers between devices: 38 us -> 49.1 us
  starting transfers between devices: 66.7 us -> 63.1 us
  Pallas kernels: 34.6 us -> 32.2 us
  local copies, waits for them, and re-layouts: 7.07 us -> 4.82 us
  other arithmetic: 3.24 us -> 1.66 us
    all_to_all x6, waiting for transfers between devices: 35.9 us -> 47.1 us  [exchanged(): lax.all_to_all(blocks, 'owner', split_axis=0, concat_axis=0, axis_index_g...]
    all_to_all x6, starting transfers between devices: 26.7 us -> 21.6 us  [exchanged(): lax.all_to_all(blocks, 'owner', split_axis=0, concat_axis=0, axis_index_g...]
    pallas_call x6, Pallas kernels: 29.2 us -> 26.4 us  [the longest x3 17.4 us: item_and_user_grads(): call(functools.partial(step_kernel, tick, last), (shape((ITEMS_CORE, R),...]
  transfers between devices with their start and end apart: 15 -> 15, of which waited for: 8 -> 8; matrix products, arithmetic and copies ran while one was open for 2% -> 2% of each run, Pallas kernels for 7% -> 8%
where the time goes in v3:
time: 153 us; the launch traced here: 152 us
  starting transfers between devices  63.1 us (41%)
  waiting for transfers between devices  49.1 us (32%)
  Pallas kernels  32.2 us (21%)
  local copies, waits for them, and re-layouts  4.82 us (3%)
  other arithmetic  1.66 us (1%)
    all_to_all x6, waiting for transfers between devices, exchanged(): lax.all_to_all(blocks, 'owner', split_axis=0, concat_axis=0, axis_index_g...  47.1 us
    ppermute x7, starting transfers between devices, swapped(): return lax.ppermute(x, 'owner', PARTNERS)  27.6 us
    all_to_all x6, starting transfers between devices, exchanged(): lax.all_to_all(blocks, 'owner', split_axis=0, concat_axis=0, axis_index_g...  21.6 us
    pallas_call x3, Pallas kernels, item_and_user_grads(): call(functools.partial(step_kernel, tick, last), (shape((ITEMS_CORE, R),...  17.4 us
    ppermute x2, starting transfers between devices, passed_along(): return lax.ppermute(block, axis, route)  13.9 us
    pallas_call x3, Pallas kernels, turned_tiles(): call(functools.partial(turn_kernel, tick), (shape((K_MAX, HALF, TILE), f3...  8.96 us
    pallas_call x2, Pallas kernels, updated_users(): call(update_kernel, (new, new), [ANY] * 4, (ANY, ANY), [both, both, both,...  5.79 us
  transfers between devices with their start and end apart: 15, of which 8 were waited for; matrix products, arithmetic and copies ran while one was open for 2% of the time, Pallas kernels for 8%

profile of v3, /device:TPU:1, one launch (start us, length us, event | category | flops | bytes accessed | tf_op | source)
XLA Modules:
  0.0 151.9 jit_solution(16469579830578563748)
XLA Ops:
  0.7 1.4 copy.8.count_ref
  2.0 3.1 %shard_map.77 = (f32[16,64,128]{2,1,0:T(8,128)}, f32[17,64,128]{2,1,0:T(8,128)}) custom-call(s32[1]{0:T(128)} %bitcast.core_ref, s32[3,16]{1,0:T(4,128)} %rows_ref.11, s32[3,16]{1,0:T(4,128)} %cols_ref.11, s32[3,1]{1,0:T(4,128)} %copy.8.count_ref, bf16[3,16,128,128]{3,2,1,0:T(8,128)(2,1)} %tiles_hbm.5), custom_call_target="tpu_custom_call" | custom-call | flops 1000000 | bytes 1600000 | tf_op jit(solution)/shard_map/pallas_call | solution.py:115
  5.1 8.7 %collective-permute-start = (f32[17,64,128]{2,1,0:T(8,128)}, f32[17,64,128]{2,1,0:T(8,128)S(1)}, u32[]{:S(2)}, u32[]{:S(2)}) collective-permute-start(f32[17,64,128]{2,1,0:T(8,128)} %get-tuple-element.27), channel_id=1, source_target_pairs={{0,1},{1,0},{2,3},{3,2},{4,5},{5,4},{6,7},{7,6},{8,9},{9,8},{10,11... | collective-permute-start | bytes 1671176 | tf_op jit(solution)/shard_map/ppermute | solution.py:290
  13.9 1.9 %collective-permute-start.1 = (f32[512,256]{1,0:T(8,128)S(1)}, f32[512,256]{1,0:T(8,128)S(1)}, u32[]{:S(2)}, u32[]{:S(2)}) collective-permute-start(f32[512,256]{1,0:T(8,128)S(1)} %copy-done.12), channel_id=1, source_target_pairs={{0,1},{1,0},{2,3},{3,2},{4,5},{5,4},{6,7},{7,6},{8,9},{9,8},{10,11... | collective-permute-start | bytes 1572872 | tf_op jit(solution)/shard_map/ppermute | solution.py:290
  16.7 3.6 %all-to-all-start = ((f32[16,32,256]{2,1,0:T(8,128)}), f32[16,32,256]{2,1,0:T(8,128)S(1)}, u32[]{:S(2)}, u32[]{:S(2)}) async-start(f32[16,32,256]{2,1,0:T(8,128)} %broadcast_in_dim.6), calls=%async_computation | async-start | bytes 1048576 | tf_op jit(solution)/shard_map/all_to_all | solution.py:294
  20.3 10.8 %all-to-all-done = f32[16,32,256]{2,1,0:T(8,128)S(1)} async-done(((f32[16,32,256]{2,1,0:T(8,128)}), f32[16,32,256]{2,1,0:T(8,128)S(1)}, u32[]{:S(2)}, u32[]{:S(2)}) %all-to-all-start) | async-done | bytes 524320 | tf_op jit(solution)/shard_map/all_to_all | solution.py:294
  31.1 5.7 %shard_map.78 = (f32[512,256]{1,0:T(8,128)}, f32[1024,256]{1,0:T(8,128)}) custom-call(s32[3,16]{1,0:T(4,128)S(1)} %copy-done.3, s32[3,16]{1,0:T(4,128)S(1)} %copy-done.6, s32[3,1]{1,0:T(4,128)S(1)} %copy-done, s32[32]{0:T(128)S(1)} %convert_bitcast_fusion.other_map, f32[512,256]{1,0:T(8,128)S(1)} %bitcast.14, f32[512,256]{1,0:T(8,128)} %own_hbm.1, ...), custom_call_target="tpu_custom_call" | custom-call | flops 2400000000 | bytes 4000000 | tf_op jit(solution)/shard_map/pallas_call | solution.py:233
  36.7 3.6 %collective-permute-start.2 = (f32[1024,256]{1,0:T(8,128)}, f32[1024,256]{1,0:T(8,128)S(1)}, u32[]{:S(2)}, u32[]{:S(2)}) collective-permute-start(f32[1024,256]{1,0:T(8,128)} %get-tuple-element.31.here_hbm), channel_id=1, source_target_pairs={{0,1},{1,0},{2,3},{3,2},{4,5},{5,4},{6,7},{7,6},{8,9},{9,8},{10,11... | collective-permute-start | bytes 3145736 | tf_op jit(solution)/shard_map/ppermute | solution.py:290
  40.3 3.6 %all-to-all-start.1 = ((f32[16,32,256]{2,1,0:T(8,128)}), f32[16,32,256]{2,1,0:T(8,128)S(1)}, u32[]{:S(2)}, u32[]{:S(2)}) async-start(f32[16,32,256]{2,1,0:T(8,128)} %bitcast.3), calls=%async_computation.1 | async-start | bytes 1048576 | tf_op jit(solution)/shard_map/all_to_all | solution.py:294
  43.9 2.9 %shard_map.80 = (f32[16,64,128]{2,1,0:T(8,128)}, f32[17,64,128]{2,1,0:T(8,128)}) custom-call(s32[1]{0:T(128)} %bitcast.core_ref, s32[3,16]{1,0:T(4,128)} %rows_ref.11, s32[3,16]{1,0:T(4,128)} %cols_ref.11, s32[3,1]{1,0:T(4,128)} %copy.8.count_ref, bf16[3,16,128,128]{3,2,1,0:T(8,128)(2,1)} %tiles_hbm.5), custom_call_target="tpu_custom_call" | custom-call | flops 1000000 | bytes 1600000 | tf_op jit(solution)/shard_map/pallas_call | solution.py:115
  46.9 1.9 %collective-permute-start.3 = (f32[17,64,128]{2,1,0:T(8,128)}, f32[17,64,128]{2,1,0:T(8,128)S(1)}, u32[]{:S(2)}, u32[]{:S(2)}) collective-permute-start(f32[17,64,128]{2,1,0:T(8,128)} %get-tuple-element.36), channel_id=1, source_target_pairs={{0,1},{1,0},{2,3},{3,2},{4,5},{5,4},{6,7},{7,6},{8,9},{9,8},{10,11... | collective-permute-start | bytes 1671176 | tf_op jit(solution)/shard_map/ppermute | solution.py:290
  48.8 6.4 %all-to-all-done.1 = f32[16,32,256]{2,1,0:T(8,128)S(1)} async-done(((f32[16,32,256]{2,1,0:T(8,128)}), f32[16,32,256]{2,1,0:T(8,128)S(1)}, u32[]{:S(2)}, u32[]{:S(2)}) %all-to-all-start.1) | async-done | bytes 524320 | tf_op jit(solution)/shard_map/all_to_all | solution.py:294
  55.3 9.0 %collective-permute-start.4 = (f32[32,256]{1,0:T(8,128)S(1)}, f32[32,256]{1,0:T(8,128)S(1)}, u32[]{:S(2)}, u32[]{:S(2)}) collective-permute-start(f32[32,256]{1,0:T(8,128)S(1)} %multiply_add_fusion.3), channel_id=1, source_target_pairs={{32,0},{64,32},{96,64},{128,96},{160,128},{192,160},{224,192},{256... | collective-permute-start | bytes 98312 | tf_op jit(solution)/shard_map/ppermute | solution.py:300
  64.3 1.0 collective-permute-done.4
  66.1 3.6 %all-to-all-start.2 = ((f32[16,32,256]{2,1,0:T(8,128)}), f32[16,32,256]{2,1,0:T(8,128)S(1)}, u32[]{:S(2)}, u32[]{:S(2)}) async-start(f32[16,32,256]{2,1,0:T(8,128)} %broadcast_in_dim.7), calls=%async_computation.2 | async-start | bytes 1048576 | tf_op jit(solution)/shard_map/all_to_all | solution.py:294
  69.8 2.9 %shard_map.79 = (f32[512,256]{1,0:T(8,128)}, f32[512,256]{1,0:T(8,128)}) custom-call(f32[512,256]{1,0:T(8,128)} %own_hbm.1, f32[512,256]{1,0:T(8,128)} %copy-done.13, f32[1024,256]{1,0:T(8,128)} %get-tuple-element.31.here_hbm, f32[1024,256]{1,0:T(8,128)} %copy-done.10), custom_call_target="tpu_custom_call" | custom-call | flops 1000000 | bytes 4000000 | tf_op jit(solution)/shard_map/pallas_call | solution.py:283
  72.7 6.7 %all-to-all-done.2 = f32[16,32,256]{2,1,0:T(8,128)S(1)} async-done(((f32[16,32,256]{2,1,0:T(8,128)}), f32[16,32,256]{2,1,0:T(8,128)S(1)}, u32[]{:S(2)}, u32[]{:S(2)}) %all-to-all-start.2) | async-done | bytes 524320 | tf_op jit(solution)/shard_map/all_to_all | solution.py:294
  79.4 5.7 %shard_map.81 = (f32[512,256]{1,0:T(8,128)}, f32[1024,256]{1,0:T(8,128)}) custom-call(s32[3,16]{1,0:T(4,128)S(1)} %copy-done.4, s32[3,16]{1,0:T(4,128)S(1)} %copy-done.7, s32[3,1]{1,0:T(4,128)S(1)} %copy-done.1, s32[32]{0:T(128)S(1)} %fusion.1.other_map, f32[512,256]{1,0:T(8,128)S(1)} %bitcast.13, f32[512,256]{1,0:T(8,128)} %get-tuple-element.34.own_users.own_hbm, ...), custom_call_target="tpu_custom_call" | custom-call | flops 2400000000 | bytes 4000000 | tf_op jit(solution)/shard_map/pallas_call | solution.py:233
  85.1 4.7 %collective-permute-start.5 = (f32[1024,256]{1,0:T(8,128)}, f32[1024,256]{1,0:T(8,128)S(1)}, u32[]{:S(2)}, u32[]{:S(2)}) collective-permute-start(f32[1024,256]{1,0:T(8,128)} %get-tuple-element.39.here_hbm), channel_id=1, source_target_pairs={{0,1},{1,0},{2,3},{3,2},{4,5},{5,4},{6,7},{7,6},{8,9},{9,8},{10,11... | collective-permute-start | bytes 3145736 | tf_op jit(solution)/shard_map/ppermute | solution.py:290
  89.8 3.6 %all-to-all-start.3 = ((f32[16,32,256]{2,1,0:T(8,128)}), f32[16,32,256]{2,1,0:T(8,128)S(1)}, u32[]{:S(2)}, u32[]{:S(2)}) async-start(f32[16,32,256]{2,1,0:T(8,128)} %bitcast.6), calls=%async_computation.3 | async-start | bytes 1048576 | tf_op jit(solution)/shard_map/all_to_all | solution.py:294
  93.4 2.9 %shard_map.83 = (f32[16,64,128]{2,1,0:T(8,128)}, f32[17,64,128]{2,1,0:T(8,128)}) custom-call(s32[1]{0:T(128)} %bitcast.core_ref, s32[3,16]{1,0:T(4,128)} %rows_ref.11, s32[3,16]{1,0:T(4,128)} %cols_ref.11, s32[3,1]{1,0:T(4,128)} %copy.8.count_ref, bf16[3,16,128,128]{3,2,1,0:T(8,128)(2,1)} %tiles_hbm.5), custom_call_target="tpu_custom_call" | custom-call | flops 1000000 | bytes 1600000 | tf_op jit(solution)/shard_map/pallas_call | solution.py:115
  96.4 1.9 %collective-permute-start.6 = (f32[17,64,128]{2,1,0:T(8,128)}, f32[17,64,128]{2,1,0:T(8,128)S(1)}, u32[]{:S(2)}, u32[]{:S(2)}) collective-permute-start(f32[17,64,128]{2,1,0:T(8,128)} %get-tuple-element.43), channel_id=1, source_target_pairs={{0,1},{1,0},{2,3},{3,2},{4,5},{5,4},{6,7},{7,6},{8,9},{9,8},{10,11... | collective-permute-start | bytes 1671176 | tf_op jit(solution)/shard_map/ppermute | solution.py:290
  98.3 6.4 %all-to-all-done.3 = f32[16,32,256]{2,1,0:T(8,128)S(1)} async-done(((f32[16,32,256]{2,1,0:T(8,128)}), f32[16,32,256]{2,1,0:T(8,128)S(1)}, u32[]{:S(2)}, u32[]{:S(2)}) %all-to-all-start.3) | async-done | bytes 524320 | tf_op jit(solution)/shard_map/all_to_all | solution.py:294
  104.8 4.9 %collective-permute-start.7 = (f32[32,256]{1,0:T(8,128)S(1)}, f32[32,256]{1,0:T(8,128)S(1)}, u32[]{:S(2)}, u32[]{:S(2)}) collective-permute-start(f32[32,256]{1,0:T(8,128)S(1)} %multiply_add_fusion.2), channel_id=1, source_target_pairs={{32,0},{64,32},{96,64},{128,96},{160,128},{192,160},{224,192},{256... | collective-permute-start | bytes 98312 | tf_op jit(solution)/shard_map/ppermute | solution.py:300
  109.7 1.0 collective-permute-done.7
  111.5 3.8 %all-to-all-start.4 = ((f32[16,32,256]{2,1,0:T(8,128)}), f32[16,32,256]{2,1,0:T(8,128)S(1)}, u32[]{:S(2)}, u32[]{:S(2)}) async-start(f32[16,32,256]{2,1,0:T(8,128)} %broadcast_in_dim.8), calls=%async_computation.4 | async-start | bytes 1048576 | tf_op jit(solution)/shard_map/all_to_all | solution.py:294
  115.4 2.9 %shard_map.82 = (f32[512,256]{1,0:T(8,128)}, f32[512,256]{1,0:T(8,128)}) custom-call(f32[512,256]{1,0:T(8,128)} %get-tuple-element.34.own_users.own_hbm, f32[512,256]{1,0:T(8,128)} %get-tuple-element.35.other_users.other_hbm, f32[1024,256]{1,0:T(8,128)} %get-tuple-element.39.here_hbm, f32[1024,256]{1,0:T(8,128)} %copy-done.9), custom_call_target="tpu_custom_call" | custom-call | flops 1000000 | bytes 4000000 | tf_op jit(solution)/shard_map/pallas_call | solution.py:283
  118.3 6.5 %all-to-all-done.4 = f32[16,32,256]{2,1,0:T(8,128)S(1)} async-done(((f32[16,32,256]{2,1,0:T(8,128)}), f32[16,32,256]{2,1,0:T(8,128)S(1)}, u32[]{:S(2)}, u32[]{:S(2)}) %all-to-all-start.4) | async-done | bytes 524320 | tf_op jit(solution)/shard_map/all_to_all | solution.py:294
  125.6 6.0 %shard_map.84 = (f32[512,256]{1,0:T(8,128)}, f32[512,256]{1,0:T(8,128)S(1)}, f32[512,256]{1,0:T(8,128)}) custom-call(s32[3,16]{1,0:T(4,128)S(1)} %copy-done.5, s32[3,16]{1,0:T(4,128)S(1)} %copy-done.8, s32[3,1]{1,0:T(4,128)S(1)} %copy-done.2, s32[32]{0:T(128)S(1)} %fusion.other_map, f32[512,256]{1,0:T(8,128)} %bitcast.15, ...), custom_call_target="tpu_custom_call" | custom-call | flops 2400000000 | bytes 4000000 | tf_op jit(solution)/shard_map/pallas_call | solution.py:233
  131.6 4.8 %collective-permute-start.8 = (f32[512,256]{1,0:T(8,128)}, f32[512,256]{1,0:T(8,128)S(1)}, u32[]{:S(2)}, u32[]{:S(2)}) collective-permute-start(f32[512,256]{1,0:T(8,128)} %get-tuple-element.48), channel_id=1, source_target_pairs={{0,1},{1,0},{2,3},{3,2},{4,5},{5,4},{6,7},{7,6},{8,9},{9,8},{10,11... | collective-permute-start | bytes 1572872 | tf_op jit(solution)/shard_map/ppermute | solution.py:290
  136.4 3.6 %all-to-all-start.5 = ((f32[16,32,256]{2,1,0:T(8,128)}), f32[16,32,256]{2,1,0:T(8,128)S(1)}, u32[]{:S(2)}, u32[]{:S(2)}) async-start(f32[16,32,256]{2,1,0:T(8,128)} %bitcast.9), calls=%async_computation.5 | async-start | bytes 1048576 | tf_op jit(solution)/shard_map/all_to_all | solution.py:294
  140.9 10.4 %all-to-all-done.5 = f32[16,32,256]{2,1,0:T(8,128)S(1)} async-done(((f32[16,32,256]{2,1,0:T(8,128)}), f32[16,32,256]{2,1,0:T(8,128)S(1)}, u32[]{:S(2)}, u32[]{:S(2)}) %all-to-all-start.5) | async-done | bytes 524320 | tf_op jit(solution)/shard_map/all_to_all | solution.py:294
  (58 shorter events, 5.1 us)
Async XLA Ops:
  0.6 13.2 %copy-start.12 = (f32[512,256]{1,0:T(8,128)S(1)}, f32[512,256]{1,0:T(8,128)}, u32[]{:S(2)}) copy-start(f32[512,256]{1,0:T(8,128)} %own_hbm.1) | copy-start | bytes 1572868
  0.6 15.2 %copy-start.15 = (f32[32,256]{1,0:T(8,128)S(1)}, f32[32,256]{1,0:T(8,128)}, u32[]{:S(2)}) copy-start(f32[32,256]{1,0:T(8,128)} %param.7) | copy-start | bytes 98308
  2.0 29.0 %copy-start = (s32[3,1]{1,0:T(4,128)S(1)}, s32[3,1]{1,0:T(4,128)}, u32[]{:S(2)}) copy-start(s32[3,1]{1,0:T(4,128)} %copy.8.count_ref) | copy-start | bytes 40
  2.0 29.0 %copy-start.3 = (s32[3,16]{1,0:T(4,128)S(1)}, s32[3,16]{1,0:T(4,128)}, u32[]{:S(2)}) copy-start(s32[3,16]{1,0:T(4,128)} %rows_ref.11) | copy-start | bytes 580
  2.0 29.0 %copy-start.6 = (s32[3,16]{1,0:T(4,128)S(1)}, s32[3,16]{1,0:T(4,128)}, u32[]{:S(2)}) copy-start(s32[3,16]{1,0:T(4,128)} %cols_ref.11) | copy-start | bytes 580
  5.1 15.2 %collective-permute-start = (f32[17,64,128]{2,1,0:T(8,128)}, f32[17,64,128]{2,1,0:T(8,128)S(1)}, u32[]{:S(2)}, u32[]{:S(2)}) collective-permute-start(f32[17,64,128]{2,1,0:T(8,128)} %get-tuple-element.27), channel_id=1, source_target_pairs={{0,1},{1,0},{2,3},{3,2},{4,5},{5,4},{6,7},{7,6},{8,9},{9,8},{10,11... | collective-permute-start | bytes 1671176 | tf_op jit(solution)/shard_map/ppermute | solution.py:290
  13.9 6.4 %collective-permute-start.1 = (f32[512,256]{1,0:T(8,128)S(1)}, f32[512,256]{1,0:T(8,128)S(1)}, u32[]{:S(2)}, u32[]{:S(2)}) collective-permute-start(f32[512,256]{1,0:T(8,128)S(1)} %copy-done.12), channel_id=1, source_target_pairs={{0,1},{1,0},{2,3},{3,2},{4,5},{5,4},{6,7},{7,6},{8,9},{9,8},{10,11... | collective-permute-start | bytes 1572872 | tf_op jit(solution)/shard_map/ppermute | solution.py:290
  16.7 14.4 %all-to-all-start = ((f32[16,32,256]{2,1,0:T(8,128)}), f32[16,32,256]{2,1,0:T(8,128)S(1)}, u32[]{:S(2)}, u32[]{:S(2)}) async-start(f32[16,32,256]{2,1,0:T(8,128)} %broadcast_in_dim.6), calls=%async_computation | async-start | bytes 1048576 | tf_op jit(solution)/shard_map/all_to_all | solution.py:294
  20.2 10.8 %copy-start.13 = (f32[512,256]{1,0:T(8,128)}, f32[512,256]{1,0:T(8,128)S(1)}, u32[]{:S(2)}) copy-start(f32[512,256]{1,0:T(8,128)S(1)} %collective-permute-done.1.other_users.other_hbm) | copy-start | bytes 1572868
  20.3 10.8 %copy-start.18 = (f32[17,64,128]{2,1,0:T(8,128)}, f32[17,64,128]{2,1,0:T(8,128)S(1)}, u32[]{:S(2)}) copy-start(f32[17,64,128]{2,1,0:T(8,128)S(1)} %collective-permute-done.other_hbm) | copy-start | bytes 1671172
  36.7 18.5 %collective-permute-start.2 = (f32[1024,256]{1,0:T(8,128)}, f32[1024,256]{1,0:T(8,128)S(1)}, u32[]{:S(2)}, u32[]{:S(2)}) collective-permute-start(f32[1024,256]{1,0:T(8,128)} %get-tuple-element.31.here_hbm), channel_id=1, source_target_pairs={{0,1},{1,0},{2,3},{3,2},{4,5},{5,4},{6,7},{7,6},{8,9},{9,8},{10,11... | collective-permute-start | bytes 3145736 | tf_op jit(solution)/shard_map/ppermute | solution.py:290
  40.3 14.9 %all-to-all-start.1 = ((f32[16,32,256]{2,1,0:T(8,128)}), f32[16,32,256]{2,1,0:T(8,128)S(1)}, u32[]{:S(2)}, u32[]{:S(2)}) async-start(f32[16,32,256]{2,1,0:T(8,128)} %bitcast.3), calls=%async_computation.1 | async-start | bytes 1048576 | tf_op jit(solution)/shard_map/all_to_all | solution.py:294
  46.9 22.8 %collective-permute-start.3 = (f32[17,64,128]{2,1,0:T(8,128)}, f32[17,64,128]{2,1,0:T(8,128)S(1)}, u32[]{:S(2)}, u32[]{:S(2)}) collective-permute-start(f32[17,64,128]{2,1,0:T(8,128)} %get-tuple-element.36), channel_id=1, source_target_pairs={{0,1},{1,0},{2,3},{3,2},{4,5},{5,4},{6,7},{7,6},{8,9},{9,8},{10,11... | collective-permute-start | bytes 1671176 | tf_op jit(solution)/shard_map/ppermute | solution.py:290
  55.3 14.5 %copy-start.10 = (f32[1024,256]{1,0:T(8,128)}, f32[1024,256]{1,0:T(8,128)S(1)}, u32[]{:S(2)}) copy-start(f32[1024,256]{1,0:T(8,128)S(1)} %collective-permute-done.2.there_hbm) | copy-start | bytes 3145732
  55.3 10.0 %collective-permute-start.4 = (f32[32,256]{1,0:T(8,128)S(1)}, f32[32,256]{1,0:T(8,128)S(1)}, u32[]{:S(2)}, u32[]{:S(2)}) collective-permute-start(f32[32,256]{1,0:T(8,128)S(1)} %multiply_add_fusion.3), channel_id=1, source_target_pairs={{32,0},{64,32},{96,64},{128,96},{160,128},{192,160},{224,192},{256... | collective-permute-start | bytes 98312 | tf_op jit(solution)/shard_map/ppermute | solution.py:300
  66.1 13.2 %all-to-all-start.2 = ((f32[16,32,256]{2,1,0:T(8,128)}), f32[16,32,256]{2,1,0:T(8,128)S(1)}, u32[]{:S(2)}, u32[]{:S(2)}) async-start(f32[16,32,256]{2,1,0:T(8,128)} %broadcast_in_dim.7), calls=%async_computation.2 | async-start | bytes 1048576 | tf_op jit(solution)/shard_map/all_to_all | solution.py:294
  69.7 9.6 %copy-start.1 = (s32[3,1]{1,0:T(4,128)S(1)}, s32[3,1]{1,0:T(4,128)}, u32[]{:S(2)}) copy-start(s32[3,1]{1,0:T(4,128)} %copy.8.count_ref) | copy-start | bytes 40
  69.8 9.6 %copy-start.4 = (s32[3,16]{1,0:T(4,128)S(1)}, s32[3,16]{1,0:T(4,128)}, u32[]{:S(2)}) copy-start(s32[3,16]{1,0:T(4,128)} %rows_ref.11) | copy-start | bytes 580
  69.8 9.6 %copy-start.7 = (s32[3,16]{1,0:T(4,128)S(1)}, s32[3,16]{1,0:T(4,128)}, u32[]{:S(2)}) copy-start(s32[3,16]{1,0:T(4,128)} %cols_ref.11) | copy-start | bytes 580
  85.1 19.7 %collective-permute-start.5 = (f32[1024,256]{1,0:T(8,128)}, f32[1024,256]{1,0:T(8,128)S(1)}, u32[]{:S(2)}, u32[]{:S(2)}) collective-permute-start(f32[1024,256]{1,0:T(8,128)} %get-tuple-element.39.here_hbm), channel_id=1, source_target_pairs={{0,1},{1,0},{2,3},{3,2},{4,5},{5,4},{6,7},{7,6},{8,9},{9,8},{10,11... | collective-permute-start | bytes 3145736 | tf_op jit(solution)/shard_map/ppermute | solution.py:290
  89.8 14.9 %all-to-all-start.3 = ((f32[16,32,256]{2,1,0:T(8,128)}), f32[16,32,256]{2,1,0:T(8,128)S(1)}, u32[]{:S(2)}, u32[]{:S(2)}) async-start(f32[16,32,256]{2,1,0:T(8,128)} %bitcast.6), calls=%async_computation.3 | async-start | bytes 1048576 | tf_op jit(solution)/shard_map/all_to_all | solution.py:294
  96.4 18.9 %collective-permute-start.6 = (f32[17,64,128]{2,1,0:T(8,128)}, f32[17,64,128]{2,1,0:T(8,128)S(1)}, u32[]{:S(2)}, u32[]{:S(2)}) collective-permute-start(f32[17,64,128]{2,1,0:T(8,128)} %get-tuple-element.43), channel_id=1, source_target_pairs={{0,1},{1,0},{2,3},{3,2},{4,5},{5,4},{6,7},{7,6},{8,9},{9,8},{10,11... | collective-permute-start | bytes 1671176 | tf_op jit(solution)/shard_map/ppermute | solution.py:290
  104.8 10.5 %copy-start.9 = (f32[1024,256]{1,0:T(8,128)}, f32[1024,256]{1,0:T(8,128)S(1)}, u32[]{:S(2)}) copy-start(f32[1024,256]{1,0:T(8,128)S(1)} %collective-permute-done.5.there_hbm) | copy-start | bytes 3145732
  104.8 5.9 %collective-permute-start.7 = (f32[32,256]{1,0:T(8,128)S(1)}, f32[32,256]{1,0:T(8,128)S(1)}, u32[]{:S(2)}, u32[]{:S(2)}) collective-permute-start(f32[32,256]{1,0:T(8,128)S(1)} %multiply_add_fusion.2), channel_id=1, source_target_pairs={{32,0},{64,32},{96,64},{128,96},{160,128},{192,160},{224,192},{256... | collective-permute-start | bytes 98312 | tf_op jit(solution)/shard_map/ppermute | solution.py:300
  111.5 13.2 %all-to-all-start.4 = ((f32[16,32,256]{2,1,0:T(8,128)}), f32[16,32,256]{2,1,0:T(8,128)S(1)}, u32[]{:S(2)}, u32[]{:S(2)}) async-start(f32[16,32,256]{2,1,0:T(8,128)} %broadcast_in_dim.8), calls=%async_computation.4 | async-start | bytes 1048576 | tf_op jit(solution)/shard_map/all_to_all | solution.py:294
  115.3 3.0 %copy-start.16 = (f32[17,64,128]{2,1,0:T(8,128)}, f32[17,64,128]{2,1,0:T(8,128)S(1)}, u32[]{:S(2)}) copy-start(f32[17,64,128]{2,1,0:T(8,128)S(1)} %collective-permute-done.6.other_hbm) | copy-start | bytes 1671172
  115.3 10.2 %copy-start.2 = (s32[3,1]{1,0:T(4,128)S(1)}, s32[3,1]{1,0:T(4,128)}, u32[]{:S(2)}) copy-start(s32[3,1]{1,0:T(4,128)} %copy.8.count_ref) | copy-start | bytes 40
  115.4 10.2 %copy-start.5 = (s32[3,16]{1,0:T(4,128)S(1)}, s32[3,16]{1,0:T(4,128)}, u32[]{:S(2)}) copy-start(s32[3,16]{1,0:T(4,128)} %rows_ref.11) | copy-start | bytes 580
  115.4 10.2 %copy-start.8 = (s32[3,16]{1,0:T(4,128)S(1)}, s32[3,16]{1,0:T(4,128)}, u32[]{:S(2)}) copy-start(s32[3,16]{1,0:T(4,128)} %cols_ref.11) | copy-start | bytes 580
  125.6 14.4 %copy-start.14 = (f32[512,256]{1,0:T(8,128)S(1)}, f32[512,256]{1,0:T(8,128)}, u32[]{:S(2)}) copy-start(f32[512,256]{1,0:T(8,128)} %get-tuple-element.42.own_users) | copy-start | bytes 1572868
  131.6 8.4 %collective-permute-start.8 = (f32[512,256]{1,0:T(8,128)}, f32[512,256]{1,0:T(8,128)S(1)}, u32[]{:S(2)}, u32[]{:S(2)}) collective-permute-start(f32[512,256]{1,0:T(8,128)} %get-tuple-element.48), channel_id=1, source_target_pairs={{0,1},{1,0},{2,3},{3,2},{4,5},{5,4},{6,7},{7,6},{8,9},{9,8},{10,11... | collective-permute-start | bytes 1572872 | tf_op jit(solution)/shard_map/ppermute | solution.py:290
  136.4 14.9 %all-to-all-start.5 = ((f32[16,32,256]{2,1,0:T(8,128)}), f32[16,32,256]{2,1,0:T(8,128)S(1)}, u32[]{:S(2)}, u32[]{:S(2)}) async-start(f32[16,32,256]{2,1,0:T(8,128)} %bitcast.9), calls=%async_computation.5 | async-start | bytes 1048576 | tf_op jit(solution)/shard_map/all_to_all | solution.py:294
  (2 other events, 3.8 us)

commit v4 on v3

--- a/solution.py
+++ b/solution.py
@@ -47,7 +47,9 @@
 SMEM = pl.BlockSpec(memory_space=pltpu.SMEM)
 WIDTH = 2 * TILE
 BLOCKS = 2 * U_DEV // WIDTH
+FIRST_GRANT = 53000
 STEP_GRANT = 54000
+LAST_GRANT = 53000
 UPDATE_GRANT = 60 * 1024
 
 
@@ -87,7 +89,7 @@
     row = jnp.full((8, TILE), -1, jnp.int32)
     for k in range(K_MAX):
         cell = rows_ref[tick, k] * I_TILES + cols_ref[tick, k]
-        row = jnp.where((lane == cell) & (k < count_ref[tick, 0]), k, row)
+        row = jnp.where((lane == cell) & (k < count_ref[tick]), k, row)
     sent[K_MAX, pl.ds(0, 8), :] = row.astype(f32)
     sent[K_MAX, pl.ds(8, HALF - 8), :] = jnp.zeros((HALF - 8, TILE), f32)
     last = pltpu.make_async_copy(sent.at[pl.ds(K_MAX, 1)], sent_hbm.at[pl.ds(K_MAX, 1)], sems.at[12])
@@ -155,7 +157,7 @@
         own_map[cell] = -1
     for k in range(K_MAX):
         cell = rows_ref[tick, k] * I_TILES + cols_ref[tick, k]
-        own_map[cell] = jnp.where(k < count_ref[tick, 0], k, own_map[cell])
+        own_map[cell] = jnp.where(k < count_ref[tick], k, own_map[cell])
 
     def split(block):
         return halves(users[rows(block), :])
@@ -190,9 +192,9 @@
             item_grad[...] += grad
 
     panel_load.wait()
+    panel = halves(panel_ref[...])
     user_loads[0].wait()
     user_loads[1].wait()
-    panel = halves(panel_ref[...])
     predict(0)
     predict(1)
     own_load.wait()
@@ -237,7 +239,7 @@
         [half_panel, both, pltpu.VMEM(cut, f32), pltpu.VMEM(cut, f32),
          pltpu.VMEM((BLOCKS, ITEMS_CORE, WIDTH), f32), half_panel, both, pltpu.SMEM((CELLS,), jnp.int32),
          pltpu.SemaphoreType.DMA((3 + 2 * BLOCKS + ITEMS_CORE // TILE,))],
-        2400000000, 4000000, STEP_GRANT,
+        2400000000, 4000000, (FIRST_GRANT, STEP_GRANT, LAST_GRANT)[tick],
     )(rows, cols, count, other_map, panel, own, other, own_tiles, other_tiles)
 
 
@@ -303,6 +305,7 @@
 def shards(user_factors, item_factors, ratings, tile_users, tile_items, tile_count):
     core = lax.rem(lax.axis_index("owner"), 2).reshape(1)
     own, share = user_factors, item_factors
+    tile_count = tile_count.reshape(TICKS)
     other = swapped(own)
     for tick in range(TICKS):
         kept, sent = turned_tiles(tick, core, tile_users, tile_items, tile_count, ratings)

time: 153 us -> 150 us (0.980)
  local copies, waits for them, and re-layouts: 4.82 us -> 2.67 us
    unnamed x39 -> x36, local copies, waits for them, and re-layouts: 2.24 us -> 0.1 us
where the time goes in v4:
time: 150 us; the launch traced here: 149 us
  starting transfers between devices  63 us (42%)
  waiting for transfers between devices  49.1 us (33%)
  Pallas kernels  31.3 us (21%)
  local copies, waits for them, and re-layouts  2.67 us (2%)
  other arithmetic  1.66 us (1%)
    all_to_all x6, waiting for transfers between devices, exchanged(): lax.all_to_all(blocks, 'owner', split_axis=0, concat_axis=0, axis_index_g...  47.1 us
    ppermute x7, starting transfers between devices, swapped(): return lax.ppermute(x, 'owner', PARTNERS)  27.5 us
    all_to_all x6, starting transfers between devices, exchanged(): lax.all_to_all(blocks, 'owner', split_axis=0, concat_axis=0, axis_index_g...  21.6 us
    pallas_call x3, Pallas kernels, item_and_user_grads(): call(functools.partial(step_kernel, tick, last), (shape((ITEMS_CORE, R),...  16.6 us
    ppermute x2, starting transfers between devices, passed_along(): return lax.ppermute(block, axis, route)  13.9 us
    pallas_call x3, Pallas kernels, turned_tiles(): call(functools.partial(turn_kernel, tick), (shape((K_MAX, HALF, TILE), f3...  8.91 us
    pallas_call x2, Pallas kernels, updated_users(): call(update_kernel, (new, new), [ANY] * 4, (ANY, ANY), [both, both, both,...  5.81 us
  transfers between devices with their start and end apart: 15, of which 8 were waited for; matrix products, arithmetic and copies ran while one was open for 2% of the time, Pallas kernels for 8%

profile of v4, /device:TPU:1, one launch (start us, length us, event | category | flops | bytes accessed | tf_op | source)
XLA Modules:
  0.0 149.0 jit_solution(10625371111664893422)
XLA Ops:
  0.7 3.0 %shard_map.77 = (f32[16,64,128]{2,1,0:T(8,128)}, f32[17,64,128]{2,1,0:T(8,128)}) custom-call(s32[1]{0:T(128)} %bitcast.core_ref, s32[3,16]{1,0:T(4,128)} %rows_ref.11, s32[3,16]{1,0:T(4,128)} %cols_ref.11, s32[3]{0:T(128)} %bitcast.17, bf16[3,16,128,128]{3,2,1,0:T(8,128)(2,1)} %tiles_hbm.5), custom_call_target="tpu_custom_call" | custom-call | flops 1000000 | bytes 1600000 | tf_op jit(solution)/shard_map/pallas_call | solution.py:117
  3.7 8.7 %collective-permute-start = (f32[17,64,128]{2,1,0:T(8,128)}, f32[17,64,128]{2,1,0:T(8,128)S(1)}, u32[]{:S(2)}, u32[]{:S(2)}) collective-permute-start(f32[17,64,128]{2,1,0:T(8,128)} %get-tuple-element.27), channel_id=1, source_target_pairs={{0,1},{1,0},{2,3},{3,2},{4,5},{5,4},{6,7},{7,6},{8,9},{9,8},{10,11... | collective-permute-start | bytes 1671176 | tf_op jit(solution)/shard_map/ppermute | solution.py:292
  12.5 1.9 %collective-permute-start.1 = (f32[512,256]{1,0:T(8,128)S(1)}, f32[512,256]{1,0:T(8,128)S(1)}, u32[]{:S(2)}, u32[]{:S(2)}) collective-permute-start(f32[512,256]{1,0:T(8,128)S(1)} %copy-done), channel_id=1, source_target_pairs={{0,1},{1,0},{2,3},{3,2},{4,5},{5,4},{6,7},{7,6},{8,9},{9,8},{10,11... | collective-permute-start | bytes 1572872 | tf_op jit(solution)/shard_map/ppermute | solution.py:292
  15.3 3.6 %all-to-all-start = ((f32[16,32,256]{2,1,0:T(8,128)}), f32[16,32,256]{2,1,0:T(8,128)S(1)}, u32[]{:S(2)}, u32[]{:S(2)}) async-start(f32[16,32,256]{2,1,0:T(8,128)} %broadcast_in_dim.6), calls=%async_computation | async-start | bytes 1048576 | tf_op jit(solution)/shard_map/all_to_all | solution.py:296
  18.9 10.8 %all-to-all-done = f32[16,32,256]{2,1,0:T(8,128)S(1)} async-done(((f32[16,32,256]{2,1,0:T(8,128)}), f32[16,32,256]{2,1,0:T(8,128)S(1)}, u32[]{:S(2)}, u32[]{:S(2)}) %all-to-all-start) | async-done | bytes 524320 | tf_op jit(solution)/shard_map/all_to_all | solution.py:296
  29.7 5.2 %shard_map.78 = (f32[512,256]{1,0:T(8,128)}, f32[1024,256]{1,0:T(8,128)}) custom-call(s32[3,16]{1,0:T(4,128)S(1)} %copy-done.2, s32[3,16]{1,0:T(4,128)S(1)} %copy-done.5, s32[3]{0:T(128)S(1)} %bitcast.20, s32[32]{0:T(128)S(1)} %convert_bitcast_fusion.other_map, f32[512,256]{1,0:T(8,128)S(1)} %bitcast.16, f32[512,256]{1,0:T(8,128)S(1)} %copy-done, ...), custom_call_target="tpu_custom_call" | custom-call | flops 2400000000 | bytes 4000000 | tf_op jit(solution)/shard_map/pallas_call | solution.py:235
  35.0 3.6 %collective-permute-start.2 = (f32[1024,256]{1,0:T(8,128)}, f32[1024,256]{1,0:T(8,128)S(1)}, u32[]{:S(2)}, u32[]{:S(2)}) collective-permute-start(f32[1024,256]{1,0:T(8,128)} %get-tuple-element.31.here_hbm), channel_id=1, source_target_pairs={{0,1},{1,0},{2,3},{3,2},{4,5},{5,4},{6,7},{7,6},{8,9},{9,8},{10,11... | collective-permute-start | bytes 3145736 | tf_op jit(solution)/shard_map/ppermute | solution.py:292
  38.5 3.6 %all-to-all-start.1 = ((f32[16,32,256]{2,1,0:T(8,128)}), f32[16,32,256]{2,1,0:T(8,128)S(1)}, u32[]{:S(2)}, u32[]{:S(2)}) async-start(f32[16,32,256]{2,1,0:T(8,128)} %bitcast.4), calls=%async_computation.1 | async-start | bytes 1048576 | tf_op jit(solution)/shard_map/all_to_all | solution.py:296
  42.1 2.9 %shard_map.80 = (f32[16,64,128]{2,1,0:T(8,128)}, f32[17,64,128]{2,1,0:T(8,128)}) custom-call(s32[1]{0:T(128)} %bitcast.core_ref, s32[3,16]{1,0:T(4,128)} %rows_ref.11, s32[3,16]{1,0:T(4,128)} %cols_ref.11, s32[3]{0:T(128)} %bitcast.18, bf16[3,16,128,128]{3,2,1,0:T(8,128)(2,1)} %tiles_hbm.5), custom_call_target="tpu_custom_call" | custom-call | flops 1000000 | bytes 1600000 | tf_op jit(solution)/shard_map/pallas_call | solution.py:117
  45.1 1.9 %collective-permute-start.3 = (f32[17,64,128]{2,1,0:T(8,128)}, f32[17,64,128]{2,1,0:T(8,128)S(1)}, u32[]{:S(2)}, u32[]{:S(2)}) collective-permute-start(f32[17,64,128]{2,1,0:T(8,128)} %get-tuple-element.36), channel_id=1, source_target_pairs={{0,1},{1,0},{2,3},{3,2},{4,5},{5,4},{6,7},{7,6},{8,9},{9,8},{10,11... | collective-permute-start | bytes 1671176 | tf_op jit(solution)/shard_map/ppermute | solution.py:292
  47.0 6.4 %all-to-all-done.1 = f32[16,32,256]{2,1,0:T(8,128)S(1)} async-done(((f32[16,32,256]{2,1,0:T(8,128)}), f32[16,32,256]{2,1,0:T(8,128)S(1)}, u32[]{:S(2)}, u32[]{:S(2)}) %all-to-all-start.1) | async-done | bytes 524320 | tf_op jit(solution)/shard_map/all_to_all | solution.py:296
  53.5 9.0 %collective-permute-start.4 = (f32[32,256]{1,0:T(8,128)S(1)}, f32[32,256]{1,0:T(8,128)S(1)}, u32[]{:S(2)}, u32[]{:S(2)}) collective-permute-start(f32[32,256]{1,0:T(8,128)S(1)} %multiply_add_fusion.3), channel_id=1, source_target_pairs={{32,0},{64,32},{96,64},{128,96},{160,128},{192,160},{224,192},{256... | collective-permute-start | bytes 98312 | tf_op jit(solution)/shard_map/ppermute | solution.py:302
  62.5 1.0 collective-permute-done.4
  64.3 3.6 %all-to-all-start.2 = ((f32[16,32,256]{2,1,0:T(8,128)}), f32[16,32,256]{2,1,0:T(8,128)S(1)}, u32[]{:S(2)}, u32[]{:S(2)}) async-start(f32[16,32,256]{2,1,0:T(8,128)} %broadcast_in_dim.7), calls=%async_computation.2 | async-start | bytes 1048576 | tf_op jit(solution)/shard_map/all_to_all | solution.py:296
  68.0 2.9 %shard_map.79 = (f32[512,256]{1,0:T(8,128)}, f32[512,256]{1,0:T(8,128)}) custom-call(f32[512,256]{1,0:T(8,128)} %own_hbm.1, f32[512,256]{1,0:T(8,128)} %copy-done.1, f32[1024,256]{1,0:T(8,128)} %get-tuple-element.31.here_hbm, f32[1024,256]{1,0:T(8,128)} %copy-done.12), custom_call_target="tpu_custom_call" | custom-call | flops 1000000 | bytes 4000000 | tf_op jit(solution)/shard_map/pallas_call | solution.py:285
  70.9 6.7 %all-to-all-done.2 = f32[16,32,256]{2,1,0:T(8,128)S(1)} async-done(((f32[16,32,256]{2,1,0:T(8,128)}), f32[16,32,256]{2,1,0:T(8,128)S(1)}, u32[]{:S(2)}, u32[]{:S(2)}) %all-to-all-start.2) | async-done | bytes 524320 | tf_op jit(solution)/shard_map/all_to_all | solution.py:296
  77.6 5.7 %shard_map.81 = (f32[512,256]{1,0:T(8,128)}, f32[1024,256]{1,0:T(8,128)}) custom-call(s32[3,16]{1,0:T(4,128)S(1)} %copy-done.3, s32[3,16]{1,0:T(4,128)S(1)} %copy-done.6, s32[3]{0:T(128)S(1)} %bitcast.21, s32[32]{0:T(128)S(1)} %fusion.1.other_map, f32[512,256]{1,0:T(8,128)S(1)} %bitcast.15, f32[512,256]{1,0:T(8,128)} %get-tuple-element.34.own_users.own_hbm, ...), custom_call_target="tpu_custom_call" | custom-call | flops 2400000000 | bytes 4000000 | tf_op jit(solution)/shard_map/pallas_call | solution.py:235
  83.3 4.7 %collective-permute-start.5 = (f32[1024,256]{1,0:T(8,128)}, f32[1024,256]{1,0:T(8,128)S(1)}, u32[]{:S(2)}, u32[]{:S(2)}) collective-permute-start(f32[1024,256]{1,0:T(8,128)} %get-tuple-element.39.here_hbm), channel_id=1, source_target_pairs={{0,1},{1,0},{2,3},{3,2},{4,5},{5,4},{6,7},{7,6},{8,9},{9,8},{10,11... | collective-permute-start | bytes 3145736 | tf_op jit(solution)/shard_map/ppermute | solution.py:292
  88.0 3.6 %all-to-all-start.3 = ((f32[16,32,256]{2,1,0:T(8,128)}), f32[16,32,256]{2,1,0:T(8,128)S(1)}, u32[]{:S(2)}, u32[]{:S(2)}) async-start(f32[16,32,256]{2,1,0:T(8,128)} %bitcast.7), calls=%async_computation.3 | async-start | bytes 1048576 | tf_op jit(solution)/shard_map/all_to_all | solution.py:296
  91.6 2.9 %shard_map.83 = (f32[16,64,128]{2,1,0:T(8,128)}, f32[17,64,128]{2,1,0:T(8,128)}) custom-call(s32[1]{0:T(128)} %bitcast.core_ref, s32[3,16]{1,0:T(4,128)} %rows_ref.11, s32[3,16]{1,0:T(4,128)} %cols_ref.11, s32[3]{0:T(128)} %bitcast.19, bf16[3,16,128,128]{3,2,1,0:T(8,128)(2,1)} %tiles_hbm.5), custom_call_target="tpu_custom_call" | custom-call | flops 1000000 | bytes 1600000 | tf_op jit(solution)/shard_map/pallas_call | solution.py:117
  94.6 1.9 %collective-permute-start.6 = (f32[17,64,128]{2,1,0:T(8,128)}, f32[17,64,128]{2,1,0:T(8,128)S(1)}, u32[]{:S(2)}, u32[]{:S(2)}) collective-permute-start(f32[17,64,128]{2,1,0:T(8,128)} %get-tuple-element.43), channel_id=1, source_target_pairs={{0,1},{1,0},{2,3},{3,2},{4,5},{5,4},{6,7},{7,6},{8,9},{9,8},{10,11... | collective-permute-start | bytes 1671176 | tf_op jit(solution)/shard_map/ppermute | solution.py:292
  96.5 6.4 %all-to-all-done.3 = f32[16,32,256]{2,1,0:T(8,128)S(1)} async-done(((f32[16,32,256]{2,1,0:T(8,128)}), f32[16,32,256]{2,1,0:T(8,128)S(1)}, u32[]{:S(2)}, u32[]{:S(2)}) %all-to-all-start.3) | async-done | bytes 524320 | tf_op jit(solution)/shard_map/all_to_all | solution.py:296
  103.0 4.9 %collective-permute-start.7 = (f32[32,256]{1,0:T(8,128)S(1)}, f32[32,256]{1,0:T(8,128)S(1)}, u32[]{:S(2)}, u32[]{:S(2)}) collective-permute-start(f32[32,256]{1,0:T(8,128)S(1)} %multiply_add_fusion.2), channel_id=1, source_target_pairs={{32,0},{64,32},{96,64},{128,96},{160,128},{192,160},{224,192},{256... | collective-permute-start | bytes 98312 | tf_op jit(solution)/shard_map/ppermute | solution.py:302
  107.9 1.0 collective-permute-done.7
  109.7 3.8 %all-to-all-start.4 = ((f32[16,32,256]{2,1,0:T(8,128)}), f32[16,32,256]{2,1,0:T(8,128)S(1)}, u32[]{:S(2)}, u32[]{:S(2)}) async-start(f32[16,32,256]{2,1,0:T(8,128)} %broadcast_in_dim.8), calls=%async_computation.4 | async-start | bytes 1048576 | tf_op jit(solution)/shard_map/all_to_all | solution.py:296
  113.6 2.9 %shard_map.82 = (f32[512,256]{1,0:T(8,128)}, f32[512,256]{1,0:T(8,128)}) custom-call(f32[512,256]{1,0:T(8,128)} %get-tuple-element.34.own_users.own_hbm, f32[512,256]{1,0:T(8,128)} %get-tuple-element.35.other_users.other_hbm, f32[1024,256]{1,0:T(8,128)} %get-tuple-element.39.here_hbm, f32[1024,256]{1,0:T(8,128)} %copy-done.11), custom_call_target="tpu_custom_call" | custom-call | flops 1000000 | bytes 4000000 | tf_op jit(solution)/shard_map/pallas_call | solution.py:285
  116.5 6.5 %all-to-all-done.4 = f32[16,32,256]{2,1,0:T(8,128)S(1)} async-done(((f32[16,32,256]{2,1,0:T(8,128)}), f32[16,32,256]{2,1,0:T(8,128)S(1)}, u32[]{:S(2)}, u32[]{:S(2)}) %all-to-all-start.4) | async-done | bytes 524320 | tf_op jit(solution)/shard_map/all_to_all | solution.py:296
  123.0 5.7 %shard_map.84 = (f32[512,256]{1,0:T(8,128)}, f32[512,256]{1,0:T(8,128)S(1)}, f32[512,256]{1,0:T(8,128)S(1)}) custom-call(s32[3,16]{1,0:T(4,128)S(1)} %copy-done.4, s32[3,16]{1,0:T(4,128)S(1)} %copy-done.7, s32[3]{0:T(128)S(1)} %bitcast.22, s32[32]{0:T(128)S(1)} %fusion.other_map, f32[512,256]{1,0:T(8,128)S(1)} %bitcast.14, ...), custom_call_target="tpu_custom_call" | custom-call | flops 2400000000 | bytes 4000000 | tf_op jit(solution)/shard_map/pallas_call | solution.py:235
  128.7 4.7 %collective-permute-start.8 = (f32[512,256]{1,0:T(8,128)S(1)}, f32[512,256]{1,0:T(8,128)S(1)}, u32[]{:S(2)}, u32[]{:S(2)}) collective-permute-start(f32[512,256]{1,0:T(8,128)S(1)} %get-tuple-element.48), channel_id=1, source_target_pairs={{0,1},{1,0},{2,3},{3,2},{4,5},{5,4},{6,7},{7,6},{8,9},{9,8},{10,11... | collective-permute-start | bytes 1572872 | tf_op jit(solution)/shard_map/ppermute | solution.py:292
  133.4 3.6 %all-to-all-start.5 = ((f32[16,32,256]{2,1,0:T(8,128)}), f32[16,32,256]{2,1,0:T(8,128)S(1)}, u32[]{:S(2)}, u32[]{:S(2)}) async-start(f32[16,32,256]{2,1,0:T(8,128)} %bitcast.10), calls=%async_computation.5 | async-start | bytes 1048576 | tf_op jit(solution)/shard_map/all_to_all | solution.py:296
  137.0 0.9 multiply_add_fusion
  137.9 10.4 %all-to-all-done.5 = f32[16,32,256]{2,1,0:T(8,128)S(1)} async-done(((f32[16,32,256]{2,1,0:T(8,128)}), f32[16,32,256]{2,1,0:T(8,128)S(1)}, u32[]{:S(2)}, u32[]{:S(2)}) %all-to-all-start.5) | async-done | bytes 524320 | tf_op jit(solution)/shard_map/all_to_all | solution.py:296
  (55 shorter events, 3.5 us)
Async XLA Ops:
  0.6 11.9 %copy-start = (f32[512,256]{1,0:T(8,128)S(1)}, f32[512,256]{1,0:T(8,128)}, u32[]{:S(2)}) copy-start(f32[512,256]{1,0:T(8,128)} %own_hbm.1) | copy-start | bytes 1572868
  0.6 13.8 %copy-start.14 = (f32[32,256]{1,0:T(8,128)S(1)}, f32[32,256]{1,0:T(8,128)}, u32[]{:S(2)}) copy-start(f32[32,256]{1,0:T(8,128)} %param.7) | copy-start | bytes 98308
  0.7 29.0 %copy-start.2 = (s32[3,16]{1,0:T(4,128)S(1)}, s32[3,16]{1,0:T(4,128)}, u32[]{:S(2)}) copy-start(s32[3,16]{1,0:T(4,128)} %rows_ref.11) | copy-start | bytes 580
  0.7 29.0 %copy-start.5 = (s32[3,16]{1,0:T(4,128)S(1)}, s32[3,16]{1,0:T(4,128)}, u32[]{:S(2)}) copy-start(s32[3,16]{1,0:T(4,128)} %cols_ref.11) | copy-start | bytes 580
  0.7 29.0 %copy-start.8 = (s32[3,1]{0,1:T(1,128)S(1)}, s32[3,1]{0,1:T(1,128)}, u32[]{:S(2)}) copy-start(s32[3,1]{0,1:T(1,128)} %param.11) | copy-start | bytes 40
  3.7 15.2 %collective-permute-start = (f32[17,64,128]{2,1,0:T(8,128)}, f32[17,64,128]{2,1,0:T(8,128)S(1)}, u32[]{:S(2)}, u32[]{:S(2)}) collective-permute-start(f32[17,64,128]{2,1,0:T(8,128)} %get-tuple-element.27), channel_id=1, source_target_pairs={{0,1},{1,0},{2,3},{3,2},{4,5},{5,4},{6,7},{7,6},{8,9},{9,8},{10,11... | collective-permute-start | bytes 1671176 | tf_op jit(solution)/shard_map/ppermute | solution.py:292
  12.5 6.4 %collective-permute-start.1 = (f32[512,256]{1,0:T(8,128)S(1)}, f32[512,256]{1,0:T(8,128)S(1)}, u32[]{:S(2)}, u32[]{:S(2)}) collective-permute-start(f32[512,256]{1,0:T(8,128)S(1)} %copy-done), channel_id=1, source_target_pairs={{0,1},{1,0},{2,3},{3,2},{4,5},{5,4},{6,7},{7,6},{8,9},{9,8},{10,11... | collective-permute-start | bytes 1572872 | tf_op jit(solution)/shard_map/ppermute | solution.py:292
  15.3 14.4 %all-to-all-start = ((f32[16,32,256]{2,1,0:T(8,128)}), f32[16,32,256]{2,1,0:T(8,128)S(1)}, u32[]{:S(2)}, u32[]{:S(2)}) async-start(f32[16,32,256]{2,1,0:T(8,128)} %broadcast_in_dim.6), calls=%async_computation | async-start | bytes 1048576 | tf_op jit(solution)/shard_map/all_to_all | solution.py:296
  18.9 16.1 %copy-start.1 = (f32[512,256]{1,0:T(8,128)}, f32[512,256]{1,0:T(8,128)S(1)}, u32[]{:S(2)}) copy-start(f32[512,256]{1,0:T(8,128)S(1)} %collective-permute-done.1.other_users.other_hbm) | copy-start | bytes 1572868
  18.9 10.8 %copy-start.17 = (f32[17,64,128]{2,1,0:T(8,128)}, f32[17,64,128]{2,1,0:T(8,128)S(1)}, u32[]{:S(2)}) copy-start(f32[17,64,128]{2,1,0:T(8,128)S(1)} %collective-permute-done.other_hbm) | copy-start | bytes 1671172
  35.0 18.5 %collective-permute-start.2 = (f32[1024,256]{1,0:T(8,128)}, f32[1024,256]{1,0:T(8,128)S(1)}, u32[]{:S(2)}, u32[]{:S(2)}) collective-permute-start(f32[1024,256]{1,0:T(8,128)} %get-tuple-element.31.here_hbm), channel_id=1, source_target_pairs={{0,1},{1,0},{2,3},{3,2},{4,5},{5,4},{6,7},{7,6},{8,9},{9,8},{10,11... | collective-permute-start | bytes 3145736 | tf_op jit(solution)/shard_map/ppermute | solution.py:292
  38.5 14.9 %all-to-all-start.1 = ((f32[16,32,256]{2,1,0:T(8,128)}), f32[16,32,256]{2,1,0:T(8,128)S(1)}, u32[]{:S(2)}, u32[]{:S(2)}) async-start(f32[16,32,256]{2,1,0:T(8,128)} %bitcast.4), calls=%async_computation.1 | async-start | bytes 1048576 | tf_op jit(solution)/shard_map/all_to_all | solution.py:296
  45.1 22.9 %collective-permute-start.3 = (f32[17,64,128]{2,1,0:T(8,128)}, f32[17,64,128]{2,1,0:T(8,128)S(1)}, u32[]{:S(2)}, u32[]{:S(2)}) collective-permute-start(f32[17,64,128]{2,1,0:T(8,128)} %get-tuple-element.36), channel_id=1, source_target_pairs={{0,1},{1,0},{2,3},{3,2},{4,5},{5,4},{6,7},{7,6},{8,9},{9,8},{10,11... | collective-permute-start | bytes 1671176 | tf_op jit(solution)/shard_map/ppermute | solution.py:292
  53.5 14.5 %copy-start.12 = (f32[1024,256]{1,0:T(8,128)}, f32[1024,256]{1,0:T(8,128)S(1)}, u32[]{:S(2)}) copy-start(f32[1024,256]{1,0:T(8,128)S(1)} %collective-permute-done.2.there_hbm) | copy-start | bytes 3145732
  53.5 10.0 %collective-permute-start.4 = (f32[32,256]{1,0:T(8,128)S(1)}, f32[32,256]{1,0:T(8,128)S(1)}, u32[]{:S(2)}, u32[]{:S(2)}) collective-permute-start(f32[32,256]{1,0:T(8,128)S(1)} %multiply_add_fusion.3), channel_id=1, source_target_pairs={{32,0},{64,32},{96,64},{128,96},{160,128},{192,160},{224,192},{256... | collective-permute-start | bytes 98312 | tf_op jit(solution)/shard_map/ppermute | solution.py:302
  64.3 13.2 %all-to-all-start.2 = ((f32[16,32,256]{2,1,0:T(8,128)}), f32[16,32,256]{2,1,0:T(8,128)S(1)}, u32[]{:S(2)}, u32[]{:S(2)}) async-start(f32[16,32,256]{2,1,0:T(8,128)} %broadcast_in_dim.7), calls=%async_computation.2 | async-start | bytes 1048576 | tf_op jit(solution)/shard_map/all_to_all | solution.py:296
  68.0 9.6 %copy-start.3 = (s32[3,16]{1,0:T(4,128)S(1)}, s32[3,16]{1,0:T(4,128)}, u32[]{:S(2)}) copy-start(s32[3,16]{1,0:T(4,128)} %rows_ref.11) | copy-start | bytes 580
  68.0 9.6 %copy-start.6 = (s32[3,16]{1,0:T(4,128)S(1)}, s32[3,16]{1,0:T(4,128)}, u32[]{:S(2)}) copy-start(s32[3,16]{1,0:T(4,128)} %cols_ref.11) | copy-start | bytes 580
  68.0 9.6 %copy-start.9 = (s32[3,1]{0,1:T(1,128)S(1)}, s32[3,1]{0,1:T(1,128)}, u32[]{:S(2)}) copy-start(s32[3,1]{0,1:T(1,128)} %param.11) | copy-start | bytes 40
  83.3 19.7 %collective-permute-start.5 = (f32[1024,256]{1,0:T(8,128)}, f32[1024,256]{1,0:T(8,128)S(1)}, u32[]{:S(2)}, u32[]{:S(2)}) collective-permute-start(f32[1024,256]{1,0:T(8,128)} %get-tuple-element.39.here_hbm), channel_id=1, source_target_pairs={{0,1},{1,0},{2,3},{3,2},{4,5},{5,4},{6,7},{7,6},{8,9},{9,8},{10,11... | collective-permute-start | bytes 3145736 | tf_op jit(solution)/shard_map/ppermute | solution.py:292
  88.0 14.9 %all-to-all-start.3 = ((f32[16,32,256]{2,1,0:T(8,128)}), f32[16,32,256]{2,1,0:T(8,128)S(1)}, u32[]{:S(2)}, u32[]{:S(2)}) async-start(f32[16,32,256]{2,1,0:T(8,128)} %bitcast.7), calls=%async_computation.3 | async-start | bytes 1048576 | tf_op jit(solution)/shard_map/all_to_all | solution.py:296
  94.6 18.9 %collective-permute-start.6 = (f32[17,64,128]{2,1,0:T(8,128)}, f32[17,64,128]{2,1,0:T(8,128)S(1)}, u32[]{:S(2)}, u32[]{:S(2)}) collective-permute-start(f32[17,64,128]{2,1,0:T(8,128)} %get-tuple-element.43), channel_id=1, source_target_pairs={{0,1},{1,0},{2,3},{3,2},{4,5},{5,4},{6,7},{7,6},{8,9},{9,8},{10,11... | collective-permute-start | bytes 1671176 | tf_op jit(solution)/shard_map/ppermute | solution.py:292
  103.0 10.5 %copy-start.11 = (f32[1024,256]{1,0:T(8,128)}, f32[1024,256]{1,0:T(8,128)S(1)}, u32[]{:S(2)}) copy-start(f32[1024,256]{1,0:T(8,128)S(1)} %collective-permute-done.5.there_hbm) | copy-start | bytes 3145732
  103.0 5.9 %collective-permute-start.7 = (f32[32,256]{1,0:T(8,128)S(1)}, f32[32,256]{1,0:T(8,128)S(1)}, u32[]{:S(2)}, u32[]{:S(2)}) collective-permute-start(f32[32,256]{1,0:T(8,128)S(1)} %multiply_add_fusion.2), channel_id=1, source_target_pairs={{32,0},{64,32},{96,64},{128,96},{160,128},{192,160},{224,192},{256... | collective-permute-start | bytes 98312 | tf_op jit(solution)/shard_map/ppermute | solution.py:302
  109.7 13.2 %all-to-all-start.4 = ((f32[16,32,256]{2,1,0:T(8,128)}), f32[16,32,256]{2,1,0:T(8,128)S(1)}, u32[]{:S(2)}, u32[]{:S(2)}) async-start(f32[16,32,256]{2,1,0:T(8,128)} %broadcast_in_dim.8), calls=%async_computation.4 | async-start | bytes 1048576 | tf_op jit(solution)/shard_map/all_to_all | solution.py:296
  113.5 3.0 %copy-start.15 = (f32[17,64,128]{2,1,0:T(8,128)}, f32[17,64,128]{2,1,0:T(8,128)S(1)}, u32[]{:S(2)}) copy-start(f32[17,64,128]{2,1,0:T(8,128)S(1)} %collective-permute-done.6.other_hbm) | copy-start | bytes 1671172
  113.5 9.4 %copy-start.4 = (s32[3,16]{1,0:T(4,128)S(1)}, s32[3,16]{1,0:T(4,128)}, u32[]{:S(2)}) copy-start(s32[3,16]{1,0:T(4,128)} %rows_ref.11) | copy-start | bytes 580
  113.5 9.4 %copy-start.7 = (s32[3,16]{1,0:T(4,128)S(1)}, s32[3,16]{1,0:T(4,128)}, u32[]{:S(2)}) copy-start(s32[3,16]{1,0:T(4,128)} %cols_ref.11) | copy-start | bytes 580
  113.6 9.4 %copy-start.10 = (s32[3,1]{0,1:T(1,128)S(1)}, s32[3,1]{0,1:T(1,128)}, u32[]{:S(2)}) copy-start(s32[3,1]{0,1:T(1,128)} %param.11) | copy-start | bytes 40
  123.0 14.1 %copy-start.13 = (f32[512,256]{1,0:T(8,128)S(1)}, f32[512,256]{1,0:T(8,128)}, u32[]{:S(2)}) copy-start(f32[512,256]{1,0:T(8,128)} %get-tuple-element.42.own_users) | copy-start | bytes 1572868
  128.7 8.3 %collective-permute-start.8 = (f32[512,256]{1,0:T(8,128)S(1)}, f32[512,256]{1,0:T(8,128)S(1)}, u32[]{:S(2)}, u32[]{:S(2)}) collective-permute-start(f32[512,256]{1,0:T(8,128)S(1)} %get-tuple-element.48), channel_id=1, source_target_pairs={{0,1},{1,0},{2,3},{3,2},{4,5},{5,4},{6,7},{7,6},{8,9},{9,8},{10,11... | collective-permute-start | bytes 1572872 | tf_op jit(solution)/shard_map/ppermute | solution.py:292
  133.4 14.9 %all-to-all-start.5 = ((f32[16,32,256]{2,1,0:T(8,128)}), f32[16,32,256]{2,1,0:T(8,128)S(1)}, u32[]{:S(2)}, u32[]{:S(2)}) async-start(f32[16,32,256]{2,1,0:T(8,128)} %bitcast.10), calls=%async_computation.5 | async-start | bytes 1048576 | tf_op jit(solution)/shard_map/all_to_all | solution.py:296
  (1 other events, 3.0 us)

commit v5 on v4

--- a/solution.py
+++ b/solution.py
@@ -69,58 +69,67 @@
     )
 
 
-def turn_kernel(tick, core_ref, rows_ref, cols_ref, count_ref, tiles_hbm, kept_hbm, sent_hbm,
+def turn_kernel(ticks, core_ref, rows_ref, cols_ref, count_ref, tiles_hbm, kept_hbm, sent_hbm,
                 tiles, kept, sent, turned, sems):
     core = core_ref[0]
     group = K_MAX // 4
-
-    def fetch(g):
-        slots = pl.ds(g * group, group)
-        return pltpu.make_async_copy(tiles_hbm.at[tick, slots], tiles.at[slots], sems.at[g])
-
-    def put(g, which):
-        buf, hbm = ((kept, kept_hbm), (sent, sent_hbm))[which]
-        slots = pl.ds(g * group, group)
-        return pltpu.make_async_copy(buf.at[slots], hbm.at[slots], sems.at[4 + 2 * g + which])
-
-    for g in range(4):
-        fetch(g).start()
+    groups = [(j, tick, g) for j, tick in enumerate(ticks) for g in range(4)]
+
+    def fetch(j, tick, g):
+        return pltpu.make_async_copy(
+            tiles_hbm.at[tick, pl.ds(g * group, group)], tiles.at[pl.ds(j * K_MAX + g * group, group)],
+            sems.at[13 * j + g])
+
+    def put(j, g, which):
+        buf, hbm, stride = ((kept, kept_hbm, K_MAX), (sent, sent_hbm, K_MAX + 1))[which]
+        slots = pl.ds(j * stride + g * group, group)
+        return pltpu.make_async_copy(buf.at[slots], hbm.at[slots], sems.at[13 * j + 4 + 2 * g + which])
+
+    def put_map(j):
+        slot = pl.ds(j * (K_MAX + 1) + K_MAX, 1)
+        return pltpu.make_async_copy(sent.at[slot], sent_hbm.at[slot], sems.at[13 * j + 12])
+
+    for at in groups:
+        fetch(*at).start()
     lane = lax.broadcasted_iota(jnp.int32, (8, TILE), 1)
-    row = jnp.full((8, TILE), -1, jnp.int32)
-    for k in range(K_MAX):
-        cell = rows_ref[tick, k] * I_TILES + cols_ref[tick, k]
-        row = jnp.where((lane == cell) & (k < count_ref[tick]), k, row)
-    sent[K_MAX, pl.ds(0, 8), :] = row.astype(f32)
-    sent[K_MAX, pl.ds(8, HALF - 8), :] = jnp.zeros((HALF - 8, TILE), f32)
-    last = pltpu.make_async_copy(sent.at[pl.ds(K_MAX, 1)], sent_hbm.at[pl.ds(K_MAX, 1)], sems.at[12])
-    last.start()
-    for g in range(4):
-        fetch(g).wait()
+    for j, tick in enumerate(ticks):
+        row = jnp.full((8, TILE), -1, jnp.int32)
+        for k in range(K_MAX):
+            cell = rows_ref[tick, k] * I_TILES + cols_ref[tick, k]
+            row = jnp.where((lane == cell) & (k < count_ref[tick]), k, row)
+        sent[j * (K_MAX + 1) + K_MAX, pl.ds(0, 8), :] = row.astype(f32)
+        sent[j * (K_MAX + 1) + K_MAX, pl.ds(8, HALF - 8), :] = jnp.zeros((HALF - 8, TILE), f32)
+        put_map(j).start()
+    for j, tick, g in groups:
+        fetch(j, tick, g).wait()
         for k in range(g * group, (g + 1) * group):
-            turned[k] = tiles[k].T
+            at = j * K_MAX + k
+            turned[at] = tiles[at].T
             for part in range(2):
                 rows = pl.ds(part * SHARE, SHARE)
                 mine = pl.multiple_of(part * HALF + core * SHARE, SHARE)
                 theirs = pl.multiple_of(part * HALF + (1 - core) * SHARE, SHARE)
-                kept[k, rows, :] = turned[k, pl.ds(mine, SHARE), :].astype(f32)
-                sent[k, rows, :] = turned[k, pl.ds(theirs, SHARE), :].astype(f32)
-        put(g, 0).start()
-        put(g, 1).start()
-    for g in range(4):
-        put(g, 0).wait()
-        put(g, 1).wait()
-    last.wait()
-
-
-def turned_tiles(tick, core, rows, cols, count, ratings):
-    tile = pltpu.VMEM((K_MAX, TILE, TILE), bf16)
+                kept[at, rows, :] = turned[at, pl.ds(mine, SHARE), :].astype(f32)
+                sent[at + j, rows, :] = turned[at, pl.ds(theirs, SHARE), :].astype(f32)
+        put(j, g, 0).start()
+        put(j, g, 1).start()
+    for j, tick, g in groups:
+        put(j, g, 0).wait()
+        put(j, g, 1).wait()
+    for j in range(len(ticks)):
+        put_map(j).wait()
+
+
+def turned_tiles(ticks, core, rows, cols, count, ratings):
+    n = len(ticks)
+    kept, sent = (n * K_MAX, HALF, TILE), (n * (K_MAX + 1), HALF, TILE)
+    tile = pltpu.VMEM((n * K_MAX, TILE, TILE), bf16)
     return call(
-        functools.partial(turn_kernel, tick),
-        (shape((K_MAX, HALF, TILE), f32), shape((K_MAX + 1, HALF, TILE), f32)),
+        functools.partial(turn_kernel, ticks),
+        (shape(kept, f32), shape(sent, f32)),
         [SMEM] * 4 + [ANY], (ANY, ANY),
-        [tile, pltpu.VMEM((K_MAX, HALF, TILE), f32), pltpu.VMEM((K_MAX + 1, HALF, TILE), f32), tile,
-         pltpu.SemaphoreType.DMA((13,))],
-        1000000, 1600000,
+        [tile, pltpu.VMEM(kept, f32), pltpu.VMEM(sent, f32), tile, pltpu.SemaphoreType.DMA((13 * n,))],
+        1000000, 1600000 * n,
     )(core, rows, cols, count, ratings)
 
 
@@ -129,13 +138,15 @@
     panel_ref, users, own_tiles, other_tiles, predicted, item_grad, user_grad, own_map, sems = refs[-9:]
     half = BLOCKS // 2
     parts = ITEMS_CORE // TILE
+    part_of = max(tick - 1, 0)
 
     def rows(block):
         return pl.ds(block * WIDTH, WIDTH)
 
     panel_load = pltpu.make_async_copy(panel_hbm, panel_ref, sems.at[0])
-    own_load = pltpu.make_async_copy(own_hbm, own_tiles, sems.at[1])
-    other_load = pltpu.make_async_copy(other_hbm.at[pl.ds(0, K_MAX)], other_tiles, sems.at[2])
+    own_load = pltpu.make_async_copy(own_hbm.at[pl.ds(part_of * K_MAX, K_MAX)], own_tiles, sems.at[1])
+    other_load = pltpu.make_async_copy(
+        other_hbm.at[pl.ds(part_of * (K_MAX + 1), K_MAX)], other_tiles, sems.at[2])
     user_loads = [
         pltpu.make_async_copy(
             (own_users if block < half else other_users).at[rows(block % half)], users.at[rows(block)],
@@ -308,11 +319,13 @@
     tile_count = tile_count.reshape(TICKS)
     other = swapped(own)
     for tick in range(TICKS):
-        kept, sent = turned_tiles(tick, core, tile_users, tile_items, tile_count, ratings)
-        got = swapped(sent)
+        if tick < 2:
+            kept, sent = turned_tiles(
+                ((0,), (1, 2))[tick], core, tile_users, tile_items, tile_count, ratings)
+            got = swapped(sent)
         if tick == 0:
             got, other = lax.optimization_barrier((got, other))
-        other_map = got[K_MAX, 0, :CELLS].astype(jnp.int32)
+        other_map = got[max(tick - 1, 0) * (K_MAX + 1) + K_MAX, 0, :CELLS].astype(jnp.int32)
         panel = exchanged(jnp.broadcast_to(share[None], (CHIPS, SHARE, R))).reshape(ITEMS_CORE, R)
         item_grad, *here = item_and_user_grads(
             tick, tick + 1 == TICKS, tile_users, tile_items, tile_count, other_map, panel, own, other, kept, got)

time: 150 us -> 155 us (1.033)
  blocking collectives: 0 us -> 27.1 us
  waiting for transfers between devices: 49.1 us -> 35.4 us
  starting transfers between devices: 63 us -> 55.7 us
    all_to_all x0 -> x2, blocking collectives: none -> 27.1 us  [exchanged(): lax.all_to_all(blocks, 'owner', split_axis=0, concat_axis=0, axis_index_g...]
    all_to_all x6 -> x4, waiting for transfers between devices: 47.1 us -> 33.4 us  [exchanged(): lax.all_to_all(blocks, 'owner', split_axis=0, concat_axis=0, axis_index_g...]
    all_to_all x6 -> x4, starting transfers between devices: 21.6 us -> 14.5 us  [exchanged(): lax.all_to_all(blocks, 'owner', split_axis=0, concat_axis=0, axis_index_g...]
    pallas_call x3 -> x2, Pallas kernels: 8.91 us -> 6.6 us  [turned_tiles(): call(functools.partial(turn_kernel, ticks), (shape(kept, f32), shape(sent...]
    pallas_call x3, Pallas kernels: 16.6 us -> 18.5 us  [item_and_user_grads(): call(functools.partial(step_kernel, tick, last), (shape((ITEMS_CORE, R),...]
    ppermute x7 -> x6, starting transfers between devices: 27.5 us -> 27.1 us  [swapped(): return lax.ppermute(x, 'owner', PARTNERS)]
  transfers between devices with their start and end apart: 15 -> 12, of which waited for: 8 -> 6; matrix products, arithmetic and copies ran while one was open for 2% -> 2% of each run, Pallas kernels for 8% -> 6%
where the time goes in v5:
time: 155 us; the launch traced here: 154 us
  starting transfers between devices  55.7 us (36%)
  waiting for transfers between devices  35.4 us (23%)
  Pallas kernels  30.9 us (20%)
  blocking collectives  27.1 us (17%)
  local copies, waits for them, and re-layouts  2.63 us (2%)
  other arithmetic  1.66 us (1%)
    all_to_all x4, waiting for transfers between devices, exchanged(): lax.all_to_all(blocks, 'owner', split_axis=0, concat_axis=0, axis_index_g...  33.4 us
    ppermute x6, starting transfers between devices, swapped(): return lax.ppermute(x, 'owner', PARTNERS)  27.1 us
    all_to_all x2, blocking collectives, exchanged(): lax.all_to_all(blocks, 'owner', split_axis=0, concat_axis=0, axis_index_g...  27.1 us
    pallas_call x3, Pallas kernels, item_and_user_grads(): call(functools.partial(step_kernel, tick, last), (shape((ITEMS_CORE, R),...  18.5 us
    all_to_all x4, starting transfers between devices, exchanged(): lax.all_to_all(blocks, 'owner', split_axis=0, concat_axis=0, axis_index_g...  14.5 us
    ppermute x2, starting transfers between devices, passed_along(): return lax.ppermute(block, axis, route)  14.1 us
    pallas_call x2, Pallas kernels, turned_tiles(): call(functools.partial(turn_kernel, ticks), (shape(kept, f32), shape(sent...  6.6 us
    pallas_call x2, Pallas kernels, updated_users(): call(update_kernel, (new, new), [ANY] * 4, (ANY, ANY), [both, both, both,...  5.83 us
  transfers between devices with their start and end apart: 12, of which 6 were waited for; matrix products, arithmetic and copies ran while one was open for 2% of the time, Pallas kernels for 6%

profile of v5, /device:TPU:1, one launch (start us, length us, event | category | flops | bytes accessed | tf_op | source)
XLA Modules:
  0.0 154.4 jit_solution(7043981251306157552)
XLA Ops:
  0.7 3.1 %shard_map.77 = (f32[16,64,128]{2,1,0:T(8,128)}, f32[17,64,128]{2,1,0:T(8,128)}) custom-call(s32[1]{0:T(128)} %bitcast.core_ref, s32[3,16]{1,0:T(4,128)} %rows_ref.9, s32[3,16]{1,0:T(4,128)} %cols_ref.9, s32[3]{0:T(128)} %bitcast.19, bf16[3,16,128,128]{3,2,1,0:T(8,128)(2,1)} %tiles_hbm.3), custom_call_target="tpu_custom_call" | custom-call | flops 1000000 | bytes 1600000 | tf_op jit(solution)/shard_map/pallas_call | solution.py:127
  3.8 8.9 %collective-permute-start = (f32[17,64,128]{2,1,0:T(8,128)}, f32[17,64,128]{2,1,0:T(8,128)S(1)}, u32[]{:S(2)}, u32[]{:S(2)}) collective-permute-start(f32[17,64,128]{2,1,0:T(8,128)} %get-tuple-element.25), channel_id=1, source_target_pairs={{0,1},{1,0},{2,3},{3,2},{4,5},{5,4},{6,7},{7,6},{8,9},{9,8},{10,11... | collective-permute-start | bytes 1671176 | tf_op jit(solution)/shard_map/ppermute | solution.py:303
  12.6 1.9 %collective-permute-start.1 = (f32[512,256]{1,0:T(8,128)S(1)}, f32[512,256]{1,0:T(8,128)S(1)}, u32[]{:S(2)}, u32[]{:S(2)}) collective-permute-start(f32[512,256]{1,0:T(8,128)S(1)} %copy-done), channel_id=1, source_target_pairs={{0,1},{1,0},{2,3},{3,2},{4,5},{5,4},{6,7},{7,6},{8,9},{9,8},{10,11... | collective-permute-start | bytes 1572872 | tf_op jit(solution)/shard_map/ppermute | solution.py:303
  14.6 0.9 broadcast_in_dim.6
  15.4 3.6 %all-to-all-start = ((f32[16,32,256]{2,1,0:T(8,128)}), f32[16,32,256]{2,1,0:T(8,128)S(1)}, u32[]{:S(2)}, u32[]{:S(2)}) async-start(f32[16,32,256]{2,1,0:T(8,128)} %broadcast_in_dim.6), calls=%async_computation | async-start | bytes 1048576 | tf_op jit(solution)/shard_map/all_to_all | solution.py:307
  19.1 10.8 %all-to-all-done = f32[16,32,256]{2,1,0:T(8,128)S(1)} async-done(((f32[16,32,256]{2,1,0:T(8,128)}), f32[16,32,256]{2,1,0:T(8,128)S(1)}, u32[]{:S(2)}, u32[]{:S(2)}) %all-to-all-start) | async-done | bytes 524320 | tf_op jit(solution)/shard_map/all_to_all | solution.py:307
  29.9 6.2 %shard_map.78 = (f32[512,256]{1,0:T(8,128)S(1)}, f32[1024,256]{1,0:T(8,128)}) custom-call(s32[3,16]{1,0:T(4,128)S(1)} %copy-done.2, s32[3,16]{1,0:T(4,128)S(1)} %copy-done.4, s32[3]{0:T(128)S(1)} %bitcast.21, s32[32]{0:T(128)S(1)} %convert_bitcast_fusion.other_map, f32[512,256]{1,0:T(8,128)S(1)} %bitcast.16, f32[512,256]{1,0:T(8,128)S(1)} %copy-done, ...), custom_call_target="tpu_custom_call" | custom-call | flops 2400000000 | bytes 4000000 | tf_op jit(solution)/shard_map/pallas_call | solution.py:246
  36.1 3.6 %collective-permute-start.2 = (f32[1024,256]{1,0:T(8,128)}, f32[1024,256]{1,0:T(8,128)S(1)}, u32[]{:S(2)}, u32[]{:S(2)}) collective-permute-start(f32[1024,256]{1,0:T(8,128)} %get-tuple-element.29.here_hbm), channel_id=1, source_target_pairs={{0,1},{1,0},{2,3},{3,2},{4,5},{5,4},{6,7},{7,6},{8,9},{9,8},{10,11... | collective-permute-start | bytes 3145736 | tf_op jit(solution)/shard_map/ppermute | solution.py:303
  39.6 3.5 %shard_map.80 = (f32[32,64,128]{2,1,0:T(8,128)}, f32[34,64,128]{2,1,0:T(8,128)}) custom-call(s32[1]{0:T(128)} %bitcast.core_ref, s32[3,16]{1,0:T(4,128)} %rows_ref.9, s32[3,16]{1,0:T(4,128)} %cols_ref.9, s32[3]{0:T(128)} %bitcast.20, bf16[3,16,128,128]{3,2,1,0:T(8,128)(2,1)} %tiles_hbm.3), custom_call_target="tpu_custom_call" | custom-call | flops 1000000 | bytes 3200000 | tf_op jit(solution)/shard_map/pallas_call | solution.py:127
  43.2 1.9 %collective-permute-start.3 = (f32[34,64,128]{2,1,0:T(8,128)}, f32[34,64,128]{2,1,0:T(8,128)S(1)}, u32[]{:S(2)}, u32[]{:S(2)}) collective-permute-start(f32[34,64,128]{2,1,0:T(8,128)} %get-tuple-element.34), channel_id=1, source_target_pairs={{0,1},{1,0},{2,3},{3,2},{4,5},{5,4},{6,7},{7,6},{8,9},{9,8},{10,11... | collective-permute-start | bytes 3342344 | tf_op jit(solution)/shard_map/ppermute | solution.py:303
  45.1 13.3 %all_to_all.30 = f32[16,32,256]{2,1,0:T(8,128)S(1)} all-to-all(f32[16,32,256]{2,1,0:T(8,128)S(1)} %bitcast.17), channel_id=1, replica_groups={{0,2,4,6,8,10,12,14,16,18,20,22,24,26,28,30},{1,3,5,7,9,11,13,15,17,19,..., dimensions={0} | all-to-all | bytes 1048576 | tf_op jit(solution)/shard_map/all_to_all | solution.py:307
  58.5 9.0 %collective-permute-start.4 = (f32[32,256]{1,0:T(8,128)S(1)}, f32[32,256]{1,0:T(8,128)S(1)}, u32[]{:S(2)}, u32[]{:S(2)}) collective-permute-start(f32[32,256]{1,0:T(8,128)S(1)} %multiply_add_fusion.3), channel_id=1, source_target_pairs={{32,0},{64,32},{96,64},{128,96},{160,128},{192,160},{224,192},{256... | collective-permute-start | bytes 98312 | tf_op jit(solution)/shard_map/ppermute | solution.py:313
  67.5 1.0 collective-permute-done.4
  68.5 0.8 broadcast_in_dim.7
  69.3 3.6 %all-to-all-start.2 = ((f32[16,32,256]{2,1,0:T(8,128)}), f32[16,32,256]{2,1,0:T(8,128)S(1)}, u32[]{:S(2)}, u32[]{:S(2)}) async-start(f32[16,32,256]{2,1,0:T(8,128)} %broadcast_in_dim.7), calls=%async_computation.2 | async-start | bytes 1048576 | tf_op jit(solution)/shard_map/all_to_all | solution.py:307
  73.0 3.1 %shard_map.79 = (f32[512,256]{1,0:T(8,128)}, f32[512,256]{1,0:T(8,128)}) custom-call(f32[512,256]{1,0:T(8,128)} %own_hbm.1, f32[512,256]{1,0:T(8,128)} %copy-done.1, f32[1024,256]{1,0:T(8,128)} %get-tuple-element.29.here_hbm, f32[1024,256]{1,0:T(8,128)} %copy-done.8), custom_call_target="tpu_custom_call" | custom-call | flops 1000000 | bytes 4000000 | tf_op jit(solution)/shard_map/pallas_call | solution.py:296
  76.1 5.8 %all-to-all-done.2 = f32[16,32,256]{2,1,0:T(8,128)S(1)} async-done(((f32[16,32,256]{2,1,0:T(8,128)}), f32[16,32,256]{2,1,0:T(8,128)S(1)}, u32[]{:S(2)}, u32[]{:S(2)}) %all-to-all-start.2) | async-done | bytes 524320 | tf_op jit(solution)/shard_map/all_to_all | solution.py:307
  82.0 6.6 %shard_map.81 = (f32[512,256]{1,0:T(8,128)S(1)}, f32[1024,256]{1,0:T(8,128)}) custom-call(s32[3,16]{1,0:T(4,128)S(1)} %copy-done.3, s32[3,16]{1,0:T(4,128)S(1)} %copy-done.5, s32[3]{0:T(128)S(1)} %bitcast.22, s32[32]{0:T(128)S(1)} %get-tuple-element.48.other_map, f32[512,256]{1,0:T(8,128)S(1)} %bitcast.14, f32[512,256]{1,0:T(8,128)} %get-tuple-element.32.own_users.own_hbm, ...), custom_call_target="tpu_custom_call" | custom-call | flops 2400000000 | bytes 4000000 | tf_op jit(solution)/shard_map/pallas_call | solution.py:246
  88.6 5.7 %collective-permute-start.5 = (f32[1024,256]{1,0:T(8,128)}, f32[1024,256]{1,0:T(8,128)S(1)}, u32[]{:S(2)}, u32[]{:S(2)}) collective-permute-start(f32[1024,256]{1,0:T(8,128)} %get-tuple-element.37.here_hbm), channel_id=1, source_target_pairs={{0,1},{1,0},{2,3},{3,2},{4,5},{5,4},{6,7},{7,6},{8,9},{9,8},{10,11... | collective-permute-start | bytes 3145736 | tf_op jit(solution)/shard_map/ppermute | solution.py:303
  94.3 13.8 %all_to_all.31 = f32[16,32,256]{2,1,0:T(8,128)S(1)} all-to-all(f32[16,32,256]{2,1,0:T(8,128)S(1)} %bitcast.18), channel_id=1, replica_groups={{0,2,4,6,8,10,12,14,16,18,20,22,24,26,28,30},{1,3,5,7,9,11,13,15,17,19,..., dimensions={0} | all-to-all | bytes 1048576 | tf_op jit(solution)/shard_map/all_to_all | solution.py:307
  108.1 5.1 %collective-permute-start.6 = (f32[32,256]{1,0:T(8,128)S(1)}, f32[32,256]{1,0:T(8,128)S(1)}, u32[]{:S(2)}, u32[]{:S(2)}) collective-permute-start(f32[32,256]{1,0:T(8,128)S(1)} %multiply_add_fusion.2), channel_id=1, source_target_pairs={{32,0},{64,32},{96,64},{128,96},{160,128},{192,160},{224,192},{256... | collective-permute-start | bytes 98312 | tf_op jit(solution)/shard_map/ppermute | solution.py:313
  113.2 1.0 collective-permute-done.6
  114.2 0.8 broadcast_in_dim.8
  115.1 3.8 %all-to-all-start.4 = ((f32[16,32,256]{2,1,0:T(8,128)}), f32[16,32,256]{2,1,0:T(8,128)S(1)}, u32[]{:S(2)}, u32[]{:S(2)}) async-start(f32[16,32,256]{2,1,0:T(8,128)} %broadcast_in_dim.8), calls=%async_computation.4 | async-start | bytes 1048576 | tf_op jit(solution)/shard_map/all_to_all | solution.py:307
  118.8 2.7 %shard_map.82 = (f32[512,256]{1,0:T(8,128)}, f32[512,256]{1,0:T(8,128)}) custom-call(f32[512,256]{1,0:T(8,128)} %get-tuple-element.32.own_users.own_hbm, f32[512,256]{1,0:T(8,128)} %get-tuple-element.33.other_users.other_hbm, f32[1024,256]{1,0:T(8,128)} %get-tuple-element.37.here_hbm, f32[1024,256]{1,0:T(8,128)} %copy-done.9), custom_call_target="tpu_custom_call" | custom-call | flops 1000000 | bytes 4000000 | tf_op jit(solution)/shard_map/pallas_call | solution.py:296
  121.6 6.5 %all-to-all-done.4 = f32[16,32,256]{2,1,0:T(8,128)S(1)} async-done(((f32[16,32,256]{2,1,0:T(8,128)}), f32[16,32,256]{2,1,0:T(8,128)S(1)}, u32[]{:S(2)}, u32[]{:S(2)}) %all-to-all-start.4) | async-done | bytes 524320 | tf_op jit(solution)/shard_map/all_to_all | solution.py:307
  128.0 5.7 %shard_map.83 = (f32[512,256]{1,0:T(8,128)}, f32[512,256]{1,0:T(8,128)S(1)}, f32[512,256]{1,0:T(8,128)S(1)}) custom-call(s32[3,16]{1,0:T(4,128)S(1)} %copy-done.3, s32[3,16]{1,0:T(4,128)S(1)} %copy-done.5, s32[3]{0:T(128)S(1)} %bitcast.23, s32[32]{0:T(128)S(1)} %get-tuple-element.49.other_map, f32[512,256]{1,0:T(8,128)S(1)} %bitcast.15, ...), custom_call_target="tpu_custom_call" | custom-call | flops 2400000000 | bytes 4000000 | tf_op jit(solution)/shard_map/pallas_call | solution.py:246
  133.7 5.2 %collective-permute-start.7 = (f32[512,256]{1,0:T(8,128)S(1)}, f32[512,256]{1,0:T(8,128)S(1)}, u32[]{:S(2)}, u32[]{:S(2)}) collective-permute-start(f32[512,256]{1,0:T(8,128)S(1)} %get-tuple-element.44), channel_id=1, source_target_pairs={{0,1},{1,0},{2,3},{3,2},{4,5},{5,4},{6,7},{7,6},{8,9},{9,8},{10,11... | collective-permute-start | bytes 1572872 | tf_op jit(solution)/shard_map/ppermute | solution.py:303
  138.9 3.6 %all-to-all-start.5 = ((f32[16,32,256]{2,1,0:T(8,128)}), f32[16,32,256]{2,1,0:T(8,128)S(1)}, u32[]{:S(2)}, u32[]{:S(2)}) async-start(f32[16,32,256]{2,1,0:T(8,128)} %bitcast.10), calls=%async_computation.5 | async-start | bytes 1048576 | tf_op jit(solution)/shard_map/all_to_all | solution.py:307
  142.5 0.9 multiply_add_fusion
  143.4 10.4 %all-to-all-done.5 = f32[16,32,256]{2,1,0:T(8,128)S(1)} async-done(((f32[16,32,256]{2,1,0:T(8,128)}), f32[16,32,256]{2,1,0:T(8,128)S(1)}, u32[]{:S(2)}, u32[]{:S(2)}) %all-to-all-start.5) | async-done | bytes 524320 | tf_op jit(solution)/shard_map/all_to_all | solution.py:307
  153.8 0.6 multiply_add_fusion.1
  (41 shorter events, 0.2 us)
Async XLA Ops:
  0.6 12.0 %copy-start = (f32[512,256]{1,0:T(8,128)S(1)}, f32[512,256]{1,0:T(8,128)}, u32[]{:S(2)}) copy-start(f32[512,256]{1,0:T(8,128)} %own_hbm.1) | copy-start | bytes 1572868
  0.6 13.9 %copy-start.11 = (f32[32,256]{1,0:T(8,128)S(1)}, f32[32,256]{1,0:T(8,128)}, u32[]{:S(2)}) copy-start(f32[32,256]{1,0:T(8,128)} %param.7) | copy-start | bytes 98308
  3.7 26.1 %copy-start.2 = (s32[3,16]{1,0:T(4,128)S(1)}, s32[3,16]{1,0:T(4,128)}, u32[]{:S(2)}) copy-start(s32[3,16]{1,0:T(4,128)} %rows_ref.9) | copy-start | bytes 580
  3.7 26.1 %copy-start.4 = (s32[3,16]{1,0:T(4,128)S(1)}, s32[3,16]{1,0:T(4,128)}, u32[]{:S(2)}) copy-start(s32[3,16]{1,0:T(4,128)} %cols_ref.9) | copy-start | bytes 580
  3.7 26.1 %copy-start.6 = (s32[3,1]{0,1:T(1,128)S(1)}, s32[3,1]{0,1:T(1,128)}, u32[]{:S(2)}) copy-start(s32[3,1]{0,1:T(1,128)} %param.11) | copy-start | bytes 40
  3.8 15.3 %collective-permute-start = (f32[17,64,128]{2,1,0:T(8,128)}, f32[17,64,128]{2,1,0:T(8,128)S(1)}, u32[]{:S(2)}, u32[]{:S(2)}) collective-permute-start(f32[17,64,128]{2,1,0:T(8,128)} %get-tuple-element.25), channel_id=1, source_target_pairs={{0,1},{1,0},{2,3},{3,2},{4,5},{5,4},{6,7},{7,6},{8,9},{9,8},{10,11... | collective-permute-start | bytes 1671176 | tf_op jit(solution)/shard_map/ppermute | solution.py:303
  12.6 6.4 %collective-permute-start.1 = (f32[512,256]{1,0:T(8,128)S(1)}, f32[512,256]{1,0:T(8,128)S(1)}, u32[]{:S(2)}, u32[]{:S(2)}) collective-permute-start(f32[512,256]{1,0:T(8,128)S(1)} %copy-done), channel_id=1, source_target_pairs={{0,1},{1,0},{2,3},{3,2},{4,5},{5,4},{6,7},{7,6},{8,9},{9,8},{10,11... | collective-permute-start | bytes 1572872 | tf_op jit(solution)/shard_map/ppermute | solution.py:303
  15.4 14.4 %all-to-all-start = ((f32[16,32,256]{2,1,0:T(8,128)}), f32[16,32,256]{2,1,0:T(8,128)S(1)}, u32[]{:S(2)}, u32[]{:S(2)}) async-start(f32[16,32,256]{2,1,0:T(8,128)} %broadcast_in_dim.6), calls=%async_computation | async-start | bytes 1048576 | tf_op jit(solution)/shard_map/all_to_all | solution.py:307
  19.0 17.0 %copy-start.1 = (f32[512,256]{1,0:T(8,128)}, f32[512,256]{1,0:T(8,128)S(1)}, u32[]{:S(2)}) copy-start(f32[512,256]{1,0:T(8,128)S(1)} %collective-permute-done.1.other_users.other_hbm) | copy-start | bytes 1572868
  19.1 10.8 %copy-start.13 = (f32[17,64,128]{2,1,0:T(8,128)}, f32[17,64,128]{2,1,0:T(8,128)S(1)}, u32[]{:S(2)}) copy-start(f32[17,64,128]{2,1,0:T(8,128)S(1)} %collective-permute-done.other_hbm) | copy-start | bytes 1671172
  36.1 22.4 %collective-permute-start.2 = (f32[1024,256]{1,0:T(8,128)}, f32[1024,256]{1,0:T(8,128)S(1)}, u32[]{:S(2)}, u32[]{:S(2)}) collective-permute-start(f32[1024,256]{1,0:T(8,128)} %get-tuple-element.29.here_hbm), channel_id=1, source_target_pairs={{0,1},{1,0},{2,3},{3,2},{4,5},{5,4},{6,7},{7,6},{8,9},{9,8},{10,11... | collective-permute-start | bytes 3145736 | tf_op jit(solution)/shard_map/ppermute | solution.py:303
  43.2 29.7 %collective-permute-start.3 = (f32[34,64,128]{2,1,0:T(8,128)}, f32[34,64,128]{2,1,0:T(8,128)S(1)}, u32[]{:S(2)}, u32[]{:S(2)}) collective-permute-start(f32[34,64,128]{2,1,0:T(8,128)} %get-tuple-element.34), channel_id=1, source_target_pairs={{0,1},{1,0},{2,3},{3,2},{4,5},{5,4},{6,7},{7,6},{8,9},{9,8},{10,11... | collective-permute-start | bytes 3342344 | tf_op jit(solution)/shard_map/ppermute | solution.py:303
  58.5 14.5 %copy-start.8 = (f32[1024,256]{1,0:T(8,128)}, f32[1024,256]{1,0:T(8,128)S(1)}, u32[]{:S(2)}) copy-start(f32[1024,256]{1,0:T(8,128)S(1)} %collective-permute-done.2.there_hbm) | copy-start | bytes 3145732
  58.5 10.0 %collective-permute-start.4 = (f32[32,256]{1,0:T(8,128)S(1)}, f32[32,256]{1,0:T(8,128)S(1)}, u32[]{:S(2)}, u32[]{:S(2)}) collective-permute-start(f32[32,256]{1,0:T(8,128)S(1)} %multiply_add_fusion.3), channel_id=1, source_target_pairs={{32,0},{64,32},{96,64},{128,96},{160,128},{192,160},{224,192},{256... | collective-permute-start | bytes 98312 | tf_op jit(solution)/shard_map/ppermute | solution.py:313
  69.3 12.6 %all-to-all-start.2 = ((f32[16,32,256]{2,1,0:T(8,128)}), f32[16,32,256]{2,1,0:T(8,128)S(1)}, u32[]{:S(2)}, u32[]{:S(2)}) async-start(f32[16,32,256]{2,1,0:T(8,128)} %broadcast_in_dim.7), calls=%async_computation.2 | async-start | bytes 1048576 | tf_op jit(solution)/shard_map/all_to_all | solution.py:307
  72.9 3.2 %copy-start.12 = (f32[34,64,128]{2,1,0:T(8,128)}, f32[34,64,128]{2,1,0:T(8,128)S(1)}, u32[]{:S(2)}) copy-start(f32[34,64,128]{2,1,0:T(8,128)S(1)} %collective-permute-done.3.other_hbm) | copy-start | bytes 3342340
  72.9 9.0 %copy-start.3 = (s32[3,16]{1,0:T(4,128)S(1)}, s32[3,16]{1,0:T(4,128)}, u32[]{:S(2)}) copy-start(s32[3,16]{1,0:T(4,128)} %rows_ref.9) | copy-start | bytes 580
  73.0 9.0 %copy-start.5 = (s32[3,16]{1,0:T(4,128)S(1)}, s32[3,16]{1,0:T(4,128)}, u32[]{:S(2)}) copy-start(s32[3,16]{1,0:T(4,128)} %cols_ref.9) | copy-start | bytes 580
  73.0 9.0 %copy-start.7 = (s32[3,1]{0,1:T(1,128)S(1)}, s32[3,1]{0,1:T(1,128)}, u32[]{:S(2)}) copy-start(s32[3,1]{0,1:T(1,128)} %param.11) | copy-start | bytes 40
  88.6 19.5 %collective-permute-start.5 = (f32[1024,256]{1,0:T(8,128)}, f32[1024,256]{1,0:T(8,128)S(1)}, u32[]{:S(2)}, u32[]{:S(2)}) collective-permute-start(f32[1024,256]{1,0:T(8,128)} %get-tuple-element.37.here_hbm), channel_id=1, source_target_pairs={{0,1},{1,0},{2,3},{3,2},{4,5},{5,4},{6,7},{7,6},{8,9},{9,8},{10,11... | collective-permute-start | bytes 3145736 | tf_op jit(solution)/shard_map/ppermute | solution.py:303
  108.1 10.7 %copy-start.9 = (f32[1024,256]{1,0:T(8,128)}, f32[1024,256]{1,0:T(8,128)S(1)}, u32[]{:S(2)}) copy-start(f32[1024,256]{1,0:T(8,128)S(1)} %collective-permute-done.5.there_hbm) | copy-start | bytes 3145732
  108.1 6.1 %collective-permute-start.6 = (f32[32,256]{1,0:T(8,128)S(1)}, f32[32,256]{1,0:T(8,128)S(1)}, u32[]{:S(2)}, u32[]{:S(2)}) collective-permute-start(f32[32,256]{1,0:T(8,128)S(1)} %multiply_add_fusion.2), channel_id=1, source_target_pairs={{32,0},{64,32},{96,64},{128,96},{160,128},{192,160},{224,192},{256... | collective-permute-start | bytes 98312 | tf_op jit(solution)/shard_map/ppermute | solution.py:313
  115.1 13.0 %all-to-all-start.4 = ((f32[16,32,256]{2,1,0:T(8,128)}), f32[16,32,256]{2,1,0:T(8,128)S(1)}, u32[]{:S(2)}, u32[]{:S(2)}) async-start(f32[16,32,256]{2,1,0:T(8,128)} %broadcast_in_dim.8), calls=%async_computation.4 | async-start | bytes 1048576 | tf_op jit(solution)/shard_map/all_to_all | solution.py:307
  133.7 8.8 %copy-start.10 = (f32[512,256]{1,0:T(8,128)S(1)}, f32[512,256]{1,0:T(8,128)}, u32[]{:S(2)}) copy-start(f32[512,256]{1,0:T(8,128)} %get-tuple-element.40.own_users) | copy-start | bytes 1572868
  133.7 8.8 %collective-permute-start.7 = (f32[512,256]{1,0:T(8,128)S(1)}, f32[512,256]{1,0:T(8,128)S(1)}, u32[]{:S(2)}, u32[]{:S(2)}) collective-permute-start(f32[512,256]{1,0:T(8,128)S(1)} %get-tuple-element.44), channel_id=1, source_target_pairs={{0,1},{1,0},{2,3},{3,2},{4,5},{5,4},{6,7},{7,6},{8,9},{9,8},{10,11... | collective-permute-start | bytes 1572872 | tf_op jit(solution)/shard_map/ppermute | solution.py:303
  138.9 14.9 %all-to-all-start.5 = ((f32[16,32,256]{2,1,0:T(8,128)}), f32[16,32,256]{2,1,0:T(8,128)S(1)}, u32[]{:S(2)}, u32[]{:S(2)}) async-start(f32[16,32,256]{2,1,0:T(8,128)} %bitcast.10), calls=%async_computation.5 | async-start | bytes 1048576 | tf_op jit(solution)/shard_map/all_to_all | solution.py:307
